TPU v7x, 128 devices: a whole 4x4x4 slice. The times are simulated.
128 devices in a mesh: dp: 8 (over z, y_hi), tensor: 16 (over y_lo, x, core).
Axes of the slice: x: 4, y: 4 (y_hi: 2, y_lo: 2; y = y_hi * 2 + y_lo), z: 4, core: 2. Of those that a mesh axis runs over, the one named last changes fastest.
Arguments:
- inputs: bfloat16 [16384, 2048], P(('dp', 'tensor')), may hold values from -24 to 24
- grad_out: bfloat16 [16384, 2048], P(('dp', 'tensor')), may hold values from -24 to 24
- gate_pre: bfloat16 [16384, 6144], P('dp', 'tensor'), may hold values from -6 to 6
- up_pre: bfloat16 [16384, 6144], P('dp', 'tensor'), may hold values from -6 to 6
- w_gate: bfloat16 [2048, 6144], P(None, 'tensor'), may hold values from -0.125 to 0.125
- w_up: bfloat16 [2048, 6144], P(None, 'tensor'), may hold values from -0.125 to 0.125
- w_down: bfloat16 [6144, 2048], P('tensor'), may hold values from -0.078125 to 0.078125
Outputs:
- d_input: float32 [16384, 2048], P(('dp', 'tensor'))
- grad_gate: float32 [2048, 6144], P('dp', 'tensor')
- grad_up: float32 [2048, 6144], P('dp', 'tensor')
- grad_down: float32 [6144, 2048], P('tensor', 'dp')
All inputs are finite; a program needn't handle non-finite values.
Results may differ from a plain program's by a relative error of at most 0.0029.
Values may be sent and summed in bfloat16 or wider, within the bound.
No kernel may reach another device: no remote copies, remote signals or barrier semaphores. Data moves between devices by JAX's collectives and lax.ppermute only.
A program may use at most 128 MiB of HBM per device.

v0:
```python
import jax
import jax.numpy as jnp
from jax import lax
from jax.sharding import PartitionSpec as P


def sum_weights(grad_gate, grad_up, grad_down):
    gate_part, up_part = (
        lax.psum_scatter(grad_gate, "dp", scatter_dimension=0, tiled=True),
        lax.psum_scatter(grad_up, "dp", scatter_dimension=0, tiled=True),
    )
    down_part = lax.psum_scatter(grad_down, "dp", scatter_dimension=1, tiled=True)
    return (gate_part, up_part, down_part)


def on_device(inputs, grad_out, gate_pre, up_pre, w_gate, w_up, w_down):
    gate = gate_pre.astype(jnp.float32)
    upper = up_pre.astype(jnp.float32)
    gate_sig = jax.nn.sigmoid(gate)
    gate_act = gate * gate_sig
    hidden = (gate_act * upper).astype(jnp.bfloat16)
    slope = gate_sig * (1.0 + gate * (1.0 - gate_sig))
    piece = lax.all_gather(grad_out, "tensor", axis=0, tiled=True)
    d_hidden = jnp.einsum("rd,fd->rf", piece, w_down, preferred_element_type=jnp.float32)
    d_gate = (d_hidden * upper * slope).astype(jnp.bfloat16)
    d_up = (d_hidden * gate_act).astype(jnp.bfloat16)
    d_gate, d_up = (d_gate, d_up)
    gate_all = d_gate
    up_all = d_up
    grad_down = jnp.einsum("rf,rd->fd", hidden, piece, preferred_element_type=jnp.float32)
    d_gate = gate_all
    d_up = up_all
    piece = lax.all_gather(inputs, "tensor", axis=0, tiled=True)
    gate_term = jnp.einsum("rd,rf->df", piece, d_gate, preferred_element_type=jnp.float32)
    up_term = jnp.einsum("rd,rf->df", piece, d_up, preferred_element_type=jnp.float32)
    gate_term, up_term = (gate_term, up_term)
    term = jnp.einsum("rf,df->rd", gate_all, w_gate, preferred_element_type=jnp.float32)
    d_input = lax.psum_scatter(
        term + jnp.einsum("rf,df->rd", up_all, w_up, preferred_element_type=jnp.float32),
        "tensor",
        scatter_dimension=0,
        tiled=True,
    )
    gate_part, up_part, down_part = sum_weights(gate_term, up_term, grad_down)
    return (d_input, gate_part, up_part, down_part)


def solution(mesh):
    in_specs = (
        P(("dp", "tensor"), None),
        P(("dp", "tensor"), None),
        P("dp", "tensor"),
        P("dp", "tensor"),
        P(None, "tensor"),
        P(None, "tensor"),
        P("tensor", None),
    )
    out_specs = (P(("dp", "tensor"), None), P("dp", "tensor"), P("dp", "tensor"), P("tensor", "dp"))
    return jax.shard_map(
        on_device, mesh=mesh, in_specs=in_specs, out_specs=out_specs, check_vma=False
    )
```

profile of v0, /device:TPU:0, one launch (start us, length us, event | category | flops | bytes accessed | tf_op | source)
XLA Modules:
  0.0 482.0 jit_solution(2514089192070290923)
XLA Ops:
  7.2 0.0 copy-start
  7.2 0.0 all-gather.3.cloned.1.call-start
  7.2 0.7 all-gather.3.cloned.1.call-update
  7.9 0.0 all-gather.5.cloned.1.call-start
  8.0 0.7 all-gather.5.cloned.1.call-update
  8.7 0.0 reduce-scatter.9.cloned.1.call-start
  8.7 55.6 %all-gather.3.cloned.1.call-done = bf16[2048,2048]{1,0:T(8,128)(2,1)} async-done(((bf16[128,2048]{1,0:T(8,128)(2,1)}), bf16[2048,2048]{1,0:T(8,128)(2,1)}) %all-gather.3.cloned.1.call-update) | async-done | bytes 8388624 | tf_op jit(solution)/shard_map/all_gather | solution.py:23
  64.3 11.8 %fusion.1 = (bf16[2048,384]{1,0:T(8,128)(2,1)S(1)}, f32[2048,384]{1,0:T(8,128)}) fusion(bf16[2048,384]{1,0:T(8,128)(2,1)} %param.10, bf16[2048,384]{1,0:T(8,128)(2,1)} %param.9, bf16[2048,2048]{1,0:T(8,128)(2,1)} %all-gather.3.cloned.1.call-done, bf16[384,2048]{1,0:T(8,128)(2,1)} %param.13), kind=kOutput, calls=%fused_computation.7 | convolution fusion | flops 3230662656 | bytes 17825792 | tf_op jit(solution)/shard_map/rd,fd->rf/dot_general | solution.py:24
  76.1 42.9 %all-gather.5.cloned.1.call-done = bf16[2048,2048]{1,0:T(8,128)(2,1)} async-done(((bf16[128,2048]{1,0:T(8,128)(2,1)}), bf16[2048,2048]{1,0:T(8,128)(2,1)}) %all-gather.5.cloned.1.call-update) | async-done | bytes 8388624 | tf_op jit(solution)/shard_map/all_gather | solution.py:33
  119.0 10.1 %convolution_bitcast_fusion = f32[2048,384]{0,1:T(8,128)} fusion(bf16[2048,2048]{1,0:T(8,128)(2,1)} %all-gather.5.cloned.1.call-done, f32[2048,384]{1,0:T(8,128)} %get-tuple-element.9, bf16[2048,384]{1,0:T(8,128)(2,1)} %param.9), kind=kOutput, calls=%fused_computation.15 | convolution fusion | flops 3226730496 | bytes 16252928 | tf_op jit(solution)/shard_map/rd,rf->df/dot_general | solution.py:35
  129.1 0.0 reduce-scatter.9.cloned.1.call-update
  129.2 0.0 reduce-scatter.7.cloned.1.call-start
  129.2 8.5 %convolution_bitcast_fusion.1 = f32[2048,384]{0,1:T(8,128)} fusion(bf16[2048,384]{1,0:T(8,128)(2,1)S(1)} %get-tuple-element.8, bf16[2048,2048]{1,0:T(8,128)(2,1)} %all-gather.5.cloned.1.call-done), kind=kOutput, calls=%fused_computation.16 | convolution fusion | flops 3221225472 | bytes 13107200 | tf_op jit(solution)/shard_map/rd,rf->df/dot_general | solution.py:34
  137.7 0.0 reduce-scatter.7.cloned.1.call-update
  137.7 0.2 reduce-scatter.11.cloned.1.call-start
  137.9 10.0 %fusion.8 = f32[384,2048]{1,0:T(8,128)} fusion(bf16[2048,2048]{1,0:T(8,128)(2,1)} %all-gather.3.cloned.1.call-done, bf16[2048,384]{1,0:T(8,128)(2,1)} %param.10, bf16[2048,384]{1,0:T(8,128)(2,1)} %param.9), kind=kOutput, calls=%fused_computation.17 | convolution fusion | flops 3227516928 | bytes 14680064 | tf_op jit(solution)/shard_map/rf,rd->fd/dot_general | solution.py:30
  147.9 0.0 reduce-scatter.11.cloned.1.call-update
  147.9 0.0 reduce-scatter.5.cloned.1.call-start
  148.0 0.0 copy-done
  148.0 0.0 copy-start.2
  148.0 0.0 copy-start.3
  148.0 0.0 copy-start.4
  148.0 8.5 %fusion.11 = f32[2048,2048]{1,0:T(8,128)} fusion(bf16[2048,384]{1,0:T(8,128)(2,1)S(1)} %get-tuple-element.8, bf16[2048,384]{1,0:T(8,128)(2,1)S(1)} %copy-done), kind=kOutput, calls=%fused_computation.19 | convolution fusion | flops 3221225472 | bytes 19922944 | tf_op jit(solution)/shard_map/rf,df->rd/dot_general | solution.py:37
  156.5 0.0 copy-done.2
  156.5 0.0 copy-done.3
  156.5 0.0 copy-done.4
  156.5 11.8 %convolution_add_fusion = f32[2048,2048]{1,0:T(8,128)} fusion(f32[2048,2048]{1,0:T(8,128)} %fusion.11, bf16[2048,384]{1,0:T(8,128)(2,1)S(1)} %copy-done.4, f32[2048,384]{1,0:T(8,128)S(1)} %copy-done.2, bf16[2048,384]{1,0:T(8,128)(2,1)S(1)} %copy-done.3), kind=kOutput, calls=%fused_computation | convolution fusion | flops 3230924800 | bytes 39845888 | tf_op jit(solution)/shard_map/rf,df->rd/dot_general | solution.py:39
  168.4 0.0 reduce-scatter.5.cloned.1.call-update
  168.4 0.0 copy-start.1
  168.4 41.7 %reduce-scatter.9.cloned.1.call-done = f32[256,384]{0,1:T(8,128)} async-done(((f32[2048,384]{0,1:T(8,128)}), f32[256,384]{0,1:T(8,128)}) %reduce-scatter.9.cloned.1.call-update) | async-done | bytes 393232 | tf_op jit(solution)/shard_map/reduce_scatter | solution.py:10
  210.1 1.9 copy.12
  212.0 80.4 %reduce-scatter.7.cloned.1.call-done = f32[256,384]{0,1:T(8,128)} async-done(((f32[2048,384]{0,1:T(8,128)}), f32[256,384]{0,1:T(8,128)}) %reduce-scatter.7.cloned.1.call-update) | async-done | bytes 393232 | tf_op jit(solution)/shard_map/reduce_scatter | solution.py:9
  292.5 1.9 copy.11
  294.4 81.0 %reduce-scatter.11.cloned.1.call-done = f32[384,256]{1,0:T(8,128)} async-done(((f32[384,2048]{1,0:T(8,128)}), f32[384,256]{1,0:T(8,128)}) %reduce-scatter.11.cloned.1.call-update) | async-done | bytes 393232 | tf_op jit(solution)/shard_map/reduce_scatter | solution.py:12
  375.4 99.8 %reduce-scatter.5.cloned.1.call-done = f32[128,2048]{1,0:T(8,128)} async-done(((f32[2048,2048]{1,0:T(8,128)}), f32[128,2048]{1,0:T(8,128)}) %reduce-scatter.5.cloned.1.call-update) | async-done | bytes 1048592 | tf_op jit(solution)/shard_map/reduce_scatter | solution.py:38
  475.2 0.0 copy-done.1
Async XLA Ops:
  7.2 140.8 %copy-start = (bf16[2048,384]{1,0:T(8,128)(2,1)S(1)}, bf16[2048,384]{1,0:T(8,128)(2,1)}, u32[]{:S(2)}) copy-start(bf16[2048,384]{1,0:T(8,128)(2,1)} %param.11) | copy-start | bytes 4718596
  7.2 57.1 %all-gather.3.cloned.1.call-start = ((), (), s32[]{:S(2)}) async-start(), calls=%async_computation.4 | async-start | bytes 8912896 | tf_op jit(solution)/shard_map/all_gather | solution.py:23
  7.9 111.1 %all-gather.5.cloned.1.call-start = ((), (), s32[]{:S(2)}) async-start(), calls=%async_computation.6 | async-start | bytes 8912896 | tf_op jit(solution)/shard_map/all_gather | solution.py:33
  8.7 201.5 %reduce-scatter.9.cloned.1.call-start = ((), (), s32[]{:S(2)}) async-start(), calls=%async_computation.8 | async-start | bytes 3538944 | tf_op jit(solution)/shard_map/reduce_scatter | solution.py:10
  129.2 163.3 %reduce-scatter.7.cloned.1.call-start = ((), (), s32[]{:S(2)}) async-start(), calls=%async_computation.7 | async-start | bytes 3538944 | tf_op jit(solution)/shard_map/reduce_scatter | solution.py:9
  137.7 237.7 %reduce-scatter.11.cloned.1.call-start = ((), (), s32[]{:S(2)}) async-start(), calls=%async_computation.9 | async-start | bytes 3538944 | tf_op jit(solution)/shard_map/reduce_scatter | solution.py:12
  147.9 327.2 %reduce-scatter.5.cloned.1.call-start = ((), (), s32[]{:S(2)}) async-start(), calls=%async_computation.5 | async-start | bytes 17825792 | tf_op jit(solution)/shard_map/reduce_scatter | solution.py:38
  148.0 8.5 %copy-start.2 = (f32[2048,384]{1,0:T(8,128)S(1)}, f32[2048,384]{1,0:T(8,128)}, u32[]{:S(2)}) copy-start(f32[2048,384]{1,0:T(8,128)} %get-tuple-element.9) | copy-start | bytes 9437188
  148.0 8.5 %copy-start.3 = (bf16[2048,384]{1,0:T(8,128)(2,1)S(1)}, bf16[2048,384]{1,0:T(8,128)(2,1)}, u32[]{:S(2)}) copy-start(bf16[2048,384]{1,0:T(8,128)(2,1)} %param.9) | copy-start | bytes 4718596
  148.0 8.5 %copy-start.4 = (bf16[2048,384]{1,0:T(8,128)(2,1)S(1)}, bf16[2048,384]{1,0:T(8,128)(2,1)}, u32[]{:S(2)}) copy-start(bf16[2048,384]{1,0:T(8,128)(2,1)} %param.12) | copy-start | bytes 4718596
  168.4 306.8 %copy-start.1 = (bf16[2048,384]{1,0:T(8,128)(2,1)S(1)}, bf16[2048,384]{1,0:T(8,128)(2,1)}, u32[]{:S(2)}) copy-start(bf16[2048,384]{1,0:T(8,128)(2,1)} %param.11) | copy-start | bytes 4718596
Sparse Core Ops, SparseCore 0:
  9.7 54.5 all-gather.2
  66.0 52.9 all-gather.4
  129.3 80.7 reduce-scatter.8
  213.8 78.6 reduce-scatter.6
  296.7 78.6 reduce-scatter.10
  378.2 96.9 reduce-scatter.4
where the time goes:
time: 482 us
  waiting for transfers between devices  403 us (84%)
  matrix products  60.7 us (13%)
  between operations  14.2 us (3%)
    reduce_scatter x1, waiting for transfers between devices, on_device(): lax.psum_scatter(term + jnp.einsum('rf,df->rd', up_all, w_up, preferred_e...  99.8 us
    reduce_scatter x1, waiting for transfers between devices, sum_weights(): lax.psum_scatter(grad_down, 'dp', scatter_dimension=1, tiled=True)  81 us
    reduce_scatter x1, waiting for transfers between devices, sum_weights(): lax.psum_scatter(grad_gate, 'dp', scatter_dimension=0, tiled=True)  80.4 us
    all_gather x1, waiting for transfers between devices, on_device(): piece = lax.all_gather(grad_out, 'tensor', axis=0, tiled=True)  55.6 us
    all_gather x1, waiting for transfers between devices, on_device(): piece = lax.all_gather(inputs, 'tensor', axis=0, tiled=True)  42.9 us
    reduce_scatter x1, waiting for transfers between devices, sum_weights(): lax.psum_scatter(grad_up, 'dp', scatter_dimension=0, tiled=True)  41.7 us
    dot_general x1, matrix products, on_device(): jnp.einsum('rf,df->rd', up_all, w_up, preferred_element_type=jnp.float32)  11.8 us
    dot_general x1, matrix products, on_device(): jnp.einsum('rd,fd->rf', piece, w_down, preferred_element_type=jnp.float32)  11.8 us
  transfers between devices with their start and end apart: 6, of which 6 were waited for; matrix products, arithmetic and copies ran while one was open for 11% of the time, Pallas kernels for 0%

commit v1 on v0

v1 whole, which is shorter than its diff:
```python
import jax
import jax.numpy as jnp
import numpy as np
from jax import lax
from jax.experimental import pallas as pl
from jax.experimental.pallas import tpu as pltpu
from jax.sharding import PartitionSpec as P

NY, NX, NC = 2, 4, 2
NZ, NF = 4, 2
BF, F32 = jnp.bfloat16, jnp.float32
ORDER = [(0, 0), (1, 0), (0, 1), (0, 3), (1, 1), (1, 3), (0, 2), (1, 2)]
CHUNKS = len(ORDER)
FARTHEST = (2, 1, 3, 0)


def tensor_pairs(move):
    index = lambda y, x, c: (y * NX + x) * NC + c
    return [(index(y, x, c), index(*move(y, x, c))) for y in range(NY) for x in range(NX) for c in range(NC)]


def dp_pairs(move):
    index = lambda z, f: z * NF + f
    return [(index(z, f), index(*move(z, f))) for z in range(NZ) for f in range(NF)]


CORE = tensor_pairs(lambda y, x, c: (y, x, 1 - c))
Y_SWAP = tensor_pairs(lambda y, x, c: (1 - y, x, c))
X_UP = tensor_pairs(lambda y, x, c: (y, (x + 1) % NX, c))
X_DOWN = tensor_pairs(lambda y, x, c: (y, (x - 1) % NX, c))
Z_UP = dp_pairs(lambda z, f: ((z + 1) % NZ, f))
Z_DOWN = dp_pairs(lambda z, f: ((z - 1) % NZ, f))
Z_FAR = dp_pairs(lambda z, f: ((z + 2) % NZ, f))
F_SWAP = dp_pairs(lambda z, f: (z, 1 - f))

ROWS = np.array(
    [
        [((y ^ dy) * NX + (x + dx) % NX) * NC + c for dy, dx in ORDER]
        for y in range(NY) for x in range(NX) for c in range(NC)
    ],
    np.int32,
)
SLABS = np.array(
    [
        [((z + dz) % NZ) * NF + (f ^ df) for dz in FARTHEST for df in range(NF)]
        for z in range(NZ) for f in range(NF)
    ],
    np.int32,
)
ANY = pl.BlockSpec(memory_space=pltpu.HBM)
VMEM = pl.BlockSpec(memory_space=pltpu.VMEM)
NT = (((1,), (1,)), ((), ()))
TN = (((0,), (0,)), ((), ()))


def tsend(value, pairs):
    return lax.ppermute(value, "tensor", pairs)


def dsend(value, pairs):
    return lax.ppermute(value, "dp", pairs)


def low(value):
    return value.astype(BF)


def params():
    return pltpu.CompilerParams(vmem_limit_bytes=60 << 20)


def cost(effort, flops, moved):
    return pl.CostEstimate(flops=int(flops * effort), bytes_accessed=int(moved * effort), transcendentals=0)


def hidden_body(table_ref, *refs):
    pre, (out,) = refs[:4], refs[4:]
    width = pre[0].shape[1]
    for core in range(NC):
        gate, upper = pre[core][...].astype(F32), pre[NC + core][...].astype(F32)
        out[:, core * width : (core + 1) * width] = (gate / (1.0 + jnp.exp(-gate)) * upper).astype(BF)


def hidden_call(table, pre, step, effort):
    width = pre[0].shape[1]
    total, both = step * CHUNKS, NC * width
    return pl.pallas_call(
        hidden_body,
        out_shape=jax.ShapeDtypeStruct((total, both), BF),
        grid_spec=pltpu.PrefetchScalarGridSpec(
            num_scalar_prefetch=1,
            grid=(CHUNKS,),
            in_specs=[pl.BlockSpec((step, width), lambda k, t: (t[k], 0))] * 4,
            out_specs=pl.BlockSpec((step, both), lambda k, t: (k, 0)),
        ),
        compiler_params=params(),
        cost_estimate=cost(effort, 16 * total * both, 6 * total * both),
        name="hidden",
    )(table, *pre)


def slope_body(first, count, table_ref, *refs):
    chunks, refs = refs[:count], refs[count:]
    down_pair, pre, (dgate_ref, dup_ref) = refs[:2], refs[2:6], refs[6:8]
    cot, down, gates, uppers, chunk_sem, down_sem, pre_sem = refs[8:]
    step = chunks[0].shape[0]
    width = pre[0].shape[1]

    def down_copy(j):
        return pltpu.make_async_copy(down_pair[j], down.at[pl.ds(j * width, width)], down_sem.at[j])

    def chunk_copy(k):
        return pltpu.make_async_copy(chunks[k], cot.at[pl.ds(k * step, step)], chunk_sem.at[k])

    def pre_copy(k, j):
        target = (gates, uppers)[j // 2]
        return pltpu.make_async_copy(
            pre[j].at[pl.ds(table_ref[first + k] * step, step)],
            target.at[pl.ds(k * step, step), pl.ds((j % 2) * width, width)],
            pre_sem.at[k, j],
        )

    for j in range(2):
        down_copy(j).start()
    for k in range(count):
        chunk_copy(k).start()
        for j in range(4):
            pre_copy(k, j).start()
    for j in range(2):
        down_copy(j).wait()
    tile = 2 * step
    for i in range(count // 2):
        for k in (2 * i, 2 * i + 1):
            chunk_copy(k).wait()
            for j in range(4):
                pre_copy(k, j).wait()
        at = pl.ds(i * tile, tile)
        d_hidden = lax.dot_general(cot[at, :], down[...], NT, preferred_element_type=F32)
        gate = gates[at, :].astype(F32)
        sig = 1.0 / (1.0 + jnp.exp(-gate))
        dgate_ref[at, :] = (d_hidden * uppers[at, :].astype(F32) * sig * (1.0 + gate * (1.0 - sig))).astype(BF)
        dup_ref[at, :] = (d_hidden * (gate * sig)).astype(BF)


def slope_call(table, first, chunks, downs, pre, effort):
    count = len(chunks)
    step, depth = chunks[0].shape
    width = downs[0].shape[0]
    total, both = step * count, NC * width
    out = jax.ShapeDtypeStruct((total, both), BF)
    return pl.pallas_call(
        lambda *refs: slope_body(first, count, *refs),
        out_shape=(out, out),
        grid_spec=pltpu.PrefetchScalarGridSpec(
            num_scalar_prefetch=1,
            grid=(1,),
            in_specs=[ANY] * (count + 6),
            out_specs=[pl.BlockSpec((total, both), lambda i, t: (0, 0))] * 2,
            scratch_shapes=[
                pltpu.VMEM((total, depth), BF),
                pltpu.VMEM((both, depth), BF),
                pltpu.VMEM((total, both), BF),
                pltpu.VMEM((total, both), BF),
                pltpu.SemaphoreType.DMA((count,)),
                pltpu.SemaphoreType.DMA((2,)),
                pltpu.SemaphoreType.DMA((count, 4)),
            ],
        ),
        compiler_params=params(),
        cost_estimate=cost(effort, 2 * total * depth * both, 8 << 20),
        name="slope",
    )(table, *chunks, *downs, *pre)


def weight_body(count, wide, table_ref, *refs):
    chunks, rights, (own_ref, other_ref) = refs[:count], refs[count:-2], refs[-2:]
    parts = len(rights) // wide
    step = chunks[0].shape[0]
    per = count // parts
    width = own_ref.shape[2] // wide
    for w in range(wide):
        both = None
        for p in range(parts):
            left = jnp.concatenate([c[...] for c in chunks[p * per : (p + 1) * per]], axis=0)
            term = lax.dot_general(left, rights[w * parts + p][...], TN, preferred_element_type=F32)
            both = term if both is None else both + term
        own_ref[0, :, w * width : (w + 1) * width] = both[:, :width]
        other_ref[0, :, w * width : (w + 1) * width] = both[:, width:].astype(BF)


def weight_call(table, first, slabs, sources, rights, effort):
    wide, parts = len(rights), len(rights[0])
    rows, both = rights[0][0].shape
    step, depth = rows * parts // CHUNKS, sources[0].shape[1]
    features = depth // (NZ * NF)
    slab = (slabs, features, wide * both // NC)
    at = lambda r, t: t[CHUNKS + first + r]
    if len(sources) == 1:
        chunks = sources * CHUNKS
        maps = [lambda r, t, k=k: (t[k], at(r, t)) for k in range(CHUNKS)]
    else:
        chunks = sources
        maps = [lambda r, t: (0, at(r, t))] * CHUNKS
    block = pl.BlockSpec((1, *slab[1:]), lambda r, t: (r, 0, 0))
    return pl.pallas_call(
        lambda *refs: weight_body(CHUNKS, wide, *refs),
        out_shape=(jax.ShapeDtypeStruct(slab, F32), jax.ShapeDtypeStruct(slab, BF)),
        grid_spec=pltpu.PrefetchScalarGridSpec(
            num_scalar_prefetch=1,
            grid=(slab[0],),
            in_specs=[pl.BlockSpec((step, features), m) for m in maps]
            + [pl.BlockSpec((rows, both), lambda r, t: (0, 0))] * (wide * parts),
            out_specs=[block, block],
        ),
        compiler_params=params(),
        cost_estimate=cost(effort, 2 * slabs * features * rows * parts * both * wide, 10 << 20),
        name="weight",
    )(table, *chunks, *[part for right in rights for part in right])


KEPT = [(0, 0), (1, 0), (1, 1), (0, 3)]


def input_body(parts, *refs):
    lefts, weights, outs = refs[: 2 * parts], refs[2 * parts : 2 * parts + 4], refs[2 * parts + 4 :]
    step = outs[0].shape[0]
    gate_weight = jnp.concatenate([weights[0][...], weights[1][...]], axis=1)
    up_weight = jnp.concatenate([weights[2][...], weights[3][...]], axis=1)
    per = CHUNKS // parts
    for p in range(parts):
        total = lax.dot_general(lefts[p][...], gate_weight, NT, preferred_element_type=F32)
        total = total + lax.dot_general(lefts[parts + p][...], up_weight, NT, preferred_element_type=F32)
        for k in range(per):
            out = outs[p * per + k]
            out[...] = total[k * step : (k + 1) * step].astype(out.dtype)


def input_call(d_gates, d_ups, weights, effort):
    depth, width = weights[0].shape
    parts = len(d_gates)
    rows, both = d_gates[0].shape
    step = rows * parts // CHUNKS
    tile = 256
    outs = pl.pallas_call(
        lambda *refs: input_body(parts, *refs),
        out_shape=[jax.ShapeDtypeStruct((step, depth), F32 if o in KEPT else BF) for o in ORDER],
        grid=(depth // tile,),
        in_specs=[pl.BlockSpec((rows, both), lambda n: (0, 0))] * (2 * parts)
        + [pl.BlockSpec((tile, width), lambda n: (n, 0))] * 4,
        out_specs=[pl.BlockSpec((step, tile), lambda n: (0, n))] * CHUNKS,
        compiler_params=params(),
        cost_estimate=cost(effort, 4 * rows * parts * depth * both, 14 << 20),
        name="input",
    )(*d_gates, *d_ups, *weights)
    return dict(zip(ORDER, outs))


def after(values, *events):
    return lax.optimization_barrier((values, events))[0]


def split(slabs):
    return slabs.reshape(-1, NF, *slabs.shape[1:])


def on_device(inputs, grad_out, gate_pre, up_pre, w_gate, w_up, w_down):
    table = jnp.concatenate([jnp.asarray(ROWS)[lax.axis_index("tensor")], jnp.asarray(SLABS)[lax.axis_index("dp")]])
    step, width = grad_out.shape[0], w_down.shape[0]
    half = CHUNKS // 2
    together = lambda *values: lax.optimization_barrier(values)

    other, above, below = tsend(grad_out, Y_SWAP), tsend(grad_out, X_DOWN), tsend(grad_out, X_UP)
    other, above, below, down_in, gate_in, inputs, up_pre = together(
        other, above, below, tsend(w_down, CORE), tsend(gate_pre, CORE), inputs, up_pre
    )
    near = [grad_out, other, above, below]
    above_y, below_y, far = tsend(other, X_DOWN), tsend(other, X_UP), tsend(above, X_DOWN)
    below_in, up_in = tsend(inputs, X_UP), tsend(up_pre, CORE)
    downs, pre = (w_down, down_in), (gate_pre, gate_in, up_pre, up_in)
    firsts = slope_call(table, 0, near, downs, pre, 4)
    hidden = hidden_call(table, pre, step, 1)

    above_y, below_y, far, below_in, inputs, w_gate, w_up, _, _ = together(
        above_y, below_y, far, below_in, inputs, w_gate, w_up, firsts[0], hidden
    )
    far_y = tsend(below_y, X_UP)
    above_in, other_in = tsend(inputs, X_DOWN), tsend(inputs, Y_SWAP)
    far_y, above_in, other_in, below_in, w_gate_in, w_up_in = together(
        far_y, above_in, other_in, below_in, tsend(w_gate, CORE), tsend(w_up, CORE)
    )
    last = [above_y, below_y, far, far_y]
    rows_in = [inputs, other_in, above_in, below_in]
    above_y, below_y = tsend(other_in, X_DOWN), tsend(other_in, X_UP)
    down_own, down_other = weight_call(table, 0, NZ * NF, near + last, [(hidden,)], 12)
    down_other = tsend(down_other, CORE)
    above_y, below_y, below_in, _ = together(above_y, below_y, below_in, down_own)
    seconds = slope_call(table, half, last, after(downs, above_y, below_y, down_own), pre, 12)
    far, far_y = tsend(below_in, X_UP), tsend(above_y, X_DOWN)
    rows_in += [above_y, below_y, far, far_y]
    d_gate, d_up = zip(firsts, seconds)
    partial = input_call(*after((d_gate, d_up), down_other), (w_gate, w_gate_in, w_up, w_up_in), 12)
    far_down, one_down, three_down, rest_down = split(down_own + down_other)
    far_down = dsend(low(far_down), Z_FAR)

    d_gate, d_up = after((d_gate, d_up), partial[0, 0], far_down)
    far_own, far_other = weight_call(table, 0, NF, rows_in, (d_gate, d_up), 0.1)
    far_other = tsend(far_other, CORE)
    one, three = tsend(after(partial[1, 2], far), X_UP), tsend(after(partial[1, 3], far_y), X_DOWN)
    one_down, three_down = after((low(one_down), low(three_down)), partial[0, 0])
    one_down, three_down = dsend(one_down, Z_UP), dsend(three_down, Z_DOWN)
    d_gate, d_up, one, three, one_down, three_down, below = together(d_gate, d_up, one, three, one_down, three_down, partial[0, 2])
    d_gate, d_up = after((d_gate, d_up), far_own, far_other)
    rest_own, rest_other = weight_call(table, NF, NZ * NF - NF, rows_in, (d_gate, d_up), 12)
    far_sum = low(far_own + far_other)
    far_up, far_dn = dsend(far_sum[0], Z_UP), dsend(far_sum[1], Z_DOWN)
    above, below = tsend(low(partial[1, 1] + one), X_UP), tsend(below, X_DOWN)
    far_up, far_dn, rest_other, above, below, up = together(far_up, far_dn, rest_other, above, below, partial[0, 1])
    rest_one, rest_three, rest = split(rest_own + tsend(rest_other, CORE))
    rest_up = dsend(jnp.stack([low(rest_one[0] + far_up), low(rest_one[1])]), Z_UP)
    rest_dn = dsend(jnp.stack([low(rest_three[0]), low(rest_three[1] + far_dn)]), Z_DOWN)
    total = tsend(low(partial[1, 0] + above + three), Y_SWAP)
    below, up = tsend(low(partial[0, 3] + below), X_DOWN), tsend(up, X_UP)
    rest_up, rest_dn, below, up = together(rest_up, rest_dn, below, up)
    d_input = partial[0, 0] + below + up + total
    rest = rest + rest_up + rest_dn
    rest_down = rest_down + one_down + three_down + far_down
    down_part = (rest_down[0] + dsend(low(rest_down[1]), F_SWAP)).T
    both_part = rest[0] + dsend(low(rest[1]), F_SWAP)
    return (d_input, both_part[:, :width], both_part[:, width:], down_part)


def solution(mesh):
    in_specs = (
        P(("dp", "tensor"), None),
        P(("dp", "tensor"), None),
        P("dp", "tensor"),
        P("dp", "tensor"),
        P(None, "tensor"),
        P(None, "tensor"),
        P("tensor", None),
    )
    out_specs = (P(("dp", "tensor"), None), P("dp", "tensor"), P("dp", "tensor"), P("tensor", "dp"))
    return jax.shard_map(
        on_device, mesh=mesh, in_specs=in_specs, out_specs=out_specs, check_vma=False
    )
```

time: 482 us -> 197 us (0.41)
  waiting for transfers between devices: 403 us -> 48.5 us
  Pallas kernels: 0 us -> 62.8 us
  matrix products: 60.7 us -> 0 us
  starting transfers between devices: 0.42 us -> 53.2 us
  other arithmetic: 0 us -> 21.2 us
  between operations: 14.2 us -> 0.97 us
  local copies, waits for them, and re-layouts: 3.85 us -> 9.04 us
    reduce_scatter x4 -> x0, waiting for transfers between devices: 303 us -> none  [the longest x1 99.8 us: on_device(): lax.psum_scatter(term + jnp.einsum('rf,df->rd', up_all, w_up, preferred_e...]
    all_gather x2 -> x0, waiting for transfers between devices: 98.5 us -> none  [the longest x1 55.6 us: on_device(): piece = lax.all_gather(grad_out, 'tensor', axis=0, tiled=True)]
    pallas_call x0 -> x7, Pallas kernels: none -> 62.8 us  [the longest x3 27.7 us: weight_call(): pl.pallas_call(lambda *refs: weight_body(CHUNKS, wide, *refs), out_shape=...]
    dot_general x6 -> x0, matrix products: 60.7 us -> none  [the longest x1 11.8 us: on_device(): jnp.einsum('rf,df->rd', up_all, w_up, preferred_element_type=jnp.float32)]
    ppermute x0 -> x38, starting transfers between devices: none -> 53.2 us  [the longest x29 34.8 us: tsend(): return lax.ppermute(value, 'tensor', pairs)]
    ppermute x0 -> x38, waiting for transfers between devices: none -> 48.5 us  [the longest x29 42 us: tsend(): return lax.ppermute(value, 'tensor', pairs)]
    another operation x0 -> x5, other arithmetic: none -> 9.29 us
    convert_element_type x0 -> x4, other arithmetic: none -> 5.72 us  [low(): return value.astype(BF)]
  transfers between devices with their start and end apart: 6 -> 38, of which waited for: 6 -> 12; matrix products, arithmetic and copies ran while one was open for 11% -> 13% of each run, Pallas kernels for 0% -> 32%
where the time goes in v1:
time: 197 us; the launch traced here: 196 us
  Pallas kernels  62.8 us (32%)
  starting transfers between devices  53.2 us (27%)
  waiting for transfers between devices  48.5 us (25%)
  other arithmetic  21.2 us (11%)
  local copies, waits for them, and re-layouts  9.04 us (5%)
    ppermute x29, waiting for transfers between devices, tsend(): return lax.ppermute(value, 'tensor', pairs)  42 us
    ppermute x29, starting transfers between devices, tsend(): return lax.ppermute(value, 'tensor', pairs)  34.8 us
    pallas_call x3, Pallas kernels, weight_call(): pl.pallas_call(lambda *refs: weight_body(CHUNKS, wide, *refs), out_shape=...  27.7 us
    ppermute x9, starting transfers between devices, dsend(): return lax.ppermute(value, 'dp', pairs)  18.4 us
    pallas_call x2, Pallas kernels, slope_call(): pl.pallas_call(lambda *refs: slope_body(first, count, *refs), out_shape=(...  15.6 us
    pallas_call x1, Pallas kernels, input_call(): pl.pallas_call(lambda *refs: input_body(parts, *refs), out_shape=[jax.Sha...  12.5 us
    pallas_call x1, Pallas kernels, hidden_call(): pl.pallas_call(hidden_body, out_shape=jax.ShapeDtypeStruct((total, both),...  7.01 us
    ppermute x9, waiting for transfers between devices, dsend(): return lax.ppermute(value, 'dp', pairs)  6.53 us
  transfers between devices with their start and end apart: 38, of which 12 were waited for; matrix products, arithmetic and copies ran while one was open for 13% of the time, Pallas kernels for 32%

profile of v1, /device:TPU:0, one launch (start us, length us, event | category | flops | bytes accessed | tf_op | source)
XLA Modules:
  0.0 195.7 jit_solution(15938927719395405077)
XLA Ops:
  0.7 0.5 collective-permute-start.4
  1.2 1.6 collective-permute-start.2
  2.8 1.7 collective-permute-start.1
  4.5 1.7 collective-permute-start
  6.1 10.4 %collective-permute-done.2.refs_4_ = bf16[128,2048]{1,0:T(8,128)(2,1)S(1)} collective-permute-done((bf16[128,2048]{1,0:T(8,128)(2,1)}, bf16[128,2048]{1,0:T(8,128)(2,1)S(1)}, u32[]{:S(2)}, u32[]{:S(2)}) %collective-permute-start.2) | collective-permute-done | bytes 524320 | tf_op jit(solution)/shard_map/ppermute | solution.py:57
  16.7 1.5 collective-permute-done.refs_2_
  18.1 1.2 copy-done.13
  19.4 0.8 dynamic-slice_bitcast_fusion
  20.2 0.7 pad_add_fusion.refs_0_.table_ref
  20.8 0.4 collective-permute-start.7
  21.2 2.9 %collective-permute-start.6 = (bf16[128,2048]{1,0:T(8,128)(2,1)}, bf16[128,2048]{1,0:T(8,128)(2,1)}, u32[]{:S(2)}, u32[]{:S(2)}) collective-permute-start(bf16[128,2048]{1,0:T(8,128)(2,1)} %collective-permute-done.refs_2_), channel_id=1, source_target_pairs={{0,6},{1,7},{2,0},{3,1},{4,2},{5,3},{6,4},{7,5},{8,14},{9,15},{10,... | collective-permute-start | bytes 1572872 | tf_op jit(solution)/shard_map/ppermute | solution.py:57
  24.1 3.2 %collective-permute-start.8 = (bf16[128,2048]{1,0:T(8,128)(2,1)}, bf16[128,2048]{1,0:T(8,128)(2,1)}, u32[]{:S(2)}, u32[]{:S(2)}) collective-permute-start(bf16[128,2048]{1,0:T(8,128)(2,1)} %copy-done.17), channel_id=1, source_target_pairs={{0,6},{1,7},{2,0},{3,1},{4,2},{5,3},{6,4},{7,5},{8,14},{9,15},{10,... | collective-permute-start | bytes 1572872 | tf_op jit(solution)/shard_map/ppermute | solution.py:57
  27.3 7.0 %hidden.1.refs_9_ = bf16[1024,768]{1,0:T(8,128)(2,1)} custom-call(s32[16]{0:T(128)} %pad_add_fusion.refs_0_.table_ref, bf16[2048,384]{1,0:T(8,128)(2,1)} %refs_7_.3, bf16[2048,384]{1,0:T(8,128)(2,1)} %copy-done.3, bf16[2048,384]{1,0:T(8,128)(2,1)} %refs_9_.1, bf16[2048,384]{1,0:T(8,128)(2,1)} %collective-permute-done.5.refs_10_.refs_3_), custom_call_target="tpu_custom_call" | custom-call | flops 12582912 | bytes 4718592 | tf_op jit(solution)/shard_map/hidden/pallas_call | solution.py:87
  34.3 7.9 %slope.2 = (bf16[512,768]{1,0:T(8,128)(2,1)}, bf16[512,768]{1,0:T(8,128)(2,1)}) custom-call(s32[16]{0:T(128)} %pad_add_fusion.refs_0_.table_ref, bf16[128,2048]{1,0:T(8,128)(2,1)} %refs_1_.3, bf16[128,2048]{1,0:T(8,128)(2,1)} %collective-permute-done.refs_2_, bf16[128,2048]{1,0:T(8,128)(2,1)} %copy-done.17, bf16[128,2048]{1,0:T(8,128)(2,1)} %copy-done.16, ...), custom_call_target="tpu_custom_call" | custom-call | flops 6442450944 | bytes 33554432 | tf_op jit(solution)/shard_map/slope/pallas_call | solution.py:151
  42.2 5.6 %collective-permute-done.9.refs_4_ = bf16[128,2048]{1,0:T(8,128)(2,1)S(1)} collective-permute-done((bf16[128,2048]{1,0:T(8,128)(2,1)}, bf16[128,2048]{1,0:T(8,128)(2,1)S(1)}, u32[]{:S(2)}, u32[]{:S(2)}) %collective-permute-start.9) | collective-permute-done | bytes 524320 | tf_op jit(solution)/shard_map/ppermute | solution.py:57
  47.9 0.5 collective-permute-start.14
  48.4 0.4 collective-permute-start.10
  48.8 1.6 collective-permute-start.12
  50.3 2.9 %collective-permute-start.11 = (bf16[128,2048]{1,0:T(8,128)(2,1)S(1)}, bf16[128,2048]{1,0:T(8,128)(2,1)S(1)}, u32[]{:S(2)}, u32[]{:S(2)}) collective-permute-start(bf16[128,2048]{1,0:T(8,128)(2,1)S(1)} %copy-done.7), channel_id=1, source_target_pairs={{0,6},{1,7},{2,0},{3,1},{4,2},{5,3},{6,4},{7,5},{8,14},{9,15},{10,... | collective-permute-start | bytes 1572872 | tf_op jit(solution)/shard_map/ppermute | solution.py:57
  53.3 10.5 %collective-permute-done.10.refs_8_.refs_4_ = bf16[128,2048]{1,0:T(8,128)(2,1)S(1)} collective-permute-done((bf16[128,2048]{1,0:T(8,128)(2,1)}, bf16[128,2048]{1,0:T(8,128)(2,1)S(1)}, u32[]{:S(2)}, u32[]{:S(2)}) %collective-permute-start.10) | collective-permute-done | bytes 524320 | tf_op jit(solution)/shard_map/ppermute | solution.py:57
  63.7 0.4 collective-permute-done.11.refs_3_
  64.2 1.2 copy-done.14
  65.4 1.9 collective-permute-start.16
  67.2 3.0 %collective-permute-start.15 = (bf16[128,2048]{1,0:T(8,128)(2,1)S(1)}, bf16[128,2048]{1,0:T(8,128)(2,1)}, u32[]{:S(2)}, u32[]{:S(2)}) collective-permute-start(bf16[128,2048]{1,0:T(8,128)(2,1)S(1)} %collective-permute-done.12.refs_2_), channel_id=1, source_target_pairs={{0,6},{1,7},{2,0},{3,1},{4,2},{5,3},{6,4},{7,5},{8,14},{9,15},{10,... | collective-permute-start | bytes 1572872 | tf_op jit(solution)/shard_map/ppermute | solution.py:57
  70.2 10.4 %weight.3 = (f32[8,256,384]{2,1,0:T(8,128)}, bf16[8,256,384]{2,1,0:T(8,128)(2,1)}) custom-call(s32[16]{0:T(128)} %pad_add_fusion.refs_0_.table_ref, bf16[128,2048]{1,0:T(8,128)(2,1)} %refs_1_.3, bf16[128,2048]{1,0:T(8,128)(2,1)} %collective-permute-done.refs_2_, bf16[128,2048]{1,0:T(8,128)(2,1)} %copy-done.17, bf16[128,2048]{1,0:T(8,128)(2,1)} %copy-done.16, ...), custom_call_target="tpu_custom_call" | custom-call | flops 38654705664 | bytes 125829120 | tf_op jit(solution)/shard_map/weight/pallas_call | solution.py:205
  80.8 3.2 %collective-permute-start.19 = (bf16[128,2048]{1,0:T(8,128)(2,1)}, bf16[128,2048]{1,0:T(8,128)(2,1)}, u32[]{:S(2)}, u32[]{:S(2)}) collective-permute-start(bf16[128,2048]{1,0:T(8,128)(2,1)} %collective-permute-done.15.refs_5_), channel_id=1, source_target_pairs={{0,6},{1,7},{2,0},{3,1},{4,2},{5,3},{6,4},{7,5},{8,14},{9,15},{10,... | collective-permute-start | bytes 1572872 | tf_op jit(solution)/shard_map/ppermute | solution.py:57
  84.0 7.7 %slope.3 = (bf16[512,768]{1,0:T(8,128)(2,1)}, bf16[512,768]{1,0:T(8,128)(2,1)}) custom-call(s32[16]{0:T(128)} %pad_add_fusion.refs_0_.table_ref, bf16[128,2048]{1,0:T(8,128)(2,1)} %collective-permute-done.6.refs_5_.refs_1_, bf16[128,2048]{1,0:T(8,128)(2,1)} %collective-permute-done.7.refs_6_.refs_2_, ...), custom_call_target="tpu_custom_call" | custom-call | flops 19327352832 | bytes 100663296 | tf_op jit(solution)/shard_map/slope/pallas_call | solution.py:151
  91.8 1.2 copy-done.1
  93.0 2.8 %fusion.15 = (bf16[8,256,384]{2,1,0:T(8,128)(2,1)S(1)}, f32[8,256,384]{2,1,0:T(8,128)S(1)}) fusion(f32[8,256,384]{2,1,0:T(8,128)} %get-tuple-element.100, bf16[8,256,384]{2,1,0:T(8,128)(2,1)} %copy-done.1), kind=kLoop, calls=%fused_computation.37 | loop fusion | flops 2359296 | bytes 9437184 | tf_op jit(solution)/shard_map/convert.6
  95.8 1.0 fusion.17
  96.8 3.9 %collective-permute-start.20 = (bf16[2,256,384]{2,1,0:T(8,128)(2,1)}, bf16[2,256,384]{2,1,0:T(8,128)(2,1)}, u32[]{:S(2)}, u32[]{:S(2)}) collective-permute-start(bf16[2,256,384]{2,1,0:T(8,128)(2,1)} %get-tuple-element.174), channel_id=1, source_target_pairs={{0,64},{16,80},{32,96},{48,112},{64,0},{80,16},{96,32},{112,48},{1... | collective-permute-start | bytes 1179656 | tf_op jit(solution)/shard_map/ppermute | solution.py:61
  100.7 12.5 %input.1 = (f32[128,2048]{1,0:T(8,128)}, f32[128,2048]{1,0:T(8,128)}, bf16[128,2048]{1,0:T(8,128)(2,1)}, f32[128,2048]{1,0:T(8,128)}, f32[128,2048]{1,0:T(8,128)...) custom-call(bf16[512,768]{1,0:T(8,128)(2,1)} %get-tuple-element.135.refs_0_.refs_9_, ...), custom_call_target="tpu_custom_call" | custom-call | flops 77309411328 | bytes 176160768 | tf_op jit(solution)/shard_map/input/pallas_call | solution.py:244
  113.2 3.3 %collective-permute-start.22 = (bf16[128,2048]{1,0:T(8,128)(2,1)}, bf16[128,2048]{1,0:T(8,128)(2,1)S(1)}, u32[]{:S(2)}, u32[]{:S(2)}) collective-permute-start(bf16[128,2048]{1,0:T(8,128)(2,1)} %get-tuple-element.125), channel_id=1, source_target_pairs={{0,6},{1,7},{2,0},{3,1},{4,2},{5,3},{6,4},{7,5},{8,14},{9,15},{10,... | collective-permute-start | bytes 1572872 | tf_op jit(solution)/shard_map/ppermute | solution.py:57
  116.5 1.0 collective-permute-start.23
  117.6 2.2 %collective-permute-start.24 = (bf16[2,256,384]{2,1,0:T(8,128)(2,1)}, bf16[2,256,384]{2,1,0:T(8,128)(2,1)}, u32[]{:S(2)}, u32[]{:S(2)}) collective-permute-start(bf16[2,256,384]{2,1,0:T(8,128)(2,1)} %get-tuple-element.127), channel_id=1, source_target_pairs={{0,96},{16,112},{32,0},{48,16},{64,32},{80,48},{96,64},{112,80},{1... | collective-permute-start | bytes 1179656 | tf_op jit(solution)/shard_map/ppermute | solution.py:61
  119.8 6.1 %weight.4 = (f32[2,256,768]{2,1,0:T(8,128)}, bf16[2,256,768]{2,1,0:T(8,128)(2,1)}) custom-call(s32[16]{0:T(128)} %pad_add_fusion.refs_0_.table_ref, bf16[128,2048]{1,0:T(8,128)(2,1)} %refs_1_.5, bf16[128,2048]{1,0:T(8,128)(2,1)} %copy-done.9, bf16[128,2048]{1,0:T(8,128)(2,1)} %copy-done.10, bf16[128,2048]{1,0:T(8,128)(2,1)} %copy-done.8, ...), custom_call_target="tpu_custom_call" | custom-call | flops 161061280 | bytes 1048576 | tf_op jit(solution)/shard_map/weight/pallas_call | solution.py:205
  126.1 2.9 %collective-permute-done.21 = bf16[128,2048]{1,0:T(8,128)(2,1)} collective-permute-done((bf16[128,2048]{1,0:T(8,128)(2,1)}, bf16[128,2048]{1,0:T(8,128)(2,1)}, u32[]{:S(2)}, u32[]{:S(2)}) %collective-permute-start.21) | collective-permute-done | bytes 524320 | tf_op jit(solution)/shard_map/ppermute | solution.py:57
  129.0 2.3 %add_convert_fusion.3 = bf16[128,2048]{1,0:T(8,128)(2,1)} fusion(f32[128,2048]{1,0:T(8,128)} %get-tuple-element.141, bf16[128,2048]{1,0:T(8,128)(2,1)} %collective-permute-done.21), kind=kLoop, calls=%fused_computation.8 | loop fusion | flops 786432 | bytes 2097152 | tf_op jit(solution)/shard_map/convert_element_type | solution.py:65
  131.2 3.2 %collective-permute-start.29 = (bf16[128,2048]{1,0:T(8,128)(2,1)}, bf16[128,2048]{1,0:T(8,128)(2,1)}, u32[]{:S(2)}, u32[]{:S(2)}) collective-permute-start(bf16[128,2048]{1,0:T(8,128)(2,1)} %get-tuple-element.143), channel_id=1, source_target_pairs={{0,6},{1,7},{2,0},{3,1},{4,2},{5,3},{6,4},{7,5},{8,14},{9,15},{10,... | collective-permute-start | bytes 1572872 | tf_op jit(solution)/shard_map/ppermute | solution.py:57
  134.7 0.9 slice_bitcast_fusion.4
  135.6 0.7 collective-permute-start.27
  136.3 1.3 collective-permute-start.26
  137.6 11.1 %weight.5 = (f32[6,256,768]{2,1,0:T(8,128)}, bf16[6,256,768]{2,1,0:T(8,128)(2,1)}) custom-call(s32[16]{0:T(128)} %pad_add_fusion.refs_0_.table_ref, bf16[128,2048]{1,0:T(8,128)(2,1)} %refs_1_.5, bf16[128,2048]{1,0:T(8,128)(2,1)} %copy-done.9, bf16[128,2048]{1,0:T(8,128)(2,1)} %copy-done.10, bf16[128,2048]{1,0:T(8,128)(2,1)} %copy-done.8, ...), custom_call_target="tpu_custom_call" | custom-call | flops 57982058496 | bytes 125829120 | tf_op jit(solution)/shard_map/weight/pallas_call | solution.py:205
  148.9 1.4 fusion.2
  150.3 3.0 %collective-permute-start.37 = (bf16[256,384]{1,0:T(8,128)(2,1)S(1)}, bf16[256,384]{1,0:T(8,128)(2,1)S(1)}, u32[]{:S(2)}, u32[]{:S(2)}) collective-permute-start(bf16[256,384]{1,0:T(8,128)(2,1)S(1)} %fusion.13), channel_id=1, source_target_pairs={{0,16},{16,0},{32,48},{48,32},{64,80},{80,64},{96,112},{112,96},{1... | collective-permute-start | bytes 589832 | tf_op jit(solution)/shard_map/ppermute | solution.py:61
  153.6 3.1 %fusion.14 = (bf16[6,256,768]{2,1,0:T(8,128)(2,1)S(1)}, f32[6,256,768]{2,1,0:T(8,128)S(1)}) fusion(f32[6,256,768]{2,1,0:T(8,128)} %get-tuple-element.139, bf16[6,256,768]{2,1,0:T(8,128)(2,1)S(1)} %collective-permute-done.30), kind=kLoop, calls=%fused_computation.36 | loop fusion | flops 3538944 | bytes 14155776 | tf_op jit(solution)/shard_map/convert.3
  156.8 1.5 fusion.9
  158.3 0.6 copy-done
  158.9 1.0 pad_maximum_fusion
  159.9 1.0 collective-permute-start.31
  160.9 1.0 pad_maximum_fusion.1
  161.9 2.2 %collective-permute-start.32 = (bf16[2,256,768]{2,1,0:T(8,128)(2,1)}, bf16[2,256,768]{2,1,0:T(8,128)(2,1)S(1)}, u32[]{:S(2)}, u32[]{:S(2)}) collective-permute-start(bf16[2,256,768]{2,1,0:T(8,128)(2,1)} %pad_maximum_fusion.1), channel_id=1, source_target_pairs={{0,96},{16,112},{32,0},{48,16},{64,32},{80,48},{96,64},{112,80},{1... | collective-permute-start | bytes 2359304 | tf_op jit(solution)/shard_map/ppermute | solution.py:61
  164.1 2.0 %add_convert_fusion.2 = bf16[128,2048]{1,0:T(8,128)(2,1)} fusion(f32[128,2048]{1,0:T(8,128)S(1)} %copy-done.6, bf16[128,2048]{1,0:T(8,128)(2,1)} %collective-permute-done.29), kind=kLoop, calls=%fused_computation.7 | loop fusion | flops 786432 | bytes 2097152 | tf_op jit(solution)/shard_map/convert_element_type | solution.py:65
  166.2 1.9 collective-permute-start.34
  168.2 0.9 copy.13
  169.1 1.2 add_convert_fusion.1
  170.3 0.5 collective-permute-start.35
  170.9 9.0 %collective-permute-done.33 = bf16[128,2048]{1,0:T(8,128)(2,1)} collective-permute-done((bf16[128,2048]{1,0:T(8,128)(2,1)}, bf16[128,2048]{1,0:T(8,128)(2,1)}, u32[]{:S(2)}, u32[]{:S(2)}) %collective-permute-start.33) | collective-permute-done | bytes 524320 | tf_op jit(solution)/shard_map/ppermute | solution.py:57
  179.8 1.3 collective-permute-done.34
  181.4 1.6 fusion
  183.1 3.0 %collective-permute-start.36 = (bf16[256,768]{1,0:T(8,128)(2,1)S(1)}, bf16[256,768]{1,0:T(8,128)(2,1)S(1)}, u32[]{:S(2)}, u32[]{:S(2)}) collective-permute-start(bf16[256,768]{1,0:T(8,128)(2,1)S(1)} %fusion.10), channel_id=1, source_target_pairs={{0,16},{16,0},{32,48},{48,32},{64,80},{80,64},{96,112},{112,96},{1... | collective-permute-start | bytes 1179656 | tf_op jit(solution)/shard_map/ppermute | solution.py:61
  186.0 2.4 %convert_add_fusion.2 = f32[128,2048]{1,0:T(8,128)} fusion(bf16[128,2048]{1,0:T(8,128)(2,1)S(1)} %collective-permute-done.35, bf16[128,2048]{1,0:T(8,128)(2,1)} %collective-permute-done.34, f32[128,2048]{1,0:T(8,128)S(1)} %copy-done.4, bf16[128,2048]{1,0:T(8,128)(2,1)} %collective-permute-done.33), kind=kLoop, calls=%fused_computation.5 | loop fusion | flops 1572864 | bytes 3670016 | tf_op jit(solution)/shard_map/add | solution.py:324
  188.5 6.3 %collective-permute-done.36 = bf16[256,768]{1,0:T(8,128)(2,1)S(1)} collective-permute-done((bf16[256,768]{1,0:T(8,128)(2,1)S(1)}, bf16[256,768]{1,0:T(8,128)(2,1)S(1)}, u32[]{:S(2)}, u32[]{:S(2)}) %collective-permute-start.36) | collective-permute-done | bytes 393248 | tf_op jit(solution)/shard_map/ppermute | solution.py:61
  194.8 0.9 fusion.18
  (80 shorter events, 1.7 us)
Async XLA Ops:
  0.6 17.5 %collective-permute-start.3 = (bf16[384,2048]{1,0:T(8,128)(2,1)}, bf16[384,2048]{1,0:T(8,128)(2,1)S(1)}, u32[]{:S(2)}, u32[]{:S(2)}) collective-permute-start(bf16[384,2048]{1,0:T(8,128)(2,1)} %refs_5_.2), channel_id=1, source_target_pairs={{0,1},{1,0},{2,3},{3,2},{4,5},{5,4},{6,7},{7,6},{8,9},{9,8},{10,11... | collective-permute-start | bytes 4718600 | tf_op jit(solution)/shard_map/ppermute | solution.py:57
  0.7 17.4 %collective-permute-start.4 = (bf16[2048,384]{1,0:T(8,128)(2,1)}, bf16[2048,384]{1,0:T(8,128)(2,1)S(1)}, u32[]{:S(2)}, u32[]{:S(2)}) collective-permute-start(bf16[2048,384]{1,0:T(8,128)(2,1)} %refs_7_.3), channel_id=1, source_target_pairs={{0,1},{1,0},{2,3},{3,2},{4,5},{5,4},{6,7},{7,6},{8,9},{9,8},{10,11... | collective-permute-start | bytes 4718600 | tf_op jit(solution)/shard_map/ppermute | solution.py:57
  1.2 15.3 %collective-permute-start.2 = (bf16[128,2048]{1,0:T(8,128)(2,1)}, bf16[128,2048]{1,0:T(8,128)(2,1)S(1)}, u32[]{:S(2)}, u32[]{:S(2)}) collective-permute-start(bf16[128,2048]{1,0:T(8,128)(2,1)} %refs_1_.3), channel_id=1, source_target_pairs={{0,2},{1,3},{2,4},{3,5},{4,6},{5,7},{6,0},{7,1},{8,10},{9,11},{10,... | collective-permute-start | bytes 1572872 | tf_op jit(solution)/shard_map/ppermute | solution.py:57
  2.8 13.9 %collective-permute-start.1 = (bf16[128,2048]{1,0:T(8,128)(2,1)}, bf16[128,2048]{1,0:T(8,128)(2,1)S(1)}, u32[]{:S(2)}, u32[]{:S(2)}) collective-permute-start(bf16[128,2048]{1,0:T(8,128)(2,1)} %refs_1_.3), channel_id=1, source_target_pairs={{0,6},{1,7},{2,0},{3,1},{4,2},{5,3},{6,4},{7,5},{8,14},{9,15},{10,... | collective-permute-start | bytes 1572872 | tf_op jit(solution)/shard_map/ppermute | solution.py:57
  4.5 13.7 %collective-permute-start = (bf16[128,2048]{1,0:T(8,128)(2,1)}, bf16[128,2048]{1,0:T(8,128)(2,1)}, u32[]{:S(2)}, u32[]{:S(2)}) collective-permute-start(bf16[128,2048]{1,0:T(8,128)(2,1)} %refs_1_.3), channel_id=1, source_target_pairs={{0,8},{1,9},{2,10},{3,11},{4,12},{5,13},{6,14},{7,15},{8,0},{9,1},... | collective-permute-start | bytes 1572872 | tf_op jit(solution)/shard_map/ppermute | solution.py:57
  16.6 17.8 %copy-start.16 = (bf16[128,2048]{1,0:T(8,128)(2,1)}, bf16[128,2048]{1,0:T(8,128)(2,1)S(1)}, u32[]{:S(2)}) copy-start(bf16[128,2048]{1,0:T(8,128)(2,1)S(1)} %collective-permute-done.2.refs_4_) | copy-start | bytes 1572868
  16.6 2.7 %copy-start.17 = (bf16[128,2048]{1,0:T(8,128)(2,1)}, bf16[128,2048]{1,0:T(8,128)(2,1)S(1)}, u32[]{:S(2)}) copy-start(bf16[128,2048]{1,0:T(8,128)(2,1)S(1)} %collective-permute-done.1.refs_3_) | copy-start | bytes 1572868
  18.1 1.2 copy-start.13
  19.4 7.9 %copy-start.3 = (bf16[2048,384]{1,0:T(8,128)(2,1)}, bf16[2048,384]{1,0:T(8,128)(2,1)S(1)}, u32[]{:S(2)}) copy-start(bf16[2048,384]{1,0:T(8,128)(2,1)S(1)} %collective-permute-done.4.refs_8_.refs_1_) | copy-start | bytes 4718596
  19.4 7.9 %collective-permute-start.5 = (bf16[2048,384]{1,0:T(8,128)(2,1)}, bf16[2048,384]{1,0:T(8,128)(2,1)}, u32[]{:S(2)}, u32[]{:S(2)}) collective-permute-start(bf16[2048,384]{1,0:T(8,128)(2,1)} %refs_9_.1), channel_id=1, source_target_pairs={{0,1},{1,0},{2,3},{3,2},{4,5},{5,4},{6,7},{7,6},{8,9},{9,8},{10,11... | collective-permute-start | bytes 4718600 | tf_op jit(solution)/shard_map/ppermute | solution.py:57
  20.8 26.9 %collective-permute-start.7 = (bf16[128,2048]{1,0:T(8,128)(2,1)}, bf16[128,2048]{1,0:T(8,128)(2,1)}, u32[]{:S(2)}, u32[]{:S(2)}) collective-permute-start(bf16[128,2048]{1,0:T(8,128)(2,1)} %collective-permute-done.refs_2_), channel_id=1, source_target_pairs={{0,2},{1,3},{2,4},{3,5},{4,6},{5,7},{6,0},{7,1},{8,10},{9,11},{10,... | collective-permute-start | bytes 1572872 | tf_op jit(solution)/shard_map/ppermute | solution.py:57
  21.2 26.6 %collective-permute-start.6 = (bf16[128,2048]{1,0:T(8,128)(2,1)}, bf16[128,2048]{1,0:T(8,128)(2,1)}, u32[]{:S(2)}, u32[]{:S(2)}) collective-permute-start(bf16[128,2048]{1,0:T(8,128)(2,1)} %collective-permute-done.refs_2_), channel_id=1, source_target_pairs={{0,6},{1,7},{2,0},{3,1},{4,2},{5,3},{6,4},{7,5},{8,14},{9,15},{10,... | collective-permute-start | bytes 1572872 | tf_op jit(solution)/shard_map/ppermute | solution.py:57
  24.1 23.7 %collective-permute-start.9 = (bf16[128,2048]{1,0:T(8,128)(2,1)}, bf16[128,2048]{1,0:T(8,128)(2,1)S(1)}, u32[]{:S(2)}, u32[]{:S(2)}) collective-permute-start(bf16[128,2048]{1,0:T(8,128)(2,1)} %refs_1_.5), channel_id=1, source_target_pairs={{0,2},{1,3},{2,4},{3,5},{4,6},{5,7},{6,0},{7,1},{8,10},{9,11},{10,... | collective-permute-start | bytes 1572872 | tf_op jit(solution)/shard_map/ppermute | solution.py:57
  24.1 23.7 %collective-permute-start.8 = (bf16[128,2048]{1,0:T(8,128)(2,1)}, bf16[128,2048]{1,0:T(8,128)(2,1)}, u32[]{:S(2)}, u32[]{:S(2)}) collective-permute-start(bf16[128,2048]{1,0:T(8,128)(2,1)} %copy-done.17), channel_id=1, source_target_pairs={{0,6},{1,7},{2,0},{3,1},{4,2},{5,3},{6,4},{7,5},{8,14},{9,15},{10,... | collective-permute-start | bytes 1572872 | tf_op jit(solution)/shard_map/ppermute | solution.py:57
  34.3 14.4 %copy-start.7 = (bf16[128,2048]{1,0:T(8,128)(2,1)S(1)}, bf16[128,2048]{1,0:T(8,128)(2,1)}, u32[]{:S(2)}) copy-start(bf16[128,2048]{1,0:T(8,128)(2,1)} %refs_1_.5) | copy-start | bytes 1572868
  47.8 36.3 %copy-start.8 = (bf16[128,2048]{1,0:T(8,128)(2,1)}, bf16[128,2048]{1,0:T(8,128)(2,1)S(1)}, u32[]{:S(2)}) copy-start(bf16[128,2048]{1,0:T(8,128)(2,1)S(1)} %collective-permute-done.9.refs_4_) | copy-start | bytes 1572868
  47.8 16.4 %collective-permute-start.13 = (bf16[2048,384]{1,0:T(8,128)(2,1)}, bf16[2048,384]{1,0:T(8,128)(2,1)S(1)}, u32[]{:S(2)}, u32[]{:S(2)}) collective-permute-start(bf16[2048,384]{1,0:T(8,128)(2,1)} %refs_4_), channel_id=1, source_target_pairs={{0,1},{1,0},{2,3},{3,2},{4,5},{5,4},{6,7},{7,6},{8,9},{9,8},{10,11... | collective-permute-start | bytes 4718600 | tf_op jit(solution)/shard_map/ppermute | solution.py:57
  47.9 16.3 %collective-permute-start.14 = (bf16[2048,384]{1,0:T(8,128)(2,1)}, bf16[2048,384]{1,0:T(8,128)(2,1)S(1)}, u32[]{:S(2)}, u32[]{:S(2)}) collective-permute-start(bf16[2048,384]{1,0:T(8,128)(2,1)} %refs_6_), channel_id=1, source_target_pairs={{0,1},{1,0},{2,3},{3,2},{4,5},{5,4},{6,7},{7,6},{8,9},{9,8},{10,11... | collective-permute-start | bytes 4718600 | tf_op jit(solution)/shard_map/ppermute | solution.py:57
  48.4 15.4 %collective-permute-start.10 = (bf16[128,2048]{1,0:T(8,128)(2,1)}, bf16[128,2048]{1,0:T(8,128)(2,1)S(1)}, u32[]{:S(2)}, u32[]{:S(2)}) collective-permute-start(bf16[128,2048]{1,0:T(8,128)(2,1)} %collective-permute-done.7.refs_6_.refs_2_), channel_id=1, source_target_pairs={{0,2},{1,3},{2,4},{3,5},{4,6},{5,7},{6,0},{7,1},{8,10},{9,11},{10,... | collective-permute-start | bytes 1572872 | tf_op jit(solution)/shard_map/ppermute | solution.py:57
  48.8 15.0 %collective-permute-start.12 = (bf16[128,2048]{1,0:T(8,128)(2,1)S(1)}, bf16[128,2048]{1,0:T(8,128)(2,1)S(1)}, u32[]{:S(2)}, u32[]{:S(2)}) collective-permute-start(bf16[128,2048]{1,0:T(8,128)(2,1)S(1)} %copy-done.7), channel_id=1, source_target_pairs={{0,8},{1,9},{2,10},{3,11},{4,12},{5,13},{6,14},{7,15},{8,0},{9,1},... | collective-permute-start | bytes 1572872 | tf_op jit(solution)/shard_map/ppermute | solution.py:57
  50.3 13.8 %collective-permute-start.11 = (bf16[128,2048]{1,0:T(8,128)(2,1)S(1)}, bf16[128,2048]{1,0:T(8,128)(2,1)S(1)}, u32[]{:S(2)}, u32[]{:S(2)}) collective-permute-start(bf16[128,2048]{1,0:T(8,128)(2,1)S(1)} %copy-done.7), channel_id=1, source_target_pairs={{0,6},{1,7},{2,0},{3,1},{4,2},{5,3},{6,4},{7,5},{8,14},{9,15},{10,... | collective-permute-start | bytes 1572872 | tf_op jit(solution)/shard_map/ppermute | solution.py:57
  63.7 6.5 %copy-start.18 = (bf16[128,2048]{1,0:T(8,128)(2,1)}, bf16[128,2048]{1,0:T(8,128)(2,1)S(1)}, u32[]{:S(2)}) copy-start(bf16[128,2048]{1,0:T(8,128)(2,1)S(1)} %collective-permute-done.10.refs_8_.refs_4_) | copy-start | bytes 1572868
  63.7 17.0 %copy-start.9 = (bf16[128,2048]{1,0:T(8,128)(2,1)}, bf16[128,2048]{1,0:T(8,128)(2,1)S(1)}, u32[]{:S(2)}) copy-start(bf16[128,2048]{1,0:T(8,128)(2,1)S(1)} %collective-permute-done.12.refs_2_) | copy-start | bytes 1572868
  64.2 16.5 %copy-start.10 = (bf16[128,2048]{1,0:T(8,128)(2,1)}, bf16[128,2048]{1,0:T(8,128)(2,1)S(1)}, u32[]{:S(2)}) copy-start(bf16[128,2048]{1,0:T(8,128)(2,1)S(1)} %collective-permute-done.11.refs_3_) | copy-start | bytes 1572868
  64.2 1.2 copy-start.14
  65.4 1.9 copy-start.15
  65.4 15.4 %collective-permute-start.16 = (bf16[128,2048]{1,0:T(8,128)(2,1)S(1)}, bf16[128,2048]{1,0:T(8,128)(2,1)S(1)}, u32[]{:S(2)}, u32[]{:S(2)}) collective-permute-start(bf16[128,2048]{1,0:T(8,128)(2,1)S(1)} %collective-permute-done.12.refs_2_), channel_id=1, source_target_pairs={{0,2},{1,3},{2,4},{3,5},{4,6},{5,7},{6,0},{7,1},{8,10},{9,11},{10,... | collective-permute-start | bytes 1572872 | tf_op jit(solution)/shard_map/ppermute | solution.py:57
  67.2 13.6 %collective-permute-start.15 = (bf16[128,2048]{1,0:T(8,128)(2,1)S(1)}, bf16[128,2048]{1,0:T(8,128)(2,1)}, u32[]{:S(2)}, u32[]{:S(2)}) collective-permute-start(bf16[128,2048]{1,0:T(8,128)(2,1)S(1)} %collective-permute-done.12.refs_2_), channel_id=1, source_target_pairs={{0,6},{1,7},{2,0},{3,1},{4,2},{5,3},{6,4},{7,5},{8,14},{9,15},{10,... | collective-permute-start | bytes 1572872 | tf_op jit(solution)/shard_map/ppermute | solution.py:57
  80.7 11.1 %collective-permute-start.17 = (bf16[8,256,384]{2,1,0:T(8,128)(2,1)}, bf16[8,256,384]{2,1,0:T(8,128)(2,1)S(1)}, u32[]{:S(2)}, u32[]{:S(2)}) collective-permute-start(bf16[8,256,384]{2,1,0:T(8,128)(2,1)} %get-tuple-element.108), channel_id=1, source_target_pairs={{0,1},{1,0},{2,3},{3,2},{4,5},{5,4},{6,7},{7,6},{8,9},{9,8},{10,11... | collective-permute-start | bytes 4718600 | tf_op jit(solution)/shard_map/ppermute | solution.py:57
  80.8 10.9 %copy-start.11 = (bf16[128,2048]{1,0:T(8,128)(2,1)}, bf16[128,2048]{1,0:T(8,128)(2,1)S(1)}, u32[]{:S(2)}) copy-start(bf16[128,2048]{1,0:T(8,128)(2,1)S(1)} %collective-permute-done.16.refs_6_) | copy-start | bytes 1572868
  80.8 32.4 %collective-permute-start.19 = (bf16[128,2048]{1,0:T(8,128)(2,1)}, bf16[128,2048]{1,0:T(8,128)(2,1)}, u32[]{:S(2)}, u32[]{:S(2)}) collective-permute-start(bf16[128,2048]{1,0:T(8,128)(2,1)} %collective-permute-done.15.refs_5_), channel_id=1, source_target_pairs={{0,6},{1,7},{2,0},{3,1},{4,2},{5,3},{6,4},{7,5},{8,14},{9,15},{10,... | collective-permute-start | bytes 1572872 | tf_op jit(solution)/shard_map/ppermute | solution.py:57
  84.0 29.2 %collective-permute-start.18 = (bf16[128,2048]{1,0:T(8,128)(2,1)S(1)}, bf16[128,2048]{1,0:T(8,128)(2,1)}, u32[]{:S(2)}, u32[]{:S(2)}) collective-permute-start(bf16[128,2048]{1,0:T(8,128)(2,1)S(1)} %collective-permute-done.9.refs_4_), channel_id=1, source_target_pairs={{0,2},{1,3},{2,4},{3,5},{4,6},{5,7},{6,0},{7,1},{8,10},{9,11},{10,... | collective-permute-start | bytes 1572872 | tf_op jit(solution)/shard_map/ppermute | solution.py:57
  91.8 1.2 copy-start.1
  96.8 22.9 %collective-permute-start.20 = (bf16[2,256,384]{2,1,0:T(8,128)(2,1)}, bf16[2,256,384]{2,1,0:T(8,128)(2,1)}, u32[]{:S(2)}, u32[]{:S(2)}) collective-permute-start(bf16[2,256,384]{2,1,0:T(8,128)(2,1)} %get-tuple-element.174), channel_id=1, source_target_pairs={{0,64},{16,80},{32,96},{48,112},{64,0},{80,16},{96,32},{112,48},{1... | collective-permute-start | bytes 1179656 | tf_op jit(solution)/shard_map/ppermute | solution.py:61
  113.2 12.8 %collective-permute-start.22 = (bf16[128,2048]{1,0:T(8,128)(2,1)}, bf16[128,2048]{1,0:T(8,128)(2,1)S(1)}, u32[]{:S(2)}, u32[]{:S(2)}) collective-permute-start(bf16[128,2048]{1,0:T(8,128)(2,1)} %get-tuple-element.125), channel_id=1, source_target_pairs={{0,6},{1,7},{2,0},{3,1},{4,2},{5,3},{6,4},{7,5},{8,14},{9,15},{10,... | collective-permute-start | bytes 1572872 | tf_op jit(solution)/shard_map/ppermute | solution.py:57
  116.5 12.4 %collective-permute-start.21 = (bf16[128,2048]{1,0:T(8,128)(2,1)}, bf16[128,2048]{1,0:T(8,128)(2,1)}, u32[]{:S(2)}, u32[]{:S(2)}) collective-permute-start(bf16[128,2048]{1,0:T(8,128)(2,1)} %get-tuple-element.123), channel_id=1, source_target_pairs={{0,2},{1,3},{2,4},{3,5},{4,6},{5,7},{6,0},{7,1},{8,10},{9,11},{10,... | collective-permute-start | bytes 1572872 | tf_op jit(solution)/shard_map/ppermute | solution.py:57
  116.5 9.5 %collective-permute-start.23 = (bf16[2,256,384]{2,1,0:T(8,128)(2,1)}, bf16[2,256,384]{2,1,0:T(8,128)(2,1)S(1)}, u32[]{:S(2)}, u32[]{:S(2)}) collective-permute-start(bf16[2,256,384]{2,1,0:T(8,128)(2,1)} %get-tuple-element.126), channel_id=1, source_target_pairs={{0,32},{16,48},{32,64},{48,80},{64,96},{80,112},{96,0},{112,16},{1... | collective-permute-start | bytes 1179656 | tf_op jit(solution)/shard_map/ppermute | solution.py:61
  117.6 8.5 %collective-permute-start.24 = (bf16[2,256,384]{2,1,0:T(8,128)(2,1)}, bf16[2,256,384]{2,1,0:T(8,128)(2,1)}, u32[]{:S(2)}, u32[]{:S(2)}) collective-permute-start(bf16[2,256,384]{2,1,0:T(8,128)(2,1)} %get-tuple-element.127), channel_id=1, source_target_pairs={{0,96},{16,112},{32,0},{48,16},{64,32},{80,48},{96,64},{112,80},{1... | collective-permute-start | bytes 1179656 | tf_op jit(solution)/shard_map/ppermute | solution.py:61
  125.9 8.6 %copy-start.2 = (f32[2,256,768]{2,1,0:T(8,128)S(1)}, f32[2,256,768]{2,1,0:T(8,128)}, u32[]{:S(2)}) copy-start(f32[2,256,768]{2,1,0:T(8,128)} %get-tuple-element.133) | copy-start | bytes 4718596
  125.9 8.6 %collective-permute-start.25 = (bf16[2,256,768]{2,1,0:T(8,128)(2,1)}, bf16[2,256,768]{2,1,0:T(8,128)(2,1)S(1)}, u32[]{:S(2)}, u32[]{:S(2)}) collective-permute-start(bf16[2,256,768]{2,1,0:T(8,128)(2,1)} %get-tuple-element.134), channel_id=1, source_target_pairs={{0,1},{1,0},{2,3},{3,2},{4,5},{5,4},{6,7},{7,6},{8,9},{9,8},{10,11... | collective-permute-start | bytes 2359304 | tf_op jit(solution)/shard_map/ppermute | solution.py:57
  126.1 8.6 %copy-start.12 = (bf16[2,256,384]{2,1,0:T(8,128)(2,1)}, bf16[2,256,384]{2,1,0:T(8,128)(2,1)S(1)}, u32[]{:S(2)}) copy-start(bf16[2,256,384]{2,1,0:T(8,128)(2,1)S(1)} %collective-permute-done.23) | copy-start | bytes 1179652
  131.2 17.5 %collective-permute-start.28 = (bf16[128,2048]{1,0:T(8,128)(2,1)}, bf16[128,2048]{1,0:T(8,128)(2,1)}, u32[]{:S(2)}, u32[]{:S(2)}) collective-permute-start(bf16[128,2048]{1,0:T(8,128)(2,1)} %add_convert_fusion.3), channel_id=1, source_target_pairs={{0,2},{1,3},{2,4},{3,5},{4,6},{5,7},{6,0},{7,1},{8,10},{9,11},{10,... | collective-permute-start | bytes 1572872 | tf_op jit(solution)/shard_map/ppermute | solution.py:57
  131.2 17.5 %collective-permute-start.29 = (bf16[128,2048]{1,0:T(8,128)(2,1)}, bf16[128,2048]{1,0:T(8,128)(2,1)}, u32[]{:S(2)}, u32[]{:S(2)}) collective-permute-start(bf16[128,2048]{1,0:T(8,128)(2,1)} %get-tuple-element.143), channel_id=1, source_target_pairs={{0,6},{1,7},{2,0},{3,1},{4,2},{5,3},{6,4},{7,5},{8,14},{9,15},{10,... | collective-permute-start | bytes 1572872 | tf_op jit(solution)/shard_map/ppermute | solution.py:57
  135.6 13.2 %collective-permute-start.27 = (bf16[256,768]{1,0:T(8,128)(2,1)}, bf16[256,768]{1,0:T(8,128)(2,1)S(1)}, u32[]{:S(2)}, u32[]{:S(2)}) collective-permute-start(bf16[256,768]{1,0:T(8,128)(2,1)} %get-tuple-element.177), channel_id=1, source_target_pairs={{0,96},{16,112},{32,0},{48,16},{64,32},{80,48},{96,64},{112,80},{1... | collective-permute-start | bytes 1179656 | tf_op jit(solution)/shard_map/ppermute | solution.py:61
  136.3 12.5 %collective-permute-start.26 = (bf16[256,768]{1,0:T(8,128)(2,1)}, bf16[256,768]{1,0:T(8,128)(2,1)}, u32[]{:S(2)}, u32[]{:S(2)}) collective-permute-start(bf16[256,768]{1,0:T(8,128)(2,1)} %get-tuple-element.178), channel_id=1, source_target_pairs={{0,32},{16,48},{32,64},{48,80},{64,96},{80,112},{96,0},{112,16},{1... | collective-permute-start | bytes 1179656 | tf_op jit(solution)/shard_map/ppermute | solution.py:61
  148.8 4.8 %collective-permute-start.30 = (bf16[6,256,768]{2,1,0:T(8,128)(2,1)}, bf16[6,256,768]{2,1,0:T(8,128)(2,1)S(1)}, u32[]{:S(2)}, u32[]{:S(2)}) collective-permute-start(bf16[6,256,768]{2,1,0:T(8,128)(2,1)} %get-tuple-element.145), channel_id=1, source_target_pairs={{0,1},{1,0},{2,3},{3,2},{4,5},{5,4},{6,7},{7,6},{8,9},{9,8},{10,11... | collective-permute-start | bytes 7077896 | tf_op jit(solution)/shard_map/ppermute | solution.py:57
  150.3 17.8 %collective-permute-start.37 = (bf16[256,384]{1,0:T(8,128)(2,1)S(1)}, bf16[256,384]{1,0:T(8,128)(2,1)S(1)}, u32[]{:S(2)}, u32[]{:S(2)}) collective-permute-start(bf16[256,384]{1,0:T(8,128)(2,1)S(1)} %fusion.13), channel_id=1, source_target_pairs={{0,16},{16,0},{32,48},{48,32},{64,80},{80,64},{96,112},{112,96},{1... | collective-permute-start | bytes 589832 | tf_op jit(solution)/shard_map/ppermute | solution.py:61
  156.7 2.2 %copy-start = (f32[6,256,768]{2,1,0:T(8,128)}, f32[6,256,768]{2,1,0:T(8,128)S(1)}, u32[]{:S(2)}) copy-start(f32[6,256,768]{2,1,0:T(8,128)S(1)} %get-tuple-element.165) | copy-start | bytes 14155780
  158.9 5.2 %copy-start.6 = (f32[128,2048]{1,0:T(8,128)S(1)}, f32[128,2048]{1,0:T(8,128)}, u32[]{:S(2)}) copy-start(f32[128,2048]{1,0:T(8,128)} %get-tuple-element.148) | copy-start | bytes 3145732
  159.9 21.3 %collective-permute-start.31 = (bf16[2,256,768]{2,1,0:T(8,128)(2,1)}, bf16[2,256,768]{2,1,0:T(8,128)(2,1)S(1)}, u32[]{:S(2)}, u32[]{:S(2)}) collective-permute-start(bf16[2,256,768]{2,1,0:T(8,128)(2,1)} %pad_maximum_fusion), channel_id=1, source_target_pairs={{0,32},{16,48},{32,64},{48,80},{64,96},{80,112},{96,0},{112,16},{1... | collective-permute-start | bytes 2359304 | tf_op jit(solution)/shard_map/ppermute | solution.py:61
  161.9 19.5 %collective-permute-start.32 = (bf16[2,256,768]{2,1,0:T(8,128)(2,1)}, bf16[2,256,768]{2,1,0:T(8,128)(2,1)S(1)}, u32[]{:S(2)}, u32[]{:S(2)}) collective-permute-start(bf16[2,256,768]{2,1,0:T(8,128)(2,1)} %pad_maximum_fusion.1), channel_id=1, source_target_pairs={{0,96},{16,112},{32,0},{48,16},{64,32},{80,48},{96,64},{112,80},{1... | collective-permute-start | bytes 2359304 | tf_op jit(solution)/shard_map/ppermute | solution.py:61
  164.1 5.0 %copy-start.5 = (f32[128,2048]{1,0:T(8,128)S(1)}, f32[128,2048]{1,0:T(8,128)}, u32[]{:S(2)}) copy-start(f32[128,2048]{1,0:T(8,128)} %get-tuple-element.153) | copy-start | bytes 3145732
  166.1 13.7 %collective-permute-start.33 = (bf16[128,2048]{1,0:T(8,128)(2,1)}, bf16[128,2048]{1,0:T(8,128)(2,1)}, u32[]{:S(2)}, u32[]{:S(2)}) collective-permute-start(bf16[128,2048]{1,0:T(8,128)(2,1)} %add_convert_fusion.2), channel_id=1, source_target_pairs={{0,6},{1,7},{2,0},{3,1},{4,2},{5,3},{6,4},{7,5},{8,14},{9,15},{10,... | collective-permute-start | bytes 1572872 | tf_op jit(solution)/shard_map/ppermute | solution.py:57
  166.2 14.9 %collective-permute-start.34 = (bf16[128,2048]{1,0:T(8,128)(2,1)}, bf16[128,2048]{1,0:T(8,128)(2,1)}, u32[]{:S(2)}, u32[]{:S(2)}) collective-permute-start(bf16[128,2048]{1,0:T(8,128)(2,1)} %get-tuple-element.150), channel_id=1, source_target_pairs={{0,2},{1,3},{2,4},{3,5},{4,6},{5,7},{6,0},{7,1},{8,10},{9,11},{10,... | collective-permute-start | bytes 1572872 | tf_op jit(solution)/shard_map/ppermute | solution.py:57
  170.3 15.7 %copy-start.4 = (f32[128,2048]{1,0:T(8,128)S(1)}, f32[128,2048]{1,0:T(8,128)}, u32[]{:S(2)}) copy-start(f32[128,2048]{1,0:T(8,128)} %get-tuple-element.115) | copy-start | bytes 3145732
  170.3 15.7 %collective-permute-start.35 = (bf16[128,2048]{1,0:T(8,128)(2,1)S(1)}, bf16[128,2048]{1,0:T(8,128)(2,1)S(1)}, u32[]{:S(2)}, u32[]{:S(2)}) collective-permute-start(bf16[128,2048]{1,0:T(8,128)(2,1)S(1)} %add_convert_fusion.1), channel_id=1, source_target_pairs={{0,8},{1,9},{2,10},{3,11},{4,12},{5,13},{6,14},{7,15},{8,0},{9,1},... | collective-permute-start | bytes 1572872 | tf_op jit(solution)/shard_map/ppermute | solution.py:57
  183.1 11.7 %collective-permute-start.36 = (bf16[256,768]{1,0:T(8,128)(2,1)S(1)}, bf16[256,768]{1,0:T(8,128)(2,1)S(1)}, u32[]{:S(2)}, u32[]{:S(2)}) collective-permute-start(bf16[256,768]{1,0:T(8,128)(2,1)S(1)} %fusion.10), channel_id=1, source_target_pairs={{0,16},{16,0},{32,48},{48,32},{64,80},{80,64},{96,112},{112,96},{1... | collective-permute-start | bytes 1179656 | tf_op jit(solution)/shard_map/ppermute | solution.py:61

commit v2 on v1

--- a/solution.py
+++ b/solution.py
@@ -11,7 +11,6 @@
 BF, F32 = jnp.bfloat16, jnp.float32
 ORDER = [(0, 0), (1, 0), (0, 1), (0, 3), (1, 1), (1, 3), (0, 2), (1, 2)]
 CHUNKS = len(ORDER)
-FARTHEST = (2, 1, 3, 0)
 
 
 def tensor_pairs(move):
@@ -33,6 +32,7 @@
 Z_FAR = dp_pairs(lambda z, f: ((z + 2) % NZ, f))
 F_SWAP = dp_pairs(lambda z, f: (z, 1 - f))
 
+FARTHEST = (2, 1, 3, 0)
 ROWS = np.array(
     [
         [((y ^ dy) * NX + (x + dx) % NX) * NC + c for dy, dx in ORDER]
@@ -40,13 +40,7 @@
     ],
     np.int32,
 )
-SLABS = np.array(
-    [
-        [((z + dz) % NZ) * NF + (f ^ df) for dz in FARTHEST for df in range(NF)]
-        for z in range(NZ) for f in range(NF)
-    ],
-    np.int32,
-)
+SLABS = np.array([[*((z + dz) % NZ for dz in FARTHEST), f] for z in range(NZ) for f in range(NF)], np.int32)
 ANY = pl.BlockSpec(memory_space=pltpu.HBM)
 VMEM = pl.BlockSpec(memory_space=pltpu.VMEM)
 NT = (((1,), (1,)), ((), ()))
@@ -66,7 +60,7 @@
 
 
 def params():
-    return pltpu.CompilerParams(vmem_limit_bytes=60 << 20)
+    return pltpu.CompilerParams(vmem_limit_bytes=24 << 20)
 
 
 def cost(effort, flops, moved):
@@ -103,14 +97,15 @@
     chunks, refs = refs[:count], refs[count:]
     down_pair, pre, (dgate_ref, dup_ref) = refs[:2], refs[2:6], refs[6:8]
     cot, down, gates, uppers, chunk_sem, down_sem, pre_sem = refs[8:]
-    step = chunks[0].shape[0]
+    step = cot.shape[0] // (CHUNKS // 2)
     width = pre[0].shape[1]
+    starts = np.cumsum([0] + [c.shape[0] for c in chunks]).tolist()
 
     def down_copy(j):
         return pltpu.make_async_copy(down_pair[j], down.at[pl.ds(j * width, width)], down_sem.at[j])
 
     def chunk_copy(k):
-        return pltpu.make_async_copy(chunks[k], cot.at[pl.ds(k * step, step)], chunk_sem.at[k])
+        return pltpu.make_async_copy(chunks[k], cot.at[pl.ds(starts[k], chunks[k].shape[0])], chunk_sem.at[k])
 
     def pre_copy(k, j):
         target = (gates, uppers)[j // 2]
@@ -124,14 +119,17 @@
         down_copy(j).start()
     for k in range(count):
         chunk_copy(k).start()
+    for k in range(CHUNKS // 2):
         for j in range(4):
             pre_copy(k, j).start()
     for j in range(2):
         down_copy(j).wait()
     tile = 2 * step
-    for i in range(count // 2):
+    for i in range(CHUNKS // 4):
+        for k in range(count):
+            if i * tile <= starts[k] < (i + 1) * tile:
+                chunk_copy(k).wait()
         for k in (2 * i, 2 * i + 1):
-            chunk_copy(k).wait()
             for j in range(4):
                 pre_copy(k, j).wait()
         at = pl.ds(i * tile, tile)
@@ -144,9 +142,9 @@
 
 def slope_call(table, first, chunks, downs, pre, effort):
     count = len(chunks)
-    step, depth = chunks[0].shape
+    total, depth = sum(c.shape[0] for c in chunks), chunks[0].shape[1]
     width = downs[0].shape[0]
-    total, both = step * count, NC * width
+    both = NC * width
     out = jax.ShapeDtypeStruct((total, both), BF)
     return pl.pallas_call(
         lambda *refs: slope_body(first, count, *refs),
@@ -163,7 +161,7 @@
                 pltpu.VMEM((total, both), BF),
                 pltpu.SemaphoreType.DMA((count,)),
                 pltpu.SemaphoreType.DMA((2,)),
-                pltpu.SemaphoreType.DMA((count, 4)),
+                pltpu.SemaphoreType.DMA((CHUNKS // 2, 4)),
             ],
         ),
         compiler_params=params(),
@@ -175,47 +173,81 @@
 def weight_body(count, wide, table_ref, *refs):
     chunks, rights, (own_ref, other_ref) = refs[:count], refs[count:-2], refs[-2:]
     parts = len(rights) // wide
-    step = chunks[0].shape[0]
-    per = count // parts
+    features = own_ref.shape[1]
     width = own_ref.shape[2] // wide
+    far = table_ref[CHUNKS + NZ]
+    starts = np.cumsum([0] + [c.shape[0] for c in chunks]).tolist()
+    per = starts[-1] // parts
+    lefts = [
+        jnp.concatenate([c[...] for c, start in zip(chunks, starts) if p * per <= start < (p + 1) * per], axis=0)
+        for p in range(parts)
+    ]
     for w in range(wide):
         both = None
         for p in range(parts):
-            left = jnp.concatenate([c[...] for c in chunks[p * per : (p + 1) * per]], axis=0)
-            term = lax.dot_general(left, rights[w * parts + p][...], TN, preferred_element_type=F32)
+            term = lax.dot_general(lefts[p], rights[w * parts + p][...], TN, preferred_element_type=F32)
             both = term if both is None else both + term
-        own_ref[0, :, w * width : (w + 1) * width] = both[:, :width]
-        other_ref[0, :, w * width : (w + 1) * width] = both[:, width:].astype(BF)
-
-
-def weight_call(table, first, slabs, sources, rights, effort):
-    wide, parts = len(rights), len(rights[0])
+        at = pl.ds(w * width, width)
+        for f in range(NF):
+            slab = both[f * features : (f + 1) * features]
+            own_ref[f ^ far, :, at] = slab[:, :width]
+            other_ref[f ^ far, :, at] = slab[:, width:].astype(BF)
+
+
+def weight_call(table, first, blocks, chunks, rights, effort):
+    count, wide, parts = len(chunks), len(rights), len(rights[0])
     rows, both = rights[0][0].shape
-    step, depth = rows * parts // CHUNKS, sources[0].shape[1]
+    depth = chunks[0].shape[1]
     features = depth // (NZ * NF)
-    slab = (slabs, features, wide * both // NC)
-    at = lambda r, t: t[CHUNKS + first + r]
-    if len(sources) == 1:
-        chunks = sources * CHUNKS
-        maps = [lambda r, t, k=k: (t[k], at(r, t)) for k in range(CHUNKS)]
-    else:
-        chunks = sources
-        maps = [lambda r, t: (0, at(r, t))] * CHUNKS
-    block = pl.BlockSpec((1, *slab[1:]), lambda r, t: (r, 0, 0))
+    slab = (blocks * NF, features, wide * both // NC)
+    block = pl.BlockSpec((NF, *slab[1:]), lambda r, t: (r, 0, 0))
     return pl.pallas_call(
-        lambda *refs: weight_body(CHUNKS, wide, *refs),
+        lambda *refs: weight_body(count, wide, *refs),
         out_shape=(jax.ShapeDtypeStruct(slab, F32), jax.ShapeDtypeStruct(slab, BF)),
         grid_spec=pltpu.PrefetchScalarGridSpec(
             num_scalar_prefetch=1,
-            grid=(slab[0],),
-            in_specs=[pl.BlockSpec((step, features), m) for m in maps]
+            grid=(blocks,),
+            in_specs=[pl.BlockSpec((c.shape[0], NF * features), lambda r, t: (0, t[CHUNKS + first + r])) for c in chunks]
             + [pl.BlockSpec((rows, both), lambda r, t: (0, 0))] * (wide * parts),
             out_specs=[block, block],
         ),
         compiler_params=params(),
-        cost_estimate=cost(effort, 2 * slabs * features * rows * parts * both * wide, 10 << 20),
+        cost_estimate=cost(effort, 2 * blocks * NF * features * rows * parts * both * wide, 10 << 20),
         name="weight",
     )(table, *chunks, *[part for right in rights for part in right])
+
+
+def ring_body(own_up, own_down, in_up, in_down, far_up, far_down, up_ref, down_ref):
+    up = own_up[...] + in_up[...].astype(F32)
+    down = own_down[...] + in_down[...].astype(F32)
+
+    @pl.when(pl.program_id(0) == 0)
+    def _():
+        up_ref[...] = (up + far_up[...].astype(F32)).astype(BF)
+        down_ref[...] = down.astype(BF)
+
+    @pl.when(pl.program_id(0) == 1)
+    def _():
+        up_ref[...] = up.astype(BF)
+        down_ref[...] = (down + far_down[...].astype(F32)).astype(BF)
+
+
+def ring_call(own, other, far_up, far_down):
+    _, features, width = own.shape
+    first = pl.BlockSpec((1, features, width), lambda f: (f, 0, 0))
+    second = pl.BlockSpec((1, features, width), lambda f: (NF + f, 0, 0))
+    whole = pl.BlockSpec((1, features, width), lambda f: (0, 0, 0))
+    out = jax.ShapeDtypeStruct((NF, features, width), BF)
+    return pl.pallas_call(
+        ring_body,
+        out_shape=(out, out),
+        grid=(NF,),
+        in_specs=[first, second, first, second, whole, whole],
+        out_specs=[first, first],
+        compiler_params=params(),
+        cost_estimate=cost(1, 8 * own.size, 8 * own.size),
+        name="ring",
+    )(own, own, other, other, far_up[None], far_down[None])
 
 
 KEPT = [(0, 0), (1, 0), (1, 1), (0, 3)]
@@ -240,7 +272,7 @@
     parts = len(d_gates)
     rows, both = d_gates[0].shape
     step = rows * parts // CHUNKS
-    tile = 256
+    tile = 512
     outs = pl.pallas_call(
         lambda *refs: input_body(parts, *refs),
         out_shape=[jax.ShapeDtypeStruct((step, depth), F32 if o in KEPT else BF) for o in ORDER],
@@ -266,64 +298,71 @@
 def on_device(inputs, grad_out, gate_pre, up_pre, w_gate, w_up, w_down):
     table = jnp.concatenate([jnp.asarray(ROWS)[lax.axis_index("tensor")], jnp.asarray(SLABS)[lax.axis_index("dp")]])
     step, width = grad_out.shape[0], w_down.shape[0]
-    half = CHUNKS // 2
+    part = step // 2
     together = lambda *values: lax.optimization_barrier(values)
 
     other, above, below = tsend(grad_out, Y_SWAP), tsend(grad_out, X_DOWN), tsend(grad_out, X_UP)
-    other, above, below, down_in, gate_in, inputs, up_pre = together(
-        other, above, below, tsend(w_down, CORE), tsend(gate_pre, CORE), inputs, up_pre
+    other, above, below, down_in, gate_in, up_pre = together(
+        other, above, below, tsend(w_down, CORE), tsend(gate_pre, CORE), up_pre
     )
     near = [grad_out, other, above, below]
-    above_y, below_y, far = tsend(other, X_DOWN), tsend(other, X_UP), tsend(above, X_DOWN)
-    below_in, up_in = tsend(inputs, X_UP), tsend(up_pre, CORE)
+    above_y, below_y = tsend(other, X_DOWN), tsend(other, X_UP)
+    far = [tsend(above[:part], X_DOWN), tsend(below[part:], X_UP)]
+    up_in = tsend(up_pre, CORE)
     downs, pre = (w_down, down_in), (gate_pre, gate_in, up_pre, up_in)
     firsts = slope_call(table, 0, near, downs, pre, 4)
     hidden = hidden_call(table, pre, step, 1)
 
-    above_y, below_y, far, below_in, inputs, w_gate, w_up, _, _ = together(
-        above_y, below_y, far, below_in, inputs, w_gate, w_up, firsts[0], hidden
-    )
-    far_y = tsend(below_y, X_UP)
-    above_in, other_in = tsend(inputs, X_DOWN), tsend(inputs, Y_SWAP)
-    far_y, above_in, other_in, below_in, w_gate_in, w_up_in = together(
-        far_y, above_in, other_in, below_in, tsend(w_gate, CORE), tsend(w_up, CORE)
-    )
-    last = [above_y, below_y, far, far_y]
+    above_y, below_y, far, inputs, w_gate, w_up, _, _ = together(
+        above_y, below_y, far, inputs, w_gate, w_up, firsts[0], hidden
+    )
+    far_y = [tsend(above_y[:part], X_DOWN), tsend(below_y[part:], X_UP)]
+    far_y, other_in, w_gate_in, w_up_in, inputs = together(
+        far_y, tsend(inputs, Y_SWAP), tsend(w_gate, CORE), tsend(w_up, CORE), inputs
+    )
+    last = [above_y, below_y, *far, *far_y]
+
+    above_in, below_in = tsend(inputs, X_DOWN), tsend(inputs, X_UP)
+    down_own, down_other = weight_call(table, 0, NZ, near + last, [(hidden,)], 12)
+    down_other = tsend(down_other, CORE)
+    above_in, below_in, other_in, _ = together(above_in, below_in, other_in, down_own)
     rows_in = [inputs, other_in, above_in, below_in]
     above_y, below_y = tsend(other_in, X_DOWN), tsend(other_in, X_UP)
-    down_own, down_other = weight_call(table, 0, NZ * NF, near + last, [(hidden,)], 12)
-    down_other = tsend(down_other, CORE)
-    above_y, below_y, below_in, _ = together(above_y, below_y, below_in, down_own)
-    seconds = slope_call(table, half, last, after(downs, above_y, below_y, down_own), pre, 12)
+    seconds = slope_call(table, CHUNKS // 2, last, after(downs, above_in, below_in, down_own), pre, 12)
+    above_y, below_y, below_in = together(above_y, below_y, below_in)
     far, far_y = tsend(below_in, X_UP), tsend(above_y, X_DOWN)
     rows_in += [above_y, below_y, far, far_y]
     d_gate, d_up = zip(firsts, seconds)
-    partial = input_call(*after((d_gate, d_up), down_other), (w_gate, w_gate_in, w_up, w_up_in), 12)
+    partial = input_call(*after((d_gate, d_up), down_other, above_y, below_y), (w_gate, w_gate_in, w_up, w_up_in), 12)
     far_down, one_down, three_down, rest_down = split(down_own + down_other)
     far_down = dsend(low(far_down), Z_FAR)
 
     d_gate, d_up = after((d_gate, d_up), partial[0, 0], far_down)
-    far_own, far_other = weight_call(table, 0, NF, rows_in, (d_gate, d_up), 0.1)
+    far_own, far_other = weight_call(table, 0, 1, rows_in, (d_gate, d_up), 0.1)
     far_other = tsend(far_other, CORE)
     one, three = tsend(after(partial[1, 2], far), X_UP), tsend(after(partial[1, 3], far_y), X_DOWN)
     one_down, three_down = after((low(one_down), low(three_down)), partial[0, 0])
     one_down, three_down = dsend(one_down, Z_UP), dsend(three_down, Z_DOWN)
-    d_gate, d_up, one, three, one_down, three_down, below = together(d_gate, d_up, one, three, one_down, three_down, partial[0, 2])
+    d_gate, d_up, one, three, one_down, three_down, below = together(
+        d_gate, d_up, one, three, one_down, three_down, partial[0, 2]
+    )
     d_gate, d_up = after((d_gate, d_up), far_own, far_other)
-    rest_own, rest_other = weight_call(table, NF, NZ * NF - NF, rows_in, (d_gate, d_up), 12)
+    ring_own, ring_other = weight_call(table, 1, 2, rows_in, (d_gate, d_up), 12)
     far_sum = low(far_own + far_other)
     far_up, far_dn = dsend(far_sum[0], Z_UP), dsend(far_sum[1], Z_DOWN)
     above, below = tsend(low(partial[1, 1] + one), X_UP), tsend(below, X_DOWN)
-    far_up, far_dn, rest_other, above, below, up = together(far_up, far_dn, rest_other, above, below, partial[0, 1])
-    rest_one, rest_three, rest = split(rest_own + tsend(rest_other, CORE))
-    rest_up = dsend(jnp.stack([low(rest_one[0] + far_up), low(rest_one[1])]), Z_UP)
-    rest_dn = dsend(jnp.stack([low(rest_three[0]), low(rest_three[1] + far_dn)]), Z_DOWN)
-    total = tsend(low(partial[1, 0] + above + three), Y_SWAP)
+    far_up, far_dn, ring_other, above, below, up = together(far_up, far_dn, ring_other, above, below, partial[0, 1])
+    d_gate, d_up = after((d_gate, d_up), ring_own)
+    rest_own, rest_other = weight_call(table, 3, 1, rows_in, (d_gate, d_up), 12)
+    ring_up, ring_dn = ring_call(ring_own, tsend(ring_other, CORE), *after((far_up, far_dn), rest_own))
+    rest_other = tsend(rest_other, CORE)
+    ring_up, ring_dn = dsend(ring_up, Z_UP), dsend(ring_dn, Z_DOWN)
+    total = tsend(low(after(partial[1, 0], rest_other) + above + three), Y_SWAP)
     below, up = tsend(low(partial[0, 3] + below), X_DOWN), tsend(up, X_UP)
-    rest_up, rest_dn, below, up = together(rest_up, rest_dn, below, up)
+    ring_up, ring_dn, below, up, rest_down = together(ring_up, ring_dn, below, up, rest_down)
+    rest_down = rest_down + one_down + three_down + far_down
+    rest = rest_own + rest_other + ring_up + ring_dn
     d_input = partial[0, 0] + below + up + total
-    rest = rest + rest_up + rest_dn
-    rest_down = rest_down + one_down + three_down + far_down
     down_part = (rest_down[0] + dsend(low(rest_down[1]), F_SWAP)).T
     both_part = rest[0] + dsend(low(rest[1]), F_SWAP)
     return (d_input, both_part[:, :width], both_part[:, width:], down_part)

time: 197 us -> 172 us (0.87)
  Pallas kernels: 62.8 us -> 34.7 us
  other arithmetic: 21.2 us -> 2.98 us
  waiting for transfers between devices: 48.5 us -> 65.2 us
  local copies, waits for them, and re-layouts: 9.04 us -> 13.4 us
    ppermute x9, waiting for transfers between devices: 6.53 us -> 20.1 us  [dsend(): return lax.ppermute(value, 'dp', pairs)]
    pallas_call x3 -> x5, Pallas kernels: 27.7 us -> 16.2 us  [the longest x4 15.6 us: weight_call(): pl.pallas_call(lambda *refs: weight_body(count, wide, *refs), out_shape=(...]
    another operation x5 -> x1, other arithmetic: 9.29 us -> 0.43 us
    pallas_call x2, Pallas kernels: 15.6 us -> 8.96 us  [slope_call(): pl.pallas_call(lambda *refs: slope_body(first, count, *refs), out_shape=(...]
    pallas_call x1, Pallas kernels: 7.01 us -> 1.76 us  [hidden_call(): pl.pallas_call(hidden_body, out_shape=jax.ShapeDtypeStruct((total, both),...]
    convert_element_type x4, other arithmetic: 5.72 us -> 0.61 us  [low(): return value.astype(BF)]
    pallas_call x1, Pallas kernels: 12.5 us -> 7.71 us  [input_call(): pl.pallas_call(lambda *refs: input_body(parts, *refs), out_shape=[jax.Sha...]
    unnamed x39 -> x27, local copies, waits for them, and re-layouts: 5.24 us -> 8.82 us
  transfers between devices with their start and end apart: 38 -> 41, of which waited for: 12 -> 17; matrix products, arithmetic and copies ran while one was open for 13% -> 4% of each run, Pallas kernels for 32% -> 20%
where the time goes in v2:
time: 172 us; the launch traced here: 171 us
  waiting for transfers between devices  65.2 us (38%)
  starting transfers between devices  54 us (31%)
  Pallas kernels  34.7 us (20%)
  local copies, waits for them, and re-layouts  13.4 us (8%)
  other arithmetic  2.98 us (2%)
    ppermute x32, waiting for transfers between devices, tsend(): return lax.ppermute(value, 'tensor', pairs)  45.1 us
    ppermute x32, starting transfers between devices, tsend(): return lax.ppermute(value, 'tensor', pairs)  37.1 us
    ppermute x9, waiting for transfers between devices, dsend(): return lax.ppermute(value, 'dp', pairs)  20.1 us
    ppermute x9, starting transfers between devices, dsend(): return lax.ppermute(value, 'dp', pairs)  16.9 us
    pallas_call x4, Pallas kernels, weight_call(): pl.pallas_call(lambda *refs: weight_body(count, wide, *refs), out_shape=(...  15.6 us
    pallas_call x2, Pallas kernels, slope_call(): pl.pallas_call(lambda *refs: slope_body(first, count, *refs), out_shape=(...  8.96 us
    unnamed x27, local copies, waits for them, and re-layouts  8.82 us
    pallas_call x1, Pallas kernels, input_call(): pl.pallas_call(lambda *refs: input_body(parts, *refs), out_shape=[jax.Sha...  7.71 us
  transfers between devices with their start and end apart: 41, of which 17 were waited for; matrix products, arithmetic and copies ran while one was open for 4% of the time, Pallas kernels for 20%

profile of v2, /device:TPU:0, one launch (start us, length us, event | category | flops | bytes accessed | tf_op | source)
XLA Modules:
  0.0 171.3 jit_solution(8693353446002027250)
XLA Ops:
  0.7 0.5 collective-permute-start.4
  1.2 1.6 collective-permute-start.2
  2.8 1.7 collective-permute-start.1
  4.5 1.7 collective-permute-start
  6.1 10.6 %collective-permute-done.2.refs_4_ = bf16[128,2048]{1,0:T(8,128)(2,1)} collective-permute-done((bf16[128,2048]{1,0:T(8,128)(2,1)}, bf16[128,2048]{1,0:T(8,128)(2,1)}, u32[]{:S(2)}, u32[]{:S(2)}) %collective-permute-start.2) | collective-permute-done | bytes 524320 | tf_op jit(solution)/shard_map/ppermute | solution.py:51
  16.8 1.4 collective-permute-done.refs_2_
  18.1 1.2 copy-done.9
  19.3 0.7 dynamic-slice_bitcast_fusion
  20.0 0.7 dynamic-slice_bitcast_fusion.1
  21.2 2.9 %collective-permute-start.6 = (bf16[128,2048]{1,0:T(8,128)(2,1)}, bf16[128,2048]{1,0:T(8,128)(2,1)S(1)}, u32[]{:S(2)}, u32[]{:S(2)}) collective-permute-start(bf16[128,2048]{1,0:T(8,128)(2,1)} %collective-permute-done.refs_2_), channel_id=1, source_target_pairs={{0,6},{1,7},{2,0},{3,1},{4,2},{5,3},{6,4},{7,5},{8,14},{9,15},{10,... | collective-permute-start | bytes 1572872 | tf_op jit(solution)/shard_map/ppermute | solution.py:51
  24.0 1.0 slice.45
  25.0 1.0 slice.46
  26.1 3.2 %collective-permute-start.8 = (bf16[64,2048]{1,0:T(8,128)(2,1)S(1)}, bf16[64,2048]{1,0:T(8,128)(2,1)S(1)}, u32[]{:S(2)}, u32[]{:S(2)}) collective-permute-start(bf16[64,2048]{1,0:T(8,128)(2,1)S(1)} %slice.45), channel_id=1, source_target_pairs={{0,6},{1,7},{2,0},{3,1},{4,2},{5,3},{6,4},{7,5},{8,14},{9,15},{10,... | collective-permute-start | bytes 786440 | tf_op jit(solution)/shard_map/ppermute | solution.py:51
  29.3 1.4 copy-done
  30.7 1.4 copy-done.2
  32.1 1.4 copy-done.5
  33.5 1.4 copy-done.10
  34.9 1.0 copy-done.12
  36.0 4.8 %slope.2 = (bf16[512,768]{1,0:T(8,128)(2,1)S(1)}, bf16[512,768]{1,0:T(8,128)(2,1)S(1)}) custom-call(s32[13]{0:T(128)S(1)} %pad_add_fusion.refs_0_.table_ref, bf16[128,2048]{1,0:T(8,128)(2,1)S(1)} %copy-done.12, bf16[128,2048]{1,0:T(8,128)(2,1)} %collective-permute-done.refs_2_, bf16[128,2048]{1,0:T(8,128)(2,1)} %collective-permute-done.1.refs_3_, ...), custom_call_target="tpu_custom_call" | custom-call | flops 6442450944 | bytes 33554432 | tf_op jit(solution)/shard_map/slope/pallas_call | solution.py:149
  40.8 1.8 %hidden.1.refs_11_ = bf16[1024,768]{1,0:T(8,128)(2,1)S(1)} custom-call(s32[13]{0:T(128)S(1)} %pad_add_fusion.refs_0_.table_ref, bf16[2048,384]{1,0:T(8,128)(2,1)S(1)} %copy-done.1, bf16[2048,384]{1,0:T(8,128)(2,1)S(1)} %collective-permute-done.4.refs_8_.refs_1_.refs_10_, bf16[2048,384]{1,0:T(8,128)(2,1)S(1)} %copy-done.2, ...), custom_call_target="tpu_custom_call" | custom-call | flops 12582912 | bytes 4718592 | tf_op jit(solution)/shard_map/hidden/pallas_call | solution.py:81
  42.7 0.5 collective-permute-start.14
  43.2 1.7 collective-permute-start.12
  45.1 3.2 %collective-permute-start.10 = (bf16[64,2048]{1,0:T(8,128)(2,1)S(1)}, bf16[64,2048]{1,0:T(8,128)(2,1)S(1)}, u32[]{:S(2)}, u32[]{:S(2)}) collective-permute-start(bf16[64,2048]{1,0:T(8,128)(2,1)S(1)} %slice.47), channel_id=1, source_target_pairs={{0,6},{1,7},{2,0},{3,1},{4,2},{5,3},{6,4},{7,5},{8,14},{9,15},{10,... | collective-permute-start | bytes 786440 | tf_op jit(solution)/shard_map/ppermute | solution.py:51
  48.3 6.0 %collective-permute-done.11.refs_10_.refs_6_ = bf16[64,2048]{1,0:T(8,128)(2,1)S(1)} collective-permute-done((bf16[64,2048]{1,0:T(8,128)(2,1)S(1)}, bf16[64,2048]{1,0:T(8,128)(2,1)S(1)}, u32[]{:S(2)}, u32[]{:S(2)}) %collective-permute-start.11) | collective-permute-done | bytes 262176 | tf_op jit(solution)/shard_map/ppermute | solution.py:51
  54.3 2.9 %collective-permute-done.12.refs_2_ = bf16[128,2048]{1,0:T(8,128)(2,1)S(1)} collective-permute-done((bf16[128,2048]{1,0:T(8,128)(2,1)S(1)}, bf16[128,2048]{1,0:T(8,128)(2,1)S(1)}, u32[]{:S(2)}, u32[]{:S(2)}) %collective-permute-start.12) | collective-permute-done | bytes 524320 | tf_op jit(solution)/shard_map/ppermute | solution.py:51
  57.2 3.2 %collective-permute-start.15 = (bf16[128,2048]{1,0:T(8,128)(2,1)S(1)}, bf16[128,2048]{1,0:T(8,128)(2,1)S(1)}, u32[]{:S(2)}, u32[]{:S(2)}) collective-permute-start(bf16[128,2048]{1,0:T(8,128)(2,1)S(1)} %copy-done.4), channel_id=1, source_target_pairs={{0,6},{1,7},{2,0},{3,1},{4,2},{5,3},{6,4},{7,5},{8,14},{9,15},{10,... | collective-permute-start | bytes 1572872 | tf_op jit(solution)/shard_map/ppermute | solution.py:51
  60.4 6.2 %weight.4 = (f32[8,256,384]{2,1,0:T(8,128)S(1)}, bf16[8,256,384]{2,1,0:T(8,128)(2,1)S(1)}) custom-call(s32[13]{0:T(128)S(1)} %pad_add_fusion.refs_0_.table_ref, bf16[128,2048]{1,0:T(8,128)(2,1)S(1)} %copy-done.12, bf16[128,2048]{1,0:T(8,128)(2,1)} %collective-permute-done.refs_2_, bf16[128,2048]{1,0:T(8,128)(2,1)} %collective-permute-done.1.refs_3_, ...), custom_call_target="tpu_custom_call" | custom-call | flops 38654705664 | bytes 125829120 | tf_op jit(solution)/shard_map/weight/pallas_call | solution.py:204
  66.8 4.7 %collective-permute-done.16.refs_4_ = bf16[128,2048]{1,0:T(8,128)(2,1)S(1)} collective-permute-done((bf16[128,2048]{1,0:T(8,128)(2,1)S(1)}, bf16[128,2048]{1,0:T(8,128)(2,1)S(1)}, u32[]{:S(2)}, u32[]{:S(2)}) %collective-permute-start.16) | collective-permute-done | bytes 524320 | tf_op jit(solution)/shard_map/ppermute | solution.py:51
  71.5 0.7 collective-permute-start.19
  72.2 2.5 %collective-permute-start.18 = (bf16[128,2048]{1,0:T(8,128)(2,1)S(1)}, bf16[128,2048]{1,0:T(8,128)(2,1)S(1)}, u32[]{:S(2)}, u32[]{:S(2)}) collective-permute-start(bf16[128,2048]{1,0:T(8,128)(2,1)S(1)} %collective-permute-done.12.refs_2_), channel_id=1, source_target_pairs={{0,6},{1,7},{2,0},{3,1},{4,2},{5,3},{6,4},{7,5},{8,14},{9,15},{10,... | collective-permute-start | bytes 1572872 | tf_op jit(solution)/shard_map/ppermute | solution.py:51
  74.7 4.2 %slope.3 = (bf16[512,768]{1,0:T(8,128)(2,1)S(1)}, bf16[512,768]{1,0:T(8,128)(2,1)S(1)}) custom-call(s32[13]{0:T(128)S(1)} %pad_add_fusion.refs_0_.table_ref, bf16[128,2048]{1,0:T(8,128)(2,1)S(1)} %collective-permute-done.6.refs_5_.refs_1_, bf16[128,2048]{1,0:T(8,128)(2,1)S(1)} %collective-permute-done.7.refs_6_.refs_2_, ...), custom_call_target="tpu_custom_call" | custom-call | flops 19327352832 | bytes 100663296 | tf_op jit(solution)/shard_map/slope/pallas_call | solution.py:149
  78.9 6.0 %collective-permute-done.19.refs_6_ = bf16[128,2048]{1,0:T(8,128)(2,1)S(1)} collective-permute-done((bf16[128,2048]{1,0:T(8,128)(2,1)S(1)}, bf16[128,2048]{1,0:T(8,128)(2,1)S(1)}, u32[]{:S(2)}, u32[]{:S(2)}) %collective-permute-start.19) | collective-permute-done | bytes 524320 | tf_op jit(solution)/shard_map/ppermute | solution.py:51
  84.9 0.9 collective-permute-start.20
  85.7 2.4 %collective-permute-start.21 = (bf16[128,2048]{1,0:T(8,128)(2,1)S(1)}, bf16[128,2048]{1,0:T(8,128)(2,1)S(1)}, u32[]{:S(2)}, u32[]{:S(2)}) collective-permute-start(bf16[128,2048]{1,0:T(8,128)(2,1)S(1)} %collective-permute-done.18.refs_5_), channel_id=1, source_target_pairs={{0,6},{1,7},{2,0},{3,1},{4,2},{5,3},{6,4},{7,5},{8,14},{9,15},{10,... | collective-permute-start | bytes 1572872 | tf_op jit(solution)/shard_map/ppermute | solution.py:51
  88.1 0.4 fusion.5
  88.7 4.0 %collective-permute-start.22 = (bf16[2,256,384]{2,1,0:T(8,128)(2,1)S(1)}, bf16[2,256,384]{2,1,0:T(8,128)(2,1)S(1)}, u32[]{:S(2)}, u32[]{:S(2)}) collective-permute-start(bf16[2,256,384]{2,1,0:T(8,128)(2,1)S(1)} %get-tuple-element.196), channel_id=1, source_target_pairs={{0,64},{16,80},{32,96},{48,112},{64,0},{80,16},{96,32},{112,48},{1... | collective-permute-start | bytes 1179656 | tf_op jit(solution)/shard_map/ppermute | solution.py:55
  92.7 7.7 %input.1 = (f32[128,2048]{1,0:T(8,128)S(1)}, f32[128,2048]{1,0:T(8,128)S(1)}, bf16[128,2048]{1,0:T(8,128)(2,1)S(1)}, f32[128,2048]{1,0:T(8,128)S(1)}, f32[128,20...) custom-call(bf16[512,768]{1,0:T(8,128)(2,1)S(1)} %get-tuple-element., ...), custom_call_target="tpu_custom_call" | custom-call | flops 77309411328 | bytes 176160768 | tf_op jit(solution)/shard_map/input/pallas_call | solution.py:276
  100.5 1.8 %collective-permute-start.24 = (bf16[128,2048]{1,0:T(8,128)(2,1)S(1)}, bf16[128,2048]{1,0:T(8,128)(2,1)S(1)}, u32[]{:S(2)}, u32[]{:S(2)}) collective-permute-start(bf16[128,2048]{1,0:T(8,128)(2,1)S(1)} %get-tuple-element.141), channel_id=1, source_target_pairs={{0,6},{1,7},{2,0},{3,1},{4,2},{5,3},{6,4},{7,5},{8,14},{9,15},{10,... | collective-permute-start | bytes 1572872 | tf_op jit(solution)/shard_map/ppermute | solution.py:51
  102.6 1.0 collective-permute-start.25
  103.6 2.2 %collective-permute-start.26 = (bf16[2,256,384]{2,1,0:T(8,128)(2,1)S(1)}, bf16[2,256,384]{2,1,0:T(8,128)(2,1)S(1)}, u32[]{:S(2)}, u32[]{:S(2)}) collective-permute-start(bf16[2,256,384]{2,1,0:T(8,128)(2,1)S(1)} %get-tuple-element.143), channel_id=1, source_target_pairs={{0,96},{16,112},{32,0},{48,16},{64,32},{80,48},{96,64},{112,80},{1... | collective-permute-start | bytes 1179656 | tf_op jit(solution)/shard_map/ppermute | solution.py:55
  105.8 2.4 %weight.5 = (f32[2,256,768]{2,1,0:T(8,128)S(1)}, bf16[2,256,768]{2,1,0:T(8,128)(2,1)S(1)}) custom-call(s32[13]{0:T(128)S(1)} %pad_add_fusion.refs_0_.table_ref, bf16[128,2048]{1,0:T(8,128)(2,1)S(1)} %copy-done.4, bf16[128,2048]{1,0:T(8,128)(2,1)S(1)} %collective-permute-done.12.refs_2_, bf16[128,2048]{1,0:T(8,128)(2,1)S(1)} %collective-permute-done.15.refs_3_, ...), custom_call_target="tpu_custom_call" | custom-call | flops 161061280 | bytes 1048576 | tf_op jit(solution)/shard_map/weight/pallas_call | solution.py:204
  108.3 3.3 %collective-permute-done.25 = bf16[2,256,384]{2,1,0:T(8,128)(2,1)S(1)} collective-permute-done((bf16[2,256,384]{2,1,0:T(8,128)(2,1)S(1)}, bf16[2,256,384]{2,1,0:T(8,128)(2,1)S(1)}, u32[]{:S(2)}, u32[]{:S(2)}) %collective-permute-start.25) | collective-permute-done | bytes 393248 | tf_op jit(solution)/shard_map/ppermute | solution.py:55
  111.5 2.3 %collective-permute-done.23 = bf16[128,2048]{1,0:T(8,128)(2,1)S(1)} collective-permute-done((bf16[128,2048]{1,0:T(8,128)(2,1)S(1)}, bf16[128,2048]{1,0:T(8,128)(2,1)S(1)}, u32[]{:S(2)}, u32[]{:S(2)}) %collective-permute-start.23) | collective-permute-done | bytes 524320 | tf_op jit(solution)/shard_map/ppermute | solution.py:51
  114.0 3.2 %collective-permute-start.31 = (bf16[128,2048]{1,0:T(8,128)(2,1)S(1)}, bf16[128,2048]{1,0:T(8,128)(2,1)S(1)}, u32[]{:S(2)}, u32[]{:S(2)}) collective-permute-start(bf16[128,2048]{1,0:T(8,128)(2,1)S(1)} %get-tuple-element.159), channel_id=1, source_target_pairs={{0,6},{1,7},{2,0},{3,1},{4,2},{5,3},{6,4},{7,5},{8,14},{9,15},{10,... | collective-permute-start | bytes 1572872 | tf_op jit(solution)/shard_map/ppermute | solution.py:51
  117.5 2.6 %collective-permute-start.29 = (bf16[256,768]{1,0:T(8,128)(2,1)S(1)}, bf16[256,768]{1,0:T(8,128)(2,1)S(1)}, u32[]{:S(2)}, u32[]{:S(2)}) collective-permute-start(bf16[256,768]{1,0:T(8,128)(2,1)S(1)} %get-tuple-element.199), channel_id=1, source_target_pairs={{0,96},{16,112},{32,0},{48,16},{64,32},{80,48},{96,64},{112,80},{1... | collective-permute-start | bytes 1179656 | tf_op jit(solution)/shard_map/ppermute | solution.py:55
  120.0 4.6 %weight.6 = (f32[4,256,768]{2,1,0:T(8,128)S(1)}, bf16[4,256,768]{2,1,0:T(8,128)(2,1)S(1)}) custom-call(s32[13]{0:T(128)S(1)} %pad_add_fusion.refs_0_.table_ref, bf16[128,2048]{1,0:T(8,128)(2,1)S(1)} %copy-done.4, bf16[128,2048]{1,0:T(8,128)(2,1)S(1)} %collective-permute-done.12.refs_2_, bf16[128,2048]{1,0:T(8,128)(2,1)S(1)} %collective-permute-done.15.refs_3_, ...), custom_call_target="tpu_custom_call" | custom-call | flops 38654705664 | bytes 125829120 | tf_op jit(solution)/shard_map/weight/pallas_call | solution.py:204
  124.7 0.7 collective-permute-done.29
  125.3 3.7 %collective-permute-done.28 = bf16[256,768]{1,0:T(8,128)(2,1)S(1)} collective-permute-done((bf16[256,768]{1,0:T(8,128)(2,1)S(1)}, bf16[256,768]{1,0:T(8,128)(2,1)S(1)}, u32[]{:S(2)}, u32[]{:S(2)}) %collective-permute-start.28) | collective-permute-done | bytes 393248 | tf_op jit(solution)/shard_map/ppermute | solution.py:55
  129.0 2.4 %weight.7 = (f32[2,256,768]{2,1,0:T(8,128)S(1)}, bf16[2,256,768]{2,1,0:T(8,128)(2,1)S(1)}) custom-call(s32[13]{0:T(128)S(1)} %pad_add_fusion.refs_0_.table_ref, bf16[128,2048]{1,0:T(8,128)(2,1)S(1)} %copy-done.4, bf16[128,2048]{1,0:T(8,128)(2,1)S(1)} %collective-permute-done.12.refs_2_, bf16[128,2048]{1,0:T(8,128)(2,1)S(1)} %collective-permute-done.15.refs_3_, ...), custom_call_target="tpu_custom_call" | custom-call | flops 19327352832 | bytes 125829120 | tf_op jit(solution)/shard_map/weight/pallas_call | solution.py:204
  131.4 0.6 collective-permute-start.37
  132.0 0.4 collective-permute-done.32.in_up.in_down
  132.4 0.7 ring.1
  133.2 3.2 %collective-permute-start.34 = (bf16[2,256,768]{2,1,0:T(8,128)(2,1)S(1)}, bf16[2,256,768]{2,1,0:T(8,128)(2,1)S(1)}, u32[]{:S(2)}, u32[]{:S(2)}) collective-permute-start(bf16[2,256,768]{2,1,0:T(8,128)(2,1)S(1)} %get-tuple-element.172), channel_id=1, source_target_pairs={{0,96},{16,112},{32,0},{48,16},{64,32},{80,48},{96,64},{112,80},{1... | collective-permute-start | bytes 2359304 | tf_op jit(solution)/shard_map/ppermute | solution.py:55
  136.8 1.8 %collective-permute-start.36 = (bf16[128,2048]{1,0:T(8,128)(2,1)S(1)}, bf16[128,2048]{1,0:T(8,128)(2,1)S(1)}, u32[]{:S(2)}, u32[]{:S(2)}) collective-permute-start(bf16[128,2048]{1,0:T(8,128)(2,1)S(1)} %get-tuple-element.175), channel_id=1, source_target_pairs={{0,2},{1,3},{2,4},{3,5},{4,6},{5,7},{6,0},{7,1},{8,10},{9,11},{10,... | collective-permute-start | bytes 1572872 | tf_op jit(solution)/shard_map/ppermute | solution.py:51
  138.9 1.7 collective-permute-start.38
  140.6 9.4 %collective-permute-done.35 = bf16[128,2048]{1,0:T(8,128)(2,1)S(1)} collective-permute-done((bf16[128,2048]{1,0:T(8,128)(2,1)S(1)}, bf16[128,2048]{1,0:T(8,128)(2,1)S(1)}, u32[]{:S(2)}, u32[]{:S(2)}) %collective-permute-start.35) | collective-permute-done | bytes 524320 | tf_op jit(solution)/shard_map/ppermute | solution.py:51
  150.0 1.3 collective-permute-done.36
  151.3 2.7 %collective-permute-done.33 = bf16[2,256,768]{2,1,0:T(8,128)(2,1)S(1)} collective-permute-done((bf16[2,256,768]{2,1,0:T(8,128)(2,1)S(1)}, bf16[2,256,768]{2,1,0:T(8,128)(2,1)S(1)}, u32[]{:S(2)}, u32[]{:S(2)}) %collective-permute-start.33) | collective-permute-done | bytes 786464 | tf_op jit(solution)/shard_map/ppermute | solution.py:55
  154.2 3.3 %collective-permute-start.40 = (bf16[256,384]{1,0:T(8,128)(2,1)S(1)}, bf16[256,384]{1,0:T(8,128)(2,1)S(1)}, u32[]{:S(2)}, u32[]{:S(2)}) collective-permute-start(bf16[256,384]{1,0:T(8,128)(2,1)S(1)} %fusion.4), channel_id=1, source_target_pairs={{0,16},{16,0},{32,48},{48,32},{64,80},{80,64},{96,112},{112,96},{1... | collective-permute-start | bytes 589832 | tf_op jit(solution)/shard_map/ppermute | solution.py:55
  158.2 1.3 convert_add_fusion.2
  159.5 3.3 %collective-permute-done.40 = bf16[256,384]{1,0:T(8,128)(2,1)S(1)} collective-permute-done((bf16[256,384]{1,0:T(8,128)(2,1)S(1)}, bf16[256,384]{1,0:T(8,128)(2,1)S(1)}, u32[]{:S(2)}, u32[]{:S(2)}) %collective-permute-start.40) | collective-permute-done | bytes 196640 | tf_op jit(solution)/shard_map/ppermute | solution.py:55
  162.9 0.9 copy.13
  163.8 6.5 %collective-permute-done.39 = bf16[256,768]{1,0:T(8,128)(2,1)S(1)} collective-permute-done((bf16[256,768]{1,0:T(8,128)(2,1)S(1)}, bf16[256,768]{1,0:T(8,128)(2,1)S(1)}, u32[]{:S(2)}, u32[]{:S(2)}) %collective-permute-start.39) | collective-permute-done | bytes 393248 | tf_op jit(solution)/shard_map/ppermute | solution.py:55
  170.4 0.9 fusion.7
  (77 shorter events, 3.8 us)
Async XLA Ops:
  0.6 17.5 %collective-permute-start.3 = (bf16[384,2048]{1,0:T(8,128)(2,1)}, bf16[384,2048]{1,0:T(8,128)(2,1)S(1)}, u32[]{:S(2)}, u32[]{:S(2)}) collective-permute-start(bf16[384,2048]{1,0:T(8,128)(2,1)} %refs_7_.2), channel_id=1, source_target_pairs={{0,1},{1,0},{2,3},{3,2},{4,5},{5,4},{6,7},{7,6},{8,9},{9,8},{10,11... | collective-permute-start | bytes 4718600 | tf_op jit(solution)/shard_map/ppermute | solution.py:51
  0.7 18.6 %collective-permute-start.4 = (bf16[2048,384]{1,0:T(8,128)(2,1)}, bf16[2048,384]{1,0:T(8,128)(2,1)S(1)}, u32[]{:S(2)}, u32[]{:S(2)}) collective-permute-start(bf16[2048,384]{1,0:T(8,128)(2,1)} %refs_9_.2), channel_id=1, source_target_pairs={{0,1},{1,0},{2,3},{3,2},{4,5},{5,4},{6,7},{7,6},{8,9},{9,8},{10,11... | collective-permute-start | bytes 4718600 | tf_op jit(solution)/shard_map/ppermute | solution.py:51
  1.2 15.4 %collective-permute-start.2 = (bf16[128,2048]{1,0:T(8,128)(2,1)}, bf16[128,2048]{1,0:T(8,128)(2,1)}, u32[]{:S(2)}, u32[]{:S(2)}) collective-permute-start(bf16[128,2048]{1,0:T(8,128)(2,1)} %refs_1_.3), channel_id=1, source_target_pairs={{0,2},{1,3},{2,4},{3,5},{4,6},{5,7},{6,0},{7,1},{8,10},{9,11},{10,... | collective-permute-start | bytes 1572872 | tf_op jit(solution)/shard_map/ppermute | solution.py:51
  2.8 14.0 %collective-permute-start.1 = (bf16[128,2048]{1,0:T(8,128)(2,1)}, bf16[128,2048]{1,0:T(8,128)(2,1)}, u32[]{:S(2)}, u32[]{:S(2)}) collective-permute-start(bf16[128,2048]{1,0:T(8,128)(2,1)} %refs_1_.3), channel_id=1, source_target_pairs={{0,6},{1,7},{2,0},{3,1},{4,2},{5,3},{6,4},{7,5},{8,14},{9,15},{10,... | collective-permute-start | bytes 1572872 | tf_op jit(solution)/shard_map/ppermute | solution.py:51
  4.5 13.7 %collective-permute-start = (bf16[128,2048]{1,0:T(8,128)(2,1)}, bf16[128,2048]{1,0:T(8,128)(2,1)}, u32[]{:S(2)}, u32[]{:S(2)}) collective-permute-start(bf16[128,2048]{1,0:T(8,128)(2,1)} %refs_1_.3), channel_id=1, source_target_pairs={{0,8},{1,9},{2,10},{3,11},{4,12},{5,13},{6,14},{7,15},{8,0},{9,1},... | collective-permute-start | bytes 1572872 | tf_op jit(solution)/shard_map/ppermute | solution.py:51
  18.1 1.2 copy-start.9
  19.3 10.0 %collective-permute-start.5 = (bf16[2048,384]{1,0:T(8,128)(2,1)}, bf16[2048,384]{1,0:T(8,128)(2,1)S(1)}, u32[]{:S(2)}, u32[]{:S(2)}) collective-permute-start(bf16[2048,384]{1,0:T(8,128)(2,1)} %refs_11_), channel_id=1, source_target_pairs={{0,1},{1,0},{2,3},{3,2},{4,5},{5,4},{6,7},{7,6},{8,9},{9,8},{10,11... | collective-permute-start | bytes 4718600 | tf_op jit(solution)/shard_map/ppermute | solution.py:51
  20.8 21.8 %collective-permute-start.7 = (bf16[128,2048]{1,0:T(8,128)(2,1)}, bf16[128,2048]{1,0:T(8,128)(2,1)S(1)}, u32[]{:S(2)}, u32[]{:S(2)}) collective-permute-start(bf16[128,2048]{1,0:T(8,128)(2,1)} %collective-permute-done.refs_2_), channel_id=1, source_target_pairs={{0,2},{1,3},{2,4},{3,5},{4,6},{5,7},{6,0},{7,1},{8,10},{9,11},{10,... | collective-permute-start | bytes 1572872 | tf_op jit(solution)/shard_map/ppermute | solution.py:51
  21.2 21.5 %collective-permute-start.6 = (bf16[128,2048]{1,0:T(8,128)(2,1)}, bf16[128,2048]{1,0:T(8,128)(2,1)S(1)}, u32[]{:S(2)}, u32[]{:S(2)}) collective-permute-start(bf16[128,2048]{1,0:T(8,128)(2,1)} %collective-permute-done.refs_2_), channel_id=1, source_target_pairs={{0,6},{1,7},{2,0},{3,1},{4,2},{5,3},{6,4},{7,5},{8,14},{9,15},{10,... | collective-permute-start | bytes 1572872 | tf_op jit(solution)/shard_map/ppermute | solution.py:51
  26.0 16.6 %collective-permute-start.9 = (bf16[64,2048]{1,0:T(8,128)(2,1)S(1)}, bf16[64,2048]{1,0:T(8,128)(2,1)S(1)}, u32[]{:S(2)}, u32[]{:S(2)}) collective-permute-start(bf16[64,2048]{1,0:T(8,128)(2,1)S(1)} %slice.46), channel_id=1, source_target_pairs={{0,2},{1,3},{2,4},{3,5},{4,6},{5,7},{6,0},{7,1},{8,10},{9,11},{10,... | collective-permute-start | bytes 786440 | tf_op jit(solution)/shard_map/ppermute | solution.py:51
  26.1 16.5 %collective-permute-start.8 = (bf16[64,2048]{1,0:T(8,128)(2,1)S(1)}, bf16[64,2048]{1,0:T(8,128)(2,1)S(1)}, u32[]{:S(2)}, u32[]{:S(2)}) collective-permute-start(bf16[64,2048]{1,0:T(8,128)(2,1)S(1)} %slice.45), channel_id=1, source_target_pairs={{0,6},{1,7},{2,0},{3,1},{4,2},{5,3},{6,4},{7,5},{8,14},{9,15},{10,... | collective-permute-start | bytes 786440 | tf_op jit(solution)/shard_map/ppermute | solution.py:51
  29.3 1.4 copy-start
  30.7 1.4 copy-start.2
  32.1 1.4 copy-start.5
  33.5 1.4 copy-start.10
  34.9 1.0 copy-start.12
  36.0 4.8 %copy-start.1 = (bf16[2048,384]{1,0:T(8,128)(2,1)S(1)}, bf16[2048,384]{1,0:T(8,128)(2,1)}, u32[]{:S(2)}) copy-start(bf16[2048,384]{1,0:T(8,128)(2,1)} %refs_9_.2) | copy-start | bytes 4718596
  40.8 1.9 %copy-start.7 = (bf16[2048,384]{1,0:T(8,128)(2,1)S(1)}, bf16[2048,384]{1,0:T(8,128)(2,1)}, u32[]{:S(2)}) copy-start(bf16[2048,384]{1,0:T(8,128)(2,1)} %refs_4_) | copy-start | bytes 4718596
  40.8 1.9 %copy-start.8 = (bf16[2048,384]{1,0:T(8,128)(2,1)S(1)}, bf16[2048,384]{1,0:T(8,128)(2,1)}, u32[]{:S(2)}) copy-start(bf16[2048,384]{1,0:T(8,128)(2,1)} %refs_6_) | copy-start | bytes 4718596
  40.8 2.4 %copy-start.4 = (bf16[128,2048]{1,0:T(8,128)(2,1)S(1)}, bf16[128,2048]{1,0:T(8,128)(2,1)}, u32[]{:S(2)}) copy-start(bf16[128,2048]{1,0:T(8,128)(2,1)} %refs_1_.6) | copy-start | bytes 1572868
  42.6 14.5 %collective-permute-start.13 = (bf16[2048,384]{1,0:T(8,128)(2,1)S(1)}, bf16[2048,384]{1,0:T(8,128)(2,1)S(1)}, u32[]{:S(2)}, u32[]{:S(2)}) collective-permute-start(bf16[2048,384]{1,0:T(8,128)(2,1)S(1)} %copy-done.7), channel_id=1, source_target_pairs={{0,1},{1,0},{2,3},{3,2},{4,5},{5,4},{6,7},{7,6},{8,9},{9,8},{10,11... | collective-permute-start | bytes 4718600 | tf_op jit(solution)/shard_map/ppermute | solution.py:51
  42.7 14.4 %collective-permute-start.14 = (bf16[2048,384]{1,0:T(8,128)(2,1)S(1)}, bf16[2048,384]{1,0:T(8,128)(2,1)S(1)}, u32[]{:S(2)}, u32[]{:S(2)}) collective-permute-start(bf16[2048,384]{1,0:T(8,128)(2,1)S(1)} %copy-done.8), channel_id=1, source_target_pairs={{0,1},{1,0},{2,3},{3,2},{4,5},{5,4},{6,7},{7,6},{8,9},{9,8},{10,11... | collective-permute-start | bytes 4718600 | tf_op jit(solution)/shard_map/ppermute | solution.py:51
  43.2 13.9 %collective-permute-start.12 = (bf16[128,2048]{1,0:T(8,128)(2,1)S(1)}, bf16[128,2048]{1,0:T(8,128)(2,1)S(1)}, u32[]{:S(2)}, u32[]{:S(2)}) collective-permute-start(bf16[128,2048]{1,0:T(8,128)(2,1)S(1)} %copy-done.4), channel_id=1, source_target_pairs={{0,8},{1,9},{2,10},{3,11},{4,12},{5,13},{6,14},{7,15},{8,0},{9,1},... | collective-permute-start | bytes 1572872 | tf_op jit(solution)/shard_map/ppermute | solution.py:51
  44.9 29.8 %copy-start.3 = (bf16[2048,384]{1,0:T(8,128)(2,1)S(1)}, bf16[2048,384]{1,0:T(8,128)(2,1)}, u32[]{:S(2)}) copy-start(bf16[2048,384]{1,0:T(8,128)(2,1)} %refs_11_) | copy-start | bytes 4718596
  45.0 29.8 %copy-start.6 = (bf16[384,2048]{1,0:T(8,128)(2,1)S(1)}, bf16[384,2048]{1,0:T(8,128)(2,1)}, u32[]{:S(2)}) copy-start(bf16[384,2048]{1,0:T(8,128)(2,1)} %refs_7_.2) | copy-start | bytes 4718596
  45.0 29.8 %copy-start.11 = (bf16[384,2048]{1,0:T(8,128)(2,1)S(1)}, bf16[384,2048]{1,0:T(8,128)(2,1)}, u32[]{:S(2)}) copy-start(bf16[384,2048]{1,0:T(8,128)(2,1)} %copy-done.9) | copy-start | bytes 4718596
  45.0 9.3 %collective-permute-start.11 = (bf16[64,2048]{1,0:T(8,128)(2,1)S(1)}, bf16[64,2048]{1,0:T(8,128)(2,1)S(1)}, u32[]{:S(2)}, u32[]{:S(2)}) collective-permute-start(bf16[64,2048]{1,0:T(8,128)(2,1)S(1)} %slice.48), channel_id=1, source_target_pairs={{0,2},{1,3},{2,4},{3,5},{4,6},{5,7},{6,0},{7,1},{8,10},{9,11},{10,... | collective-permute-start | bytes 786440 | tf_op jit(solution)/shard_map/ppermute | solution.py:51
  45.1 9.2 %collective-permute-start.10 = (bf16[64,2048]{1,0:T(8,128)(2,1)S(1)}, bf16[64,2048]{1,0:T(8,128)(2,1)S(1)}, u32[]{:S(2)}, u32[]{:S(2)}) collective-permute-start(bf16[64,2048]{1,0:T(8,128)(2,1)S(1)} %slice.47), channel_id=1, source_target_pairs={{0,6},{1,7},{2,0},{3,1},{4,2},{5,3},{6,4},{7,5},{8,14},{9,15},{10,... | collective-permute-start | bytes 786440 | tf_op jit(solution)/shard_map/ppermute | solution.py:51
  57.2 14.3 %collective-permute-start.16 = (bf16[128,2048]{1,0:T(8,128)(2,1)S(1)}, bf16[128,2048]{1,0:T(8,128)(2,1)S(1)}, u32[]{:S(2)}, u32[]{:S(2)}) collective-permute-start(bf16[128,2048]{1,0:T(8,128)(2,1)S(1)} %copy-done.4), channel_id=1, source_target_pairs={{0,2},{1,3},{2,4},{3,5},{4,6},{5,7},{6,0},{7,1},{8,10},{9,11},{10,... | collective-permute-start | bytes 1572872 | tf_op jit(solution)/shard_map/ppermute | solution.py:51
  57.2 14.3 %collective-permute-start.15 = (bf16[128,2048]{1,0:T(8,128)(2,1)S(1)}, bf16[128,2048]{1,0:T(8,128)(2,1)S(1)}, u32[]{:S(2)}, u32[]{:S(2)}) collective-permute-start(bf16[128,2048]{1,0:T(8,128)(2,1)S(1)} %copy-done.4), channel_id=1, source_target_pairs={{0,6},{1,7},{2,0},{3,1},{4,2},{5,3},{6,4},{7,5},{8,14},{9,15},{10,... | collective-permute-start | bytes 1572872 | tf_op jit(solution)/shard_map/ppermute | solution.py:51
  66.7 21.4 %collective-permute-start.17 = (bf16[8,256,384]{2,1,0:T(8,128)(2,1)S(1)}, bf16[8,256,384]{2,1,0:T(8,128)(2,1)S(1)}, u32[]{:S(2)}, u32[]{:S(2)}) collective-permute-start(bf16[8,256,384]{2,1,0:T(8,128)(2,1)S(1)} %get-tuple-element.122), channel_id=1, source_target_pairs={{0,1},{1,0},{2,3},{3,2},{4,5},{5,4},{6,7},{7,6},{8,9},{9,8},{10,11... | collective-permute-start | bytes 4718600 | tf_op jit(solution)/shard_map/ppermute | solution.py:51
  71.5 13.4 %collective-permute-start.19 = (bf16[128,2048]{1,0:T(8,128)(2,1)S(1)}, bf16[128,2048]{1,0:T(8,128)(2,1)S(1)}, u32[]{:S(2)}, u32[]{:S(2)}) collective-permute-start(bf16[128,2048]{1,0:T(8,128)(2,1)S(1)} %collective-permute-done.12.refs_2_), channel_id=1, source_target_pairs={{0,2},{1,3},{2,4},{3,5},{4,6},{5,7},{6,0},{7,1},{8,10},{9,11},{10,... | collective-permute-start | bytes 1572872 | tf_op jit(solution)/shard_map/ppermute | solution.py:51
  72.2 12.7 %collective-permute-start.18 = (bf16[128,2048]{1,0:T(8,128)(2,1)S(1)}, bf16[128,2048]{1,0:T(8,128)(2,1)S(1)}, u32[]{:S(2)}, u32[]{:S(2)}) collective-permute-start(bf16[128,2048]{1,0:T(8,128)(2,1)S(1)} %collective-permute-done.12.refs_2_), channel_id=1, source_target_pairs={{0,6},{1,7},{2,0},{3,1},{4,2},{5,3},{6,4},{7,5},{8,14},{9,15},{10,... | collective-permute-start | bytes 1572872 | tf_op jit(solution)/shard_map/ppermute | solution.py:51
  84.9 15.6 %collective-permute-start.20 = (bf16[128,2048]{1,0:T(8,128)(2,1)S(1)}, bf16[128,2048]{1,0:T(8,128)(2,1)S(1)}, u32[]{:S(2)}, u32[]{:S(2)}) collective-permute-start(bf16[128,2048]{1,0:T(8,128)(2,1)S(1)} %collective-permute-done.16.refs_4_), channel_id=1, source_target_pairs={{0,2},{1,3},{2,4},{3,5},{4,6},{5,7},{6,0},{7,1},{8,10},{9,11},{10,... | collective-permute-start | bytes 1572872 | tf_op jit(solution)/shard_map/ppermute | solution.py:51
  85.7 14.7 %collective-permute-start.21 = (bf16[128,2048]{1,0:T(8,128)(2,1)S(1)}, bf16[128,2048]{1,0:T(8,128)(2,1)S(1)}, u32[]{:S(2)}, u32[]{:S(2)}) collective-permute-start(bf16[128,2048]{1,0:T(8,128)(2,1)S(1)} %collective-permute-done.18.refs_5_), channel_id=1, source_target_pairs={{0,6},{1,7},{2,0},{3,1},{4,2},{5,3},{6,4},{7,5},{8,14},{9,15},{10,... | collective-permute-start | bytes 1572872 | tf_op jit(solution)/shard_map/ppermute | solution.py:51
  88.7 17.1 %collective-permute-start.22 = (bf16[2,256,384]{2,1,0:T(8,128)(2,1)S(1)}, bf16[2,256,384]{2,1,0:T(8,128)(2,1)S(1)}, u32[]{:S(2)}, u32[]{:S(2)}) collective-permute-start(bf16[2,256,384]{2,1,0:T(8,128)(2,1)S(1)} %get-tuple-element.196), channel_id=1, source_target_pairs={{0,64},{16,80},{32,96},{48,112},{64,0},{80,16},{96,32},{112,48},{1... | collective-permute-start | bytes 1179656 | tf_op jit(solution)/shard_map/ppermute | solution.py:55
  100.5 11.1 %collective-permute-start.24 = (bf16[128,2048]{1,0:T(8,128)(2,1)S(1)}, bf16[128,2048]{1,0:T(8,128)(2,1)S(1)}, u32[]{:S(2)}, u32[]{:S(2)}) collective-permute-start(bf16[128,2048]{1,0:T(8,128)(2,1)S(1)} %get-tuple-element.141), channel_id=1, source_target_pairs={{0,6},{1,7},{2,0},{3,1},{4,2},{5,3},{6,4},{7,5},{8,14},{9,15},{10,... | collective-permute-start | bytes 1572872 | tf_op jit(solution)/shard_map/ppermute | solution.py:51
  102.3 11.5 %collective-permute-start.23 = (bf16[128,2048]{1,0:T(8,128)(2,1)S(1)}, bf16[128,2048]{1,0:T(8,128)(2,1)S(1)}, u32[]{:S(2)}, u32[]{:S(2)}) collective-permute-start(bf16[128,2048]{1,0:T(8,128)(2,1)S(1)} %get-tuple-element.139), channel_id=1, source_target_pairs={{0,2},{1,3},{2,4},{3,5},{4,6},{5,7},{6,0},{7,1},{8,10},{9,11},{10,... | collective-permute-start | bytes 1572872 | tf_op jit(solution)/shard_map/ppermute | solution.py:51
  102.6 9.0 %collective-permute-start.25 = (bf16[2,256,384]{2,1,0:T(8,128)(2,1)S(1)}, bf16[2,256,384]{2,1,0:T(8,128)(2,1)S(1)}, u32[]{:S(2)}, u32[]{:S(2)}) collective-permute-start(bf16[2,256,384]{2,1,0:T(8,128)(2,1)S(1)} %get-tuple-element.142), channel_id=1, source_target_pairs={{0,32},{16,48},{32,64},{48,80},{64,96},{80,112},{96,0},{112,16},{1... | collective-permute-start | bytes 1179656 | tf_op jit(solution)/shard_map/ppermute | solution.py:55
  103.6 8.0 %collective-permute-start.26 = (bf16[2,256,384]{2,1,0:T(8,128)(2,1)S(1)}, bf16[2,256,384]{2,1,0:T(8,128)(2,1)S(1)}, u32[]{:S(2)}, u32[]{:S(2)}) collective-permute-start(bf16[2,256,384]{2,1,0:T(8,128)(2,1)S(1)} %get-tuple-element.143), channel_id=1, source_target_pairs={{0,96},{16,112},{32,0},{48,16},{64,32},{80,48},{96,64},{112,80},{1... | collective-permute-start | bytes 1179656 | tf_op jit(solution)/shard_map/ppermute | solution.py:55
  108.2 9.0 %collective-permute-start.27 = (bf16[2,256,768]{2,1,0:T(8,128)(2,1)S(1)}, bf16[2,256,768]{2,1,0:T(8,128)(2,1)S(1)}, u32[]{:S(2)}, u32[]{:S(2)}) collective-permute-start(bf16[2,256,768]{2,1,0:T(8,128)(2,1)S(1)} %get-tuple-element.150), channel_id=1, source_target_pairs={{0,1},{1,0},{2,3},{3,2},{4,5},{5,4},{6,7},{7,6},{8,9},{9,8},{10,11... | collective-permute-start | bytes 2359304 | tf_op jit(solution)/shard_map/ppermute | solution.py:51
  113.9 10.7 %collective-permute-start.30 = (bf16[128,2048]{1,0:T(8,128)(2,1)S(1)}, bf16[128,2048]{1,0:T(8,128)(2,1)S(1)}, u32[]{:S(2)}, u32[]{:S(2)}) collective-permute-start(bf16[128,2048]{1,0:T(8,128)(2,1)S(1)} %add_convert_fusion.3), channel_id=1, source_target_pairs={{0,2},{1,3},{2,4},{3,5},{4,6},{5,7},{6,0},{7,1},{8,10},{9,11},{10,... | collective-permute-start | bytes 1572872 | tf_op jit(solution)/shard_map/ppermute | solution.py:51
  114.0 10.7 %collective-permute-start.31 = (bf16[128,2048]{1,0:T(8,128)(2,1)S(1)}, bf16[128,2048]{1,0:T(8,128)(2,1)S(1)}, u32[]{:S(2)}, u32[]{:S(2)}) collective-permute-start(bf16[128,2048]{1,0:T(8,128)(2,1)S(1)} %get-tuple-element.159), channel_id=1, source_target_pairs={{0,6},{1,7},{2,0},{3,1},{4,2},{5,3},{6,4},{7,5},{8,14},{9,15},{10,... | collective-permute-start | bytes 1572872 | tf_op jit(solution)/shard_map/ppermute | solution.py:51
  117.5 7.9 %collective-permute-start.29 = (bf16[256,768]{1,0:T(8,128)(2,1)S(1)}, bf16[256,768]{1,0:T(8,128)(2,1)S(1)}, u32[]{:S(2)}, u32[]{:S(2)}) collective-permute-start(bf16[256,768]{1,0:T(8,128)(2,1)S(1)} %get-tuple-element.199), channel_id=1, source_target_pairs={{0,96},{16,112},{32,0},{48,16},{64,32},{80,48},{96,64},{112,80},{1... | collective-permute-start | bytes 1179656 | tf_op jit(solution)/shard_map/ppermute | solution.py:55
  120.0 9.0 %collective-permute-start.28 = (bf16[256,768]{1,0:T(8,128)(2,1)S(1)}, bf16[256,768]{1,0:T(8,128)(2,1)S(1)}, u32[]{:S(2)}, u32[]{:S(2)}) collective-permute-start(bf16[256,768]{1,0:T(8,128)(2,1)S(1)} %get-tuple-element.200), channel_id=1, source_target_pairs={{0,32},{16,48},{32,64},{48,80},{64,96},{80,112},{96,0},{112,16},{1... | collective-permute-start | bytes 1179656 | tf_op jit(solution)/shard_map/ppermute | solution.py:55
  129.0 3.4 %collective-permute-start.32 = (bf16[4,256,768]{2,1,0:T(8,128)(2,1)S(1)}, bf16[4,256,768]{2,1,0:T(8,128)(2,1)S(1)}, u32[]{:S(2)}, u32[]{:S(2)}) collective-permute-start(bf16[4,256,768]{2,1,0:T(8,128)(2,1)S(1)} %get-tuple-element.161), channel_id=1, source_target_pairs={{0,1},{1,0},{2,3},{3,2},{4,5},{5,4},{6,7},{7,6},{8,9},{9,8},{10,11... | collective-permute-start | bytes 4718600 | tf_op jit(solution)/shard_map/ppermute | solution.py:51
  131.4 7.3 %collective-permute-start.37 = (bf16[2,256,768]{2,1,0:T(8,128)(2,1)S(1)}, bf16[2,256,768]{2,1,0:T(8,128)(2,1)S(1)}, u32[]{:S(2)}, u32[]{:S(2)}) collective-permute-start(bf16[2,256,768]{2,1,0:T(8,128)(2,1)S(1)} %get-tuple-element.179), channel_id=1, source_target_pairs={{0,1},{1,0},{2,3},{3,2},{4,5},{5,4},{6,7},{7,6},{8,9},{9,8},{10,11... | collective-permute-start | bytes 2359304 | tf_op jit(solution)/shard_map/ppermute | solution.py:51
  133.1 20.9 %collective-permute-start.33 = (bf16[2,256,768]{2,1,0:T(8,128)(2,1)S(1)}, bf16[2,256,768]{2,1,0:T(8,128)(2,1)S(1)}, u32[]{:S(2)}, u32[]{:S(2)}) collective-permute-start(bf16[2,256,768]{2,1,0:T(8,128)(2,1)S(1)} %get-tuple-element.171), channel_id=1, source_target_pairs={{0,32},{16,48},{32,64},{48,80},{64,96},{80,112},{96,0},{112,16},{1... | collective-permute-start | bytes 2359304 | tf_op jit(solution)/shard_map/ppermute | solution.py:55
  133.2 20.8 %collective-permute-start.34 = (bf16[2,256,768]{2,1,0:T(8,128)(2,1)S(1)}, bf16[2,256,768]{2,1,0:T(8,128)(2,1)S(1)}, u32[]{:S(2)}, u32[]{:S(2)}) collective-permute-start(bf16[2,256,768]{2,1,0:T(8,128)(2,1)S(1)} %get-tuple-element.172), channel_id=1, source_target_pairs={{0,96},{16,112},{32,0},{48,16},{64,32},{80,48},{96,64},{112,80},{1... | collective-permute-start | bytes 2359304 | tf_op jit(solution)/shard_map/ppermute | solution.py:55
  136.5 13.5 %collective-permute-start.35 = (bf16[128,2048]{1,0:T(8,128)(2,1)S(1)}, bf16[128,2048]{1,0:T(8,128)(2,1)S(1)}, u32[]{:S(2)}, u32[]{:S(2)}) collective-permute-start(bf16[128,2048]{1,0:T(8,128)(2,1)S(1)} %add_convert_fusion.2), channel_id=1, source_target_pairs={{0,6},{1,7},{2,0},{3,1},{4,2},{5,3},{6,4},{7,5},{8,14},{9,15},{10,... | collective-permute-start | bytes 1572872 | tf_op jit(solution)/shard_map/ppermute | solution.py:51
  136.8 14.5 %collective-permute-start.36 = (bf16[128,2048]{1,0:T(8,128)(2,1)S(1)}, bf16[128,2048]{1,0:T(8,128)(2,1)S(1)}, u32[]{:S(2)}, u32[]{:S(2)}) collective-permute-start(bf16[128,2048]{1,0:T(8,128)(2,1)S(1)} %get-tuple-element.175), channel_id=1, source_target_pairs={{0,2},{1,3},{2,4},{3,5},{4,6},{5,7},{6,0},{7,1},{8,10},{9,11},{10,... | collective-permute-start | bytes 1572872 | tf_op jit(solution)/shard_map/ppermute | solution.py:51
  138.9 19.3 %collective-permute-start.38 = (bf16[128,2048]{1,0:T(8,128)(2,1)S(1)}, bf16[128,2048]{1,0:T(8,128)(2,1)S(1)}, u32[]{:S(2)}, u32[]{:S(2)}) collective-permute-start(bf16[128,2048]{1,0:T(8,128)(2,1)S(1)} %add_convert_fusion.1), channel_id=1, source_target_pairs={{0,8},{1,9},{2,10},{3,11},{4,12},{5,13},{6,14},{7,15},{8,0},{9,1},... | collective-permute-start | bytes 1572872 | tf_op jit(solution)/shard_map/ppermute | solution.py:51
  154.2 8.6 %collective-permute-start.40 = (bf16[256,384]{1,0:T(8,128)(2,1)S(1)}, bf16[256,384]{1,0:T(8,128)(2,1)S(1)}, u32[]{:S(2)}, u32[]{:S(2)}) collective-permute-start(bf16[256,384]{1,0:T(8,128)(2,1)S(1)} %fusion.4), channel_id=1, source_target_pairs={{0,16},{16,0},{32,48},{48,32},{64,80},{80,64},{96,112},{112,96},{1... | collective-permute-start | bytes 589832 | tf_op jit(solution)/shard_map/ppermute | solution.py:55
  157.8 12.5 %collective-permute-start.39 = (bf16[256,768]{1,0:T(8,128)(2,1)S(1)}, bf16[256,768]{1,0:T(8,128)(2,1)S(1)}, u32[]{:S(2)}, u32[]{:S(2)}) collective-permute-start(bf16[256,768]{1,0:T(8,128)(2,1)S(1)} %fusion.1), channel_id=1, source_target_pairs={{0,16},{16,0},{32,48},{48,32},{64,80},{80,64},{96,112},{112,96},{1... | collective-permute-start | bytes 1179656 | tf_op jit(solution)/shard_map/ppermute | solution.py:55

commit v3 on v2

--- a/solution.py
+++ b/solution.py
@@ -313,45 +313,38 @@
     firsts = slope_call(table, 0, near, downs, pre, 4)
     hidden = hidden_call(table, pre, step, 1)
 
-    above_y, below_y, far, inputs, w_gate, w_up, _, _ = together(
-        above_y, below_y, far, inputs, w_gate, w_up, firsts[0], hidden
-    )
+    above_y, below_y, far, inputs, _, _ = together(above_y, below_y, far, inputs, firsts[0], hidden)
     far_y = [tsend(above_y[:part], X_DOWN), tsend(below_y[part:], X_UP)]
-    far_y, other_in, w_gate_in, w_up_in, inputs = together(
-        far_y, tsend(inputs, Y_SWAP), tsend(w_gate, CORE), tsend(w_up, CORE), inputs
-    )
+    above_in, below_in, other_in = tsend(inputs, X_DOWN), tsend(inputs, X_UP), tsend(inputs, Y_SWAP)
     last = [above_y, below_y, *far, *far_y]
-
-    above_in, below_in = tsend(inputs, X_DOWN), tsend(inputs, X_UP)
     down_own, down_other = weight_call(table, 0, NZ, near + last, [(hidden,)], 12)
     down_other = tsend(down_other, CORE)
-    above_in, below_in, other_in, _ = together(above_in, below_in, other_in, down_own)
+    above_in, below_in, other_in, w_gate, w_up, _ = together(above_in, below_in, other_in, w_gate, w_up, down_own)
+
     rows_in = [inputs, other_in, above_in, below_in]
     above_y, below_y = tsend(other_in, X_DOWN), tsend(other_in, X_UP)
+    w_gate_in, w_up_in = tsend(w_gate, CORE), tsend(w_up, CORE)
     seconds = slope_call(table, CHUNKS // 2, last, after(downs, above_in, below_in, down_own), pre, 12)
-    above_y, below_y, below_in = together(above_y, below_y, below_in)
+    above_y, below_y, below_in, w_gate_in, w_up_in = together(above_y, below_y, below_in, w_gate_in, w_up_in)
     far, far_y = tsend(below_in, X_UP), tsend(above_y, X_DOWN)
     rows_in += [above_y, below_y, far, far_y]
     d_gate, d_up = zip(firsts, seconds)
     partial = input_call(*after((d_gate, d_up), down_other, above_y, below_y), (w_gate, w_gate_in, w_up, w_up_in), 12)
     far_down, one_down, three_down, rest_down = split(down_own + down_other)
-    far_down = dsend(low(far_down), Z_FAR)
-
-    d_gate, d_up = after((d_gate, d_up), partial[0, 0], far_down)
+    far_down, one_down, three_down = dsend(low(far_down), Z_FAR), dsend(low(one_down), Z_UP), dsend(low(three_down), Z_DOWN)
+
+    d_gate, d_up = after((d_gate, d_up), partial[0, 0], far_down, one_down, three_down)
     far_own, far_other = weight_call(table, 0, 1, rows_in, (d_gate, d_up), 0.1)
     far_other = tsend(far_other, CORE)
     one, three = tsend(after(partial[1, 2], far), X_UP), tsend(after(partial[1, 3], far_y), X_DOWN)
-    one_down, three_down = after((low(one_down), low(three_down)), partial[0, 0])
-    one_down, three_down = dsend(one_down, Z_UP), dsend(three_down, Z_DOWN)
-    d_gate, d_up, one, three, one_down, three_down, below = together(
-        d_gate, d_up, one, three, one_down, three_down, partial[0, 2]
-    )
     d_gate, d_up = after((d_gate, d_up), far_own, far_other)
     ring_own, ring_other = weight_call(table, 1, 2, rows_in, (d_gate, d_up), 12)
     far_sum = low(far_own + far_other)
     far_up, far_dn = dsend(far_sum[0], Z_UP), dsend(far_sum[1], Z_DOWN)
+    one, three, below, _ = together(one, three, partial[0, 2], ring_own)
     above, below = tsend(low(partial[1, 1] + one), X_UP), tsend(below, X_DOWN)
-    far_up, far_dn, ring_other, above, below, up = together(far_up, far_dn, ring_other, above, below, partial[0, 1])
+    far_up, far_dn, ring_other = together(far_up, far_dn, ring_other)
+    above, below, up = together(above, below, partial[0, 1])
     d_gate, d_up = after((d_gate, d_up), ring_own)
     rest_own, rest_other = weight_call(table, 3, 1, rows_in, (d_gate, d_up), 12)
     ring_up, ring_dn = ring_call(ring_own, tsend(ring_other, CORE), *after((far_up, far_dn), rest_own))

time: 172 us -> 170 us (0.988)
  waiting for transfers between devices: 65.2 us -> 59.6 us
  local copies, waits for them, and re-layouts: 13.4 us -> 16.6 us
  starting transfers between devices: 54 us -> 55.9 us
    ppermute x9, waiting for transfers between devices: 20.1 us -> 13.1 us  [dsend(): return lax.ppermute(value, 'dp', pairs)]
    unnamed x27 -> x47, local copies, waits for them, and re-layouts: 8.82 us -> 12.1 us
    ppermute x9, starting transfers between devices: 16.9 us -> 18.8 us  [dsend(): return lax.ppermute(value, 'dp', pairs)]
  transfers between devices with their start and end apart: 41 -> 41, of which waited for: 17 -> 16; matrix products, arithmetic and copies ran while one was open for 4% -> 4% of each run, Pallas kernels for 20% -> 18%
where the time goes in v3:
time: 170 us
  waiting for transfers between devices  59.6 us (35%)
  starting transfers between devices  55.9 us (33%)
  Pallas kernels  33.4 us (20%)
  local copies, waits for them, and re-layouts  16.6 us (10%)
  other arithmetic  2.91 us (2%)
    ppermute x32, waiting for transfers between devices, tsend(): return lax.ppermute(value, 'tensor', pairs)  46.5 us
    ppermute x32, starting transfers between devices, tsend(): return lax.ppermute(value, 'tensor', pairs)  37.2 us
    ppermute x9, starting transfers between devices, dsend(): return lax.ppermute(value, 'dp', pairs)  18.8 us
    pallas_call x4, Pallas kernels, weight_call(): pl.pallas_call(lambda *refs: weight_body(count, wide, *refs), out_shape=(...  14.9 us
    ppermute x9, waiting for transfers between devices, dsend(): return lax.ppermute(value, 'dp', pairs)  13.1 us
    unnamed x47, local copies, waits for them, and re-layouts  12.1 us
    pallas_call x2, Pallas kernels, slope_call(): pl.pallas_call(lambda *refs: slope_body(first, count, *refs), out_shape=(...  8.3 us
    pallas_call x1, Pallas kernels, input_call(): pl.pallas_call(lambda *refs: input_body(parts, *refs), out_shape=[jax.Sha...  7.7 us
  transfers between devices with their start and end apart: 41, of which 16 were waited for; matrix products, arithmetic and copies ran while one was open for 4% of the time, Pallas kernels for 18%

profile of v3, /device:TPU:0, one launch (start us, length us, event | category | flops | bytes accessed | tf_op | source)
XLA Modules:
  0.0 169.5 jit_solution(18324975020278460819)
XLA Ops:
  0.7 0.5 collective-permute-start.4
  1.2 1.6 collective-permute-start.2
  2.8 1.7 collective-permute-start.1
  4.5 1.7 collective-permute-start
  6.1 10.4 %collective-permute-done.2.refs_4_ = bf16[128,2048]{1,0:T(8,128)(2,1)S(1)} collective-permute-done((bf16[128,2048]{1,0:T(8,128)(2,1)}, bf16[128,2048]{1,0:T(8,128)(2,1)S(1)}, u32[]{:S(2)}, u32[]{:S(2)}) %collective-permute-start.2) | collective-permute-done | bytes 524320 | tf_op jit(solution)/shard_map/ppermute | solution.py:51
  16.7 1.4 collective-permute-done.refs_2_
  18.0 1.2 copy-done.15
  19.3 0.7 dynamic-slice_bitcast_fusion
  20.0 0.7 dynamic-slice_bitcast_fusion.1
  21.2 2.9 %collective-permute-start.6 = (bf16[128,2048]{1,0:T(8,128)(2,1)}, bf16[128,2048]{1,0:T(8,128)(2,1)S(1)}, u32[]{:S(2)}, u32[]{:S(2)}) collective-permute-start(bf16[128,2048]{1,0:T(8,128)(2,1)} %copy-done.20), channel_id=1, source_target_pairs={{0,6},{1,7},{2,0},{3,1},{4,2},{5,3},{6,4},{7,5},{8,14},{9,15},{10,... | collective-permute-start | bytes 1572872 | tf_op jit(solution)/shard_map/ppermute | solution.py:51
  24.0 1.0 slice.45
  25.0 1.0 slice.46
  26.1 3.2 %collective-permute-start.8 = (bf16[64,2048]{1,0:T(8,128)(2,1)S(1)}, bf16[64,2048]{1,0:T(8,128)(2,1)S(1)}, u32[]{:S(2)}, u32[]{:S(2)}) collective-permute-start(bf16[64,2048]{1,0:T(8,128)(2,1)S(1)} %slice.45), channel_id=1, source_target_pairs={{0,6},{1,7},{2,0},{3,1},{4,2},{5,3},{6,4},{7,5},{8,14},{9,15},{10,... | collective-permute-start | bytes 786440 | tf_op jit(solution)/shard_map/ppermute | solution.py:51
  29.3 1.4 copy-done
  30.7 1.4 copy-done.2
  32.1 1.0 copy-done.6
  33.2 1.0 copy-done.9
  34.2 1.4 copy-done.11
  35.6 1.4 copy-done.16
  37.0 1.0 copy-done.18
  38.1 1.0 copy-done.21
  39.1 4.1 %slope.2 = (bf16[512,768]{1,0:T(8,128)(2,1)S(1)}, bf16[512,768]{1,0:T(8,128)(2,1)S(1)}) custom-call(s32[13]{0:T(128)S(1)} %pad_add_fusion.refs_0_.table_ref, bf16[128,2048]{1,0:T(8,128)(2,1)S(1)} %copy-done.18, bf16[128,2048]{1,0:T(8,128)(2,1)S(1)} %copy-done.21, bf16[128,2048]{1,0:T(8,128)(2,1)S(1)} %copy-done.9, bf16[128,2048]{1,0:T(8,128)(2,1)S(1)} %copy-done.6, ...), custom_call_target="tpu_custom_call" | custom-call | flops 6442450944 | bytes 33554432 | tf_op jit(solution)/shard_map/slope/pallas_call | solution.py:149
  43.3 1.8 %hidden.1.refs_11_ = bf16[1024,768]{1,0:T(8,128)(2,1)S(1)} custom-call(s32[13]{0:T(128)S(1)} %pad_add_fusion.refs_0_.table_ref, bf16[2048,384]{1,0:T(8,128)(2,1)S(1)} %copy-done.1, bf16[2048,384]{1,0:T(8,128)(2,1)S(1)} %collective-permute-done.4.refs_8_.refs_1_.refs_10_, bf16[2048,384]{1,0:T(8,128)(2,1)S(1)} %copy-done.2, ...), custom_call_target="tpu_custom_call" | custom-call | flops 12582912 | bytes 4718592 | tf_op jit(solution)/shard_map/hidden/pallas_call | solution.py:81
  45.3 3.2 %collective-permute-start.10 = (bf16[64,2048]{1,0:T(8,128)(2,1)S(1)}, bf16[64,2048]{1,0:T(8,128)(2,1)S(1)}, u32[]{:S(2)}, u32[]{:S(2)}) collective-permute-start(bf16[64,2048]{1,0:T(8,128)(2,1)S(1)} %slice.47), channel_id=1, source_target_pairs={{0,6},{1,7},{2,0},{3,1},{4,2},{5,3},{6,4},{7,5},{8,14},{9,15},{10,... | collective-permute-start | bytes 786440 | tf_op jit(solution)/shard_map/ppermute | solution.py:51
  48.5 1.7 collective-permute-start.14
  50.2 3.2 %collective-permute-start.12 = (bf16[128,2048]{1,0:T(8,128)(2,1)S(1)}, bf16[128,2048]{1,0:T(8,128)(2,1)S(1)}, u32[]{:S(2)}, u32[]{:S(2)}) collective-permute-start(bf16[128,2048]{1,0:T(8,128)(2,1)S(1)} %copy-done.4), channel_id=1, source_target_pairs={{0,6},{1,7},{2,0},{3,1},{4,2},{5,3},{6,4},{7,5},{8,14},{9,15},{10,... | collective-permute-start | bytes 1572872 | tf_op jit(solution)/shard_map/ppermute | solution.py:51
  53.4 2.1 %collective-permute-done.11.refs_10_.refs_6_ = bf16[64,2048]{1,0:T(8,128)(2,1)S(1)} collective-permute-done((bf16[64,2048]{1,0:T(8,128)(2,1)S(1)}, bf16[64,2048]{1,0:T(8,128)(2,1)S(1)}, u32[]{:S(2)}, u32[]{:S(2)}) %collective-permute-start.11) | collective-permute-done | bytes 262176 | tf_op jit(solution)/shard_map/ppermute | solution.py:51
  55.6 5.5 %weight.4 = (f32[8,256,384]{2,1,0:T(8,128)S(1)}, bf16[8,256,384]{2,1,0:T(8,128)(2,1)S(1)}) custom-call(s32[13]{0:T(128)S(1)} %pad_add_fusion.refs_0_.table_ref, bf16[128,2048]{1,0:T(8,128)(2,1)S(1)} %copy-done.19, bf16[128,2048]{1,0:T(8,128)(2,1)S(1)} %copy-done.22, bf16[128,2048]{1,0:T(8,128)(2,1)S(1)} %copy-done.10, bf16[128,2048]{1,0:T(8,128)(2,1)S(1)} %copy-done.7, ...), custom_call_target="tpu_custom_call" | custom-call | flops 38654705664 | bytes 125829120 | tf_op jit(solution)/shard_map/weight/pallas_call | solution.py:204
  61.2 4.1 %collective-permute-done.13.refs_4_ = bf16[128,2048]{1,0:T(8,128)(2,1)S(1)} collective-permute-done((bf16[128,2048]{1,0:T(8,128)(2,1)S(1)}, bf16[128,2048]{1,0:T(8,128)(2,1)S(1)}, u32[]{:S(2)}, u32[]{:S(2)}) %collective-permute-start.13) | collective-permute-done | bytes 524320 | tf_op jit(solution)/shard_map/ppermute | solution.py:51
  65.3 3.2 %collective-permute-start.16 = (bf16[128,2048]{1,0:T(8,128)(2,1)S(1)}, bf16[128,2048]{1,0:T(8,128)(2,1)S(1)}, u32[]{:S(2)}, u32[]{:S(2)}) collective-permute-start(bf16[128,2048]{1,0:T(8,128)(2,1)S(1)} %collective-permute-done.14.refs_2_), channel_id=1, source_target_pairs={{0,6},{1,7},{2,0},{3,1},{4,2},{5,3},{6,4},{7,5},{8,14},{9,15},{10,... | collective-permute-start | bytes 1572872 | tf_op jit(solution)/shard_map/ppermute | solution.py:51
  68.5 0.5 collective-permute-start.19
  69.0 4.2 %slope.3 = (bf16[512,768]{1,0:T(8,128)(2,1)S(1)}, bf16[512,768]{1,0:T(8,128)(2,1)S(1)}) custom-call(s32[13]{0:T(128)S(1)} %pad_add_fusion.refs_0_.table_ref, bf16[128,2048]{1,0:T(8,128)(2,1)S(1)} %collective-permute-done.6.refs_5_.refs_1_, bf16[128,2048]{1,0:T(8,128)(2,1)S(1)} %collective-permute-done.7.refs_6_.refs_2_, ...), custom_call_target="tpu_custom_call" | custom-call | flops 19327352832 | bytes 100663296 | tf_op jit(solution)/shard_map/slope/pallas_call | solution.py:149
  73.2 0.4 fusion.5
  73.8 4.2 %collective-permute-start.24 = (bf16[2,256,384]{2,1,0:T(8,128)(2,1)S(1)}, bf16[2,256,384]{2,1,0:T(8,128)(2,1)S(1)}, u32[]{:S(2)}, u32[]{:S(2)}) collective-permute-start(bf16[2,256,384]{2,1,0:T(8,128)(2,1)S(1)} %get-tuple-element.170), channel_id=1, source_target_pairs={{0,96},{16,112},{32,0},{48,16},{64,32},{80,48},{96,64},{112,80},{1... | collective-permute-start | bytes 1179656 | tf_op jit(solution)/shard_map/ppermute | solution.py:55
  78.0 1.0 collective-permute-done.17.refs_6_
  78.9 1.9 %collective-permute-start.23 = (bf16[2,256,384]{2,1,0:T(8,128)(2,1)S(1)}, bf16[2,256,384]{2,1,0:T(8,128)(2,1)S(1)}, u32[]{:S(2)}, u32[]{:S(2)}) collective-permute-start(bf16[2,256,384]{2,1,0:T(8,128)(2,1)S(1)} %get-tuple-element.171), channel_id=1, source_target_pairs={{0,32},{16,48},{32,64},{48,80},{64,96},{80,112},{96,0},{112,16},{1... | collective-permute-start | bytes 1179656 | tf_op jit(solution)/shard_map/ppermute | solution.py:55
  80.9 3.6 %collective-permute-start.22 = (bf16[2,256,384]{2,1,0:T(8,128)(2,1)S(1)}, bf16[2,256,384]{2,1,0:T(8,128)(2,1)S(1)}, u32[]{:S(2)}, u32[]{:S(2)}) collective-permute-start(bf16[2,256,384]{2,1,0:T(8,128)(2,1)S(1)} %get-tuple-element.172), channel_id=1, source_target_pairs={{0,64},{16,80},{32,96},{48,112},{64,0},{80,16},{96,32},{112,48},{1... | collective-permute-start | bytes 1179656 | tf_op jit(solution)/shard_map/ppermute | solution.py:55
  84.5 3.2 %collective-permute-start.21 = (bf16[128,2048]{1,0:T(8,128)(2,1)S(1)}, bf16[128,2048]{1,0:T(8,128)(2,1)S(1)}, u32[]{:S(2)}, u32[]{:S(2)}) collective-permute-start(bf16[128,2048]{1,0:T(8,128)(2,1)S(1)} %collective-permute-done.16.refs_5_), channel_id=1, source_target_pairs={{0,6},{1,7},{2,0},{3,1},{4,2},{5,3},{6,4},{7,5},{8,14},{9,15},{10,... | collective-permute-start | bytes 1572872 | tf_op jit(solution)/shard_map/ppermute | solution.py:51
  87.7 7.7 %input.1 = (f32[128,2048]{1,0:T(8,128)S(1)}, f32[128,2048]{1,0:T(8,128)S(1)}, bf16[128,2048]{1,0:T(8,128)(2,1)S(1)}, f32[128,2048]{1,0:T(8,128)S(1)}, f32[128,20...) custom-call(bf16[512,768]{1,0:T(8,128)(2,1)S(1)} %get-tuple-element., ...), custom_call_target="tpu_custom_call" | custom-call | flops 77309411328 | bytes 176160768 | tf_op jit(solution)/shard_map/input/pallas_call | solution.py:276
  95.4 4.1 %collective-permute-done.22 = bf16[2,256,384]{2,1,0:T(8,128)(2,1)S(1)} collective-permute-done((bf16[2,256,384]{2,1,0:T(8,128)(2,1)S(1)}, bf16[2,256,384]{2,1,0:T(8,128)(2,1)S(1)}, u32[]{:S(2)}, u32[]{:S(2)}) %collective-permute-start.22) | collective-permute-done | bytes 393248 | tf_op jit(solution)/shard_map/ppermute | solution.py:55
  99.5 2.4 %weight.5 = (f32[2,256,768]{2,1,0:T(8,128)S(1)}, bf16[2,256,768]{2,1,0:T(8,128)(2,1)S(1)}) custom-call(s32[13]{0:T(128)S(1)} %pad_add_fusion.refs_0_.table_ref, bf16[128,2048]{1,0:T(8,128)(2,1)S(1)} %copy-done.4, bf16[128,2048]{1,0:T(8,128)(2,1)S(1)} %collective-permute-done.14.refs_2_, bf16[128,2048]{1,0:T(8,128)(2,1)S(1)} %collective-permute-done.12.refs_3_, ...), custom_call_target="tpu_custom_call" | custom-call | flops 161061280 | bytes 1048576 | tf_op jit(solution)/shard_map/weight/pallas_call | solution.py:204
  102.0 1.8 %collective-permute-start.32 = (bf16[128,2048]{1,0:T(8,128)(2,1)S(1)}, bf16[128,2048]{1,0:T(8,128)(2,1)S(1)}, u32[]{:S(2)}, u32[]{:S(2)}) collective-permute-start(bf16[128,2048]{1,0:T(8,128)(2,1)S(1)} %get-tuple-element.147), channel_id=1, source_target_pairs={{0,6},{1,7},{2,0},{3,1},{4,2},{5,3},{6,4},{7,5},{8,14},{9,15},{10,... | collective-permute-start | bytes 1572872 | tf_op jit(solution)/shard_map/ppermute | solution.py:51
  104.6 2.0 %collective-permute-start.26 = (bf16[256,768]{1,0:T(8,128)(2,1)S(1)}, bf16[256,768]{1,0:T(8,128)(2,1)S(1)}, u32[]{:S(2)}, u32[]{:S(2)}) collective-permute-start(bf16[256,768]{1,0:T(8,128)(2,1)S(1)} %get-tuple-element.176), channel_id=1, source_target_pairs={{0,32},{16,48},{32,64},{48,80},{64,96},{80,112},{96,0},{112,16},{1... | collective-permute-start | bytes 1179656 | tf_op jit(solution)/shard_map/ppermute | solution.py:55
  106.6 4.6 %weight.6 = (f32[4,256,768]{2,1,0:T(8,128)S(1)}, bf16[4,256,768]{2,1,0:T(8,128)(2,1)S(1)}) custom-call(s32[13]{0:T(128)S(1)} %pad_add_fusion.refs_0_.table_ref, bf16[128,2048]{1,0:T(8,128)(2,1)S(1)} %copy-done.4, bf16[128,2048]{1,0:T(8,128)(2,1)S(1)} %collective-permute-done.14.refs_2_, bf16[128,2048]{1,0:T(8,128)(2,1)S(1)} %collective-permute-done.12.refs_3_, ...), custom_call_target="tpu_custom_call" | custom-call | flops 38654705664 | bytes 125829120 | tf_op jit(solution)/shard_map/weight/pallas_call | solution.py:204
  111.2 5.1 %collective-permute-done.32 = bf16[128,2048]{1,0:T(8,128)(2,1)S(1)} collective-permute-done((bf16[128,2048]{1,0:T(8,128)(2,1)S(1)}, bf16[128,2048]{1,0:T(8,128)(2,1)S(1)}, u32[]{:S(2)}, u32[]{:S(2)}) %collective-permute-start.32) | collective-permute-done | bytes 524320 | tf_op jit(solution)/shard_map/ppermute | solution.py:51
  116.3 2.7 %collective-permute-done.31 = bf16[128,2048]{1,0:T(8,128)(2,1)S(1)} collective-permute-done((bf16[128,2048]{1,0:T(8,128)(2,1)S(1)}, bf16[128,2048]{1,0:T(8,128)(2,1)S(1)}, u32[]{:S(2)}, u32[]{:S(2)}) %collective-permute-start.31) | collective-permute-done | bytes 524320 | tf_op jit(solution)/shard_map/ppermute | solution.py:51
  119.2 3.2 %collective-permute-start.34 = (bf16[128,2048]{1,0:T(8,128)(2,1)S(1)}, bf16[128,2048]{1,0:T(8,128)(2,1)S(1)}, u32[]{:S(2)}, u32[]{:S(2)}) collective-permute-start(bf16[128,2048]{1,0:T(8,128)(2,1)S(1)} %get-tuple-element.150), channel_id=1, source_target_pairs={{0,6},{1,7},{2,0},{3,1},{4,2},{5,3},{6,4},{7,5},{8,14},{9,15},{10,... | collective-permute-start | bytes 1572872 | tf_op jit(solution)/shard_map/ppermute | solution.py:51
  122.4 2.4 %weight.7 = (f32[2,256,768]{2,1,0:T(8,128)S(1)}, bf16[2,256,768]{2,1,0:T(8,128)(2,1)S(1)}) custom-call(s32[13]{0:T(128)S(1)} %pad_add_fusion.refs_0_.table_ref, bf16[128,2048]{1,0:T(8,128)(2,1)S(1)} %copy-done.4, bf16[128,2048]{1,0:T(8,128)(2,1)S(1)} %collective-permute-done.14.refs_2_, bf16[128,2048]{1,0:T(8,128)(2,1)S(1)} %collective-permute-done.12.refs_3_, ...), custom_call_target="tpu_custom_call" | custom-call | flops 19327352832 | bytes 125829120 | tf_op jit(solution)/shard_map/weight/pallas_call | solution.py:204
  124.8 0.6 collective-permute-start.37
  125.4 8.1 %collective-permute-done.33 = bf16[128,2048]{1,0:T(8,128)(2,1)S(1)} collective-permute-done((bf16[128,2048]{1,0:T(8,128)(2,1)S(1)}, bf16[128,2048]{1,0:T(8,128)(2,1)S(1)}, u32[]{:S(2)}, u32[]{:S(2)}) %collective-permute-start.33) | collective-permute-done | bytes 524320 | tf_op jit(solution)/shard_map/ppermute | solution.py:51
  133.5 0.7 ring.1
  134.3 3.2 %collective-permute-start.30 = (bf16[2,256,768]{2,1,0:T(8,128)(2,1)S(1)}, bf16[2,256,768]{2,1,0:T(8,128)(2,1)S(1)}, u32[]{:S(2)}, u32[]{:S(2)}) collective-permute-start(bf16[2,256,768]{2,1,0:T(8,128)(2,1)S(1)} %get-tuple-element.141), channel_id=1, source_target_pairs={{0,96},{16,112},{32,0},{48,16},{64,32},{80,48},{96,64},{112,80},{1... | collective-permute-start | bytes 2359304 | tf_op jit(solution)/shard_map/ppermute | solution.py:55
  137.7 3.0 %collective-permute-start.35 = (bf16[128,2048]{1,0:T(8,128)(2,1)S(1)}, bf16[128,2048]{1,0:T(8,128)(2,1)S(1)}, u32[]{:S(2)}, u32[]{:S(2)}) collective-permute-start(bf16[128,2048]{1,0:T(8,128)(2,1)S(1)} %add_convert_fusion.2), channel_id=1, source_target_pairs={{0,6},{1,7},{2,0},{3,1},{4,2},{5,3},{6,4},{7,5},{8,14},{9,15},{10,... | collective-permute-start | bytes 1572872 | tf_op jit(solution)/shard_map/ppermute | solution.py:51
  140.9 0.8 collective-permute-start.38
  141.8 7.8 %collective-permute-done.35 = bf16[128,2048]{1,0:T(8,128)(2,1)S(1)} collective-permute-done((bf16[128,2048]{1,0:T(8,128)(2,1)S(1)}, bf16[128,2048]{1,0:T(8,128)(2,1)S(1)}, u32[]{:S(2)}, u32[]{:S(2)}) %collective-permute-start.35) | collective-permute-done | bytes 524320 | tf_op jit(solution)/shard_map/ppermute | solution.py:51
  149.6 3.4 %collective-permute-done.36 = bf16[128,2048]{1,0:T(8,128)(2,1)S(1)} collective-permute-done((bf16[128,2048]{1,0:T(8,128)(2,1)S(1)}, bf16[128,2048]{1,0:T(8,128)(2,1)S(1)}, u32[]{:S(2)}, u32[]{:S(2)}) %collective-permute-start.36) | collective-permute-done | bytes 524320 | tf_op jit(solution)/shard_map/ppermute | solution.py:51
  153.0 0.4 collective-permute-done.29
  153.6 2.7 %collective-permute-start.40 = (bf16[256,384]{1,0:T(8,128)(2,1)S(1)}, bf16[256,384]{1,0:T(8,128)(2,1)S(1)}, u32[]{:S(2)}, u32[]{:S(2)}) collective-permute-start(bf16[256,384]{1,0:T(8,128)(2,1)S(1)} %fusion.4), channel_id=1, source_target_pairs={{0,16},{16,0},{32,48},{48,32},{64,80},{80,64},{96,112},{112,96},{1... | collective-permute-start | bytes 589832 | tf_op jit(solution)/shard_map/ppermute | solution.py:55
  156.6 1.0 collective-permute-start.39
  157.6 1.3 convert_add_fusion.2
  158.9 4.0 %collective-permute-done.40 = bf16[256,384]{1,0:T(8,128)(2,1)S(1)} collective-permute-done((bf16[256,384]{1,0:T(8,128)(2,1)S(1)}, bf16[256,384]{1,0:T(8,128)(2,1)S(1)}, u32[]{:S(2)}, u32[]{:S(2)}) %collective-permute-start.40) | collective-permute-done | bytes 196640 | tf_op jit(solution)/shard_map/ppermute | solution.py:55
  162.9 0.9 copy.13
  163.9 4.7 %collective-permute-done.39 = bf16[256,768]{1,0:T(8,128)(2,1)S(1)} collective-permute-done((bf16[256,768]{1,0:T(8,128)(2,1)S(1)}, bf16[256,768]{1,0:T(8,128)(2,1)S(1)}, u32[]{:S(2)}, u32[]{:S(2)}) %collective-permute-start.39) | collective-permute-done | bytes 393248 | tf_op jit(solution)/shard_map/ppermute | solution.py:55
  168.6 0.9 fusion.7
  (97 shorter events, 3.3 us)
Async XLA Ops:
  0.6 17.4 %collective-permute-start.3 = (bf16[384,2048]{1,0:T(8,128)(2,1)}, bf16[384,2048]{1,0:T(8,128)(2,1)S(1)}, u32[]{:S(2)}, u32[]{:S(2)}) collective-permute-start(bf16[384,2048]{1,0:T(8,128)(2,1)} %refs_7_.2), channel_id=1, source_target_pairs={{0,1},{1,0},{2,3},{3,2},{4,5},{5,4},{6,7},{7,6},{8,9},{9,8},{10,11... | collective-permute-start | bytes 4718600 | tf_op jit(solution)/shard_map/ppermute | solution.py:51
  0.7 18.5 %collective-permute-start.4 = (bf16[2048,384]{1,0:T(8,128)(2,1)}, bf16[2048,384]{1,0:T(8,128)(2,1)S(1)}, u32[]{:S(2)}, u32[]{:S(2)}) collective-permute-start(bf16[2048,384]{1,0:T(8,128)(2,1)} %refs_9_.2), channel_id=1, source_target_pairs={{0,1},{1,0},{2,3},{3,2},{4,5},{5,4},{6,7},{7,6},{8,9},{9,8},{10,11... | collective-permute-start | bytes 4718600 | tf_op jit(solution)/shard_map/ppermute | solution.py:51
  1.2 15.3 %collective-permute-start.2 = (bf16[128,2048]{1,0:T(8,128)(2,1)}, bf16[128,2048]{1,0:T(8,128)(2,1)S(1)}, u32[]{:S(2)}, u32[]{:S(2)}) collective-permute-start(bf16[128,2048]{1,0:T(8,128)(2,1)} %refs_1_.3), channel_id=1, source_target_pairs={{0,2},{1,3},{2,4},{3,5},{4,6},{5,7},{6,0},{7,1},{8,10},{9,11},{10,... | collective-permute-start | bytes 1572872 | tf_op jit(solution)/shard_map/ppermute | solution.py:51
  2.8 13.9 %collective-permute-start.1 = (bf16[128,2048]{1,0:T(8,128)(2,1)}, bf16[128,2048]{1,0:T(8,128)(2,1)S(1)}, u32[]{:S(2)}, u32[]{:S(2)}) collective-permute-start(bf16[128,2048]{1,0:T(8,128)(2,1)} %refs_1_.3), channel_id=1, source_target_pairs={{0,6},{1,7},{2,0},{3,1},{4,2},{5,3},{6,4},{7,5},{8,14},{9,15},{10,... | collective-permute-start | bytes 1572872 | tf_op jit(solution)/shard_map/ppermute | solution.py:51
  4.5 13.6 %collective-permute-start = (bf16[128,2048]{1,0:T(8,128)(2,1)}, bf16[128,2048]{1,0:T(8,128)(2,1)S(1)}, u32[]{:S(2)}, u32[]{:S(2)}) collective-permute-start(bf16[128,2048]{1,0:T(8,128)(2,1)} %refs_1_.3), channel_id=1, source_target_pairs={{0,8},{1,9},{2,10},{3,11},{4,12},{5,13},{6,14},{7,15},{8,0},{9,1},... | collective-permute-start | bytes 1572872 | tf_op jit(solution)/shard_map/ppermute | solution.py:51
  16.6 2.7 %copy-start.5 = (bf16[128,2048]{1,0:T(8,128)(2,1)}, bf16[128,2048]{1,0:T(8,128)(2,1)S(1)}, u32[]{:S(2)}) copy-start(bf16[128,2048]{1,0:T(8,128)(2,1)S(1)} %collective-permute-done.2.refs_4_) | copy-start | bytes 1572868
  16.6 2.6 %copy-start.8 = (bf16[128,2048]{1,0:T(8,128)(2,1)}, bf16[128,2048]{1,0:T(8,128)(2,1)S(1)}, u32[]{:S(2)}) copy-start(bf16[128,2048]{1,0:T(8,128)(2,1)S(1)} %collective-permute-done.1.refs_3_) | copy-start | bytes 1572868
  18.0 1.3 copy-start.20
  18.0 1.2 copy-start.15
  19.2 10.0 %collective-permute-start.5 = (bf16[2048,384]{1,0:T(8,128)(2,1)}, bf16[2048,384]{1,0:T(8,128)(2,1)S(1)}, u32[]{:S(2)}, u32[]{:S(2)}) collective-permute-start(bf16[2048,384]{1,0:T(8,128)(2,1)} %refs_11_), channel_id=1, source_target_pairs={{0,1},{1,0},{2,3},{3,2},{4,5},{5,4},{6,7},{7,6},{8,9},{9,8},{10,11... | collective-permute-start | bytes 4718600 | tf_op jit(solution)/shard_map/ppermute | solution.py:51
  20.8 24.3 %collective-permute-start.7 = (bf16[128,2048]{1,0:T(8,128)(2,1)}, bf16[128,2048]{1,0:T(8,128)(2,1)S(1)}, u32[]{:S(2)}, u32[]{:S(2)}) collective-permute-start(bf16[128,2048]{1,0:T(8,128)(2,1)} %copy-done.20), channel_id=1, source_target_pairs={{0,2},{1,3},{2,4},{3,5},{4,6},{5,7},{6,0},{7,1},{8,10},{9,11},{10,... | collective-permute-start | bytes 1572872 | tf_op jit(solution)/shard_map/ppermute | solution.py:51
  21.2 23.9 %collective-permute-start.6 = (bf16[128,2048]{1,0:T(8,128)(2,1)}, bf16[128,2048]{1,0:T(8,128)(2,1)S(1)}, u32[]{:S(2)}, u32[]{:S(2)}) collective-permute-start(bf16[128,2048]{1,0:T(8,128)(2,1)} %copy-done.20), channel_id=1, source_target_pairs={{0,6},{1,7},{2,0},{3,1},{4,2},{5,3},{6,4},{7,5},{8,14},{9,15},{10,... | collective-permute-start | bytes 1572872 | tf_op jit(solution)/shard_map/ppermute | solution.py:51
  26.0 19.1 %collective-permute-start.9 = (bf16[64,2048]{1,0:T(8,128)(2,1)S(1)}, bf16[64,2048]{1,0:T(8,128)(2,1)S(1)}, u32[]{:S(2)}, u32[]{:S(2)}) collective-permute-start(bf16[64,2048]{1,0:T(8,128)(2,1)S(1)} %slice.46), channel_id=1, source_target_pairs={{0,2},{1,3},{2,4},{3,5},{4,6},{5,7},{6,0},{7,1},{8,10},{9,11},{10,... | collective-permute-start | bytes 786440 | tf_op jit(solution)/shard_map/ppermute | solution.py:51
  26.1 19.0 %collective-permute-start.8 = (bf16[64,2048]{1,0:T(8,128)(2,1)S(1)}, bf16[64,2048]{1,0:T(8,128)(2,1)S(1)}, u32[]{:S(2)}, u32[]{:S(2)}) collective-permute-start(bf16[64,2048]{1,0:T(8,128)(2,1)S(1)} %slice.45), channel_id=1, source_target_pairs={{0,6},{1,7},{2,0},{3,1},{4,2},{5,3},{6,4},{7,5},{8,14},{9,15},{10,... | collective-permute-start | bytes 786440 | tf_op jit(solution)/shard_map/ppermute | solution.py:51
  29.3 1.4 copy-start
  30.7 1.4 copy-start.2
  32.1 1.0 copy-start.6
  33.2 1.0 copy-start.9
  34.2 1.4 copy-start.11
  35.6 1.4 copy-start.16
  37.0 1.0 copy-start.18
  38.1 1.0 copy-start.21
  39.1 4.1 %copy-start.1 = (bf16[2048,384]{1,0:T(8,128)(2,1)S(1)}, bf16[2048,384]{1,0:T(8,128)(2,1)}, u32[]{:S(2)}) copy-start(bf16[2048,384]{1,0:T(8,128)(2,1)} %refs_9_.2) | copy-start | bytes 4718596
  43.3 5.3 %copy-start.4 = (bf16[128,2048]{1,0:T(8,128)(2,1)S(1)}, bf16[128,2048]{1,0:T(8,128)(2,1)}, u32[]{:S(2)}) copy-start(bf16[128,2048]{1,0:T(8,128)(2,1)} %refs_1_.6) | copy-start | bytes 1572868
  43.3 12.3 %copy-start.7 = (bf16[128,2048]{1,0:T(8,128)(2,1)S(1)}, bf16[128,2048]{1,0:T(8,128)(2,1)}, u32[]{:S(2)}) copy-start(bf16[128,2048]{1,0:T(8,128)(2,1)} %copy-done.5) | copy-start | bytes 1572868
  43.3 12.3 %copy-start.10 = (bf16[128,2048]{1,0:T(8,128)(2,1)S(1)}, bf16[128,2048]{1,0:T(8,128)(2,1)}, u32[]{:S(2)}) copy-start(bf16[128,2048]{1,0:T(8,128)(2,1)} %copy-done.8) | copy-start | bytes 1572868
  43.3 12.3 %copy-start.19 = (bf16[128,2048]{1,0:T(8,128)(2,1)S(1)}, bf16[128,2048]{1,0:T(8,128)(2,1)}, u32[]{:S(2)}) copy-start(bf16[128,2048]{1,0:T(8,128)(2,1)} %refs_1_.3) | copy-start | bytes 1572868
  43.3 12.3 %copy-start.22 = (bf16[128,2048]{1,0:T(8,128)(2,1)S(1)}, bf16[128,2048]{1,0:T(8,128)(2,1)}, u32[]{:S(2)}) copy-start(bf16[128,2048]{1,0:T(8,128)(2,1)} %copy-done.20) | copy-start | bytes 1572868
  45.2 23.3 %copy-start.13 = (bf16[2048,384]{1,0:T(8,128)(2,1)S(1)}, bf16[2048,384]{1,0:T(8,128)(2,1)}, u32[]{:S(2)}) copy-start(bf16[2048,384]{1,0:T(8,128)(2,1)} %refs_4_) | copy-start | bytes 4718596
  45.2 23.3 %copy-start.14 = (bf16[2048,384]{1,0:T(8,128)(2,1)S(1)}, bf16[2048,384]{1,0:T(8,128)(2,1)}, u32[]{:S(2)}) copy-start(bf16[2048,384]{1,0:T(8,128)(2,1)} %refs_6_) | copy-start | bytes 4718596
  45.2 23.8 %copy-start.3 = (bf16[2048,384]{1,0:T(8,128)(2,1)S(1)}, bf16[2048,384]{1,0:T(8,128)(2,1)}, u32[]{:S(2)}) copy-start(bf16[2048,384]{1,0:T(8,128)(2,1)} %refs_11_) | copy-start | bytes 4718596
  45.2 23.8 %copy-start.12 = (bf16[384,2048]{1,0:T(8,128)(2,1)S(1)}, bf16[384,2048]{1,0:T(8,128)(2,1)}, u32[]{:S(2)}) copy-start(bf16[384,2048]{1,0:T(8,128)(2,1)} %refs_7_.2) | copy-start | bytes 4718596
  45.2 23.8 %copy-start.17 = (bf16[384,2048]{1,0:T(8,128)(2,1)S(1)}, bf16[384,2048]{1,0:T(8,128)(2,1)}, u32[]{:S(2)}) copy-start(bf16[384,2048]{1,0:T(8,128)(2,1)} %copy-done.15) | copy-start | bytes 4718596
  45.2 10.3 %collective-permute-start.11 = (bf16[64,2048]{1,0:T(8,128)(2,1)S(1)}, bf16[64,2048]{1,0:T(8,128)(2,1)S(1)}, u32[]{:S(2)}, u32[]{:S(2)}) collective-permute-start(bf16[64,2048]{1,0:T(8,128)(2,1)S(1)} %slice.48), channel_id=1, source_target_pairs={{0,2},{1,3},{2,4},{3,5},{4,6},{5,7},{6,0},{7,1},{8,10},{9,11},{10,... | collective-permute-start | bytes 786440 | tf_op jit(solution)/shard_map/ppermute | solution.py:51
  45.3 10.2 %collective-permute-start.10 = (bf16[64,2048]{1,0:T(8,128)(2,1)S(1)}, bf16[64,2048]{1,0:T(8,128)(2,1)S(1)}, u32[]{:S(2)}, u32[]{:S(2)}) collective-permute-start(bf16[64,2048]{1,0:T(8,128)(2,1)S(1)} %slice.47), channel_id=1, source_target_pairs={{0,6},{1,7},{2,0},{3,1},{4,2},{5,3},{6,4},{7,5},{8,14},{9,15},{10,... | collective-permute-start | bytes 786440 | tf_op jit(solution)/shard_map/ppermute | solution.py:51
  48.5 12.6 %collective-permute-start.14 = (bf16[128,2048]{1,0:T(8,128)(2,1)S(1)}, bf16[128,2048]{1,0:T(8,128)(2,1)S(1)}, u32[]{:S(2)}, u32[]{:S(2)}) collective-permute-start(bf16[128,2048]{1,0:T(8,128)(2,1)S(1)} %copy-done.4), channel_id=1, source_target_pairs={{0,8},{1,9},{2,10},{3,11},{4,12},{5,13},{6,14},{7,15},{8,0},{9,1},... | collective-permute-start | bytes 1572872 | tf_op jit(solution)/shard_map/ppermute | solution.py:51
  50.2 15.1 %collective-permute-start.13 = (bf16[128,2048]{1,0:T(8,128)(2,1)S(1)}, bf16[128,2048]{1,0:T(8,128)(2,1)S(1)}, u32[]{:S(2)}, u32[]{:S(2)}) collective-permute-start(bf16[128,2048]{1,0:T(8,128)(2,1)S(1)} %copy-done.4), channel_id=1, source_target_pairs={{0,2},{1,3},{2,4},{3,5},{4,6},{5,7},{6,0},{7,1},{8,10},{9,11},{10,... | collective-permute-start | bytes 1572872 | tf_op jit(solution)/shard_map/ppermute | solution.py:51
  50.2 15.1 %collective-permute-start.12 = (bf16[128,2048]{1,0:T(8,128)(2,1)S(1)}, bf16[128,2048]{1,0:T(8,128)(2,1)S(1)}, u32[]{:S(2)}, u32[]{:S(2)}) collective-permute-start(bf16[128,2048]{1,0:T(8,128)(2,1)S(1)} %copy-done.4), channel_id=1, source_target_pairs={{0,6},{1,7},{2,0},{3,1},{4,2},{5,3},{6,4},{7,5},{8,14},{9,15},{10,... | collective-permute-start | bytes 1572872 | tf_op jit(solution)/shard_map/ppermute | solution.py:51
  61.1 12.2 %collective-permute-start.15 = (bf16[8,256,384]{2,1,0:T(8,128)(2,1)S(1)}, bf16[8,256,384]{2,1,0:T(8,128)(2,1)S(1)}, u32[]{:S(2)}, u32[]{:S(2)}) collective-permute-start(bf16[8,256,384]{2,1,0:T(8,128)(2,1)S(1)} %get-tuple-element.104), channel_id=1, source_target_pairs={{0,1},{1,0},{2,3},{3,2},{4,5},{5,4},{6,7},{7,6},{8,9},{9,8},{10,11... | collective-permute-start | bytes 4718600 | tf_op jit(solution)/shard_map/ppermute | solution.py:51
  65.3 13.7 %collective-permute-start.17 = (bf16[128,2048]{1,0:T(8,128)(2,1)S(1)}, bf16[128,2048]{1,0:T(8,128)(2,1)S(1)}, u32[]{:S(2)}, u32[]{:S(2)}) collective-permute-start(bf16[128,2048]{1,0:T(8,128)(2,1)S(1)} %collective-permute-done.14.refs_2_), channel_id=1, source_target_pairs={{0,2},{1,3},{2,4},{3,5},{4,6},{5,7},{6,0},{7,1},{8,10},{9,11},{10,... | collective-permute-start | bytes 1572872 | tf_op jit(solution)/shard_map/ppermute | solution.py:51
  65.3 15.6 %collective-permute-start.16 = (bf16[128,2048]{1,0:T(8,128)(2,1)S(1)}, bf16[128,2048]{1,0:T(8,128)(2,1)S(1)}, u32[]{:S(2)}, u32[]{:S(2)}) collective-permute-start(bf16[128,2048]{1,0:T(8,128)(2,1)S(1)} %collective-permute-done.14.refs_2_), channel_id=1, source_target_pairs={{0,6},{1,7},{2,0},{3,1},{4,2},{5,3},{6,4},{7,5},{8,14},{9,15},{10,... | collective-permute-start | bytes 1572872 | tf_op jit(solution)/shard_map/ppermute | solution.py:51
  68.5 15.9 %collective-permute-start.18 = (bf16[2048,384]{1,0:T(8,128)(2,1)S(1)}, bf16[2048,384]{1,0:T(8,128)(2,1)S(1)}, u32[]{:S(2)}, u32[]{:S(2)}) collective-permute-start(bf16[2048,384]{1,0:T(8,128)(2,1)S(1)} %copy-done.13), channel_id=1, source_target_pairs={{0,1},{1,0},{2,3},{3,2},{4,5},{5,4},{6,7},{7,6},{8,9},{9,8},{10,11... | collective-permute-start | bytes 4718600 | tf_op jit(solution)/shard_map/ppermute | solution.py:51
  68.5 15.9 %collective-permute-start.19 = (bf16[2048,384]{1,0:T(8,128)(2,1)S(1)}, bf16[2048,384]{1,0:T(8,128)(2,1)S(1)}, u32[]{:S(2)}, u32[]{:S(2)}) collective-permute-start(bf16[2048,384]{1,0:T(8,128)(2,1)S(1)} %copy-done.14), channel_id=1, source_target_pairs={{0,1},{1,0},{2,3},{3,2},{4,5},{5,4},{6,7},{7,6},{8,9},{9,8},{10,11... | collective-permute-start | bytes 4718600 | tf_op jit(solution)/shard_map/ppermute | solution.py:51
  73.8 21.6 %collective-permute-start.24 = (bf16[2,256,384]{2,1,0:T(8,128)(2,1)S(1)}, bf16[2,256,384]{2,1,0:T(8,128)(2,1)S(1)}, u32[]{:S(2)}, u32[]{:S(2)}) collective-permute-start(bf16[2,256,384]{2,1,0:T(8,128)(2,1)S(1)} %get-tuple-element.170), channel_id=1, source_target_pairs={{0,96},{16,112},{32,0},{48,16},{64,32},{80,48},{96,64},{112,80},{1... | collective-permute-start | bytes 1179656 | tf_op jit(solution)/shard_map/ppermute | solution.py:55
  78.9 16.5 %collective-permute-start.23 = (bf16[2,256,384]{2,1,0:T(8,128)(2,1)S(1)}, bf16[2,256,384]{2,1,0:T(8,128)(2,1)S(1)}, u32[]{:S(2)}, u32[]{:S(2)}) collective-permute-start(bf16[2,256,384]{2,1,0:T(8,128)(2,1)S(1)} %get-tuple-element.171), channel_id=1, source_target_pairs={{0,32},{16,48},{32,64},{48,80},{64,96},{80,112},{96,0},{112,16},{1... | collective-permute-start | bytes 1179656 | tf_op jit(solution)/shard_map/ppermute | solution.py:55
  80.9 18.6 %collective-permute-start.22 = (bf16[2,256,384]{2,1,0:T(8,128)(2,1)S(1)}, bf16[2,256,384]{2,1,0:T(8,128)(2,1)S(1)}, u32[]{:S(2)}, u32[]{:S(2)}) collective-permute-start(bf16[2,256,384]{2,1,0:T(8,128)(2,1)S(1)} %get-tuple-element.172), channel_id=1, source_target_pairs={{0,64},{16,80},{32,96},{48,112},{64,0},{80,16},{96,32},{112,48},{1... | collective-permute-start | bytes 1179656 | tf_op jit(solution)/shard_map/ppermute | solution.py:55
  84.5 15.0 %collective-permute-start.20 = (bf16[128,2048]{1,0:T(8,128)(2,1)S(1)}, bf16[128,2048]{1,0:T(8,128)(2,1)S(1)}, u32[]{:S(2)}, u32[]{:S(2)}) collective-permute-start(bf16[128,2048]{1,0:T(8,128)(2,1)S(1)} %collective-permute-done.13.refs_4_), channel_id=1, source_target_pairs={{0,2},{1,3},{2,4},{3,5},{4,6},{5,7},{6,0},{7,1},{8,10},{9,11},{10,... | collective-permute-start | bytes 1572872 | tf_op jit(solution)/shard_map/ppermute | solution.py:51
  84.5 15.0 %collective-permute-start.21 = (bf16[128,2048]{1,0:T(8,128)(2,1)S(1)}, bf16[128,2048]{1,0:T(8,128)(2,1)S(1)}, u32[]{:S(2)}, u32[]{:S(2)}) collective-permute-start(bf16[128,2048]{1,0:T(8,128)(2,1)S(1)} %collective-permute-done.16.refs_5_), channel_id=1, source_target_pairs={{0,6},{1,7},{2,0},{3,1},{4,2},{5,3},{6,4},{7,5},{8,14},{9,15},{10,... | collective-permute-start | bytes 1572872 | tf_op jit(solution)/shard_map/ppermute | solution.py:51
  101.9 2.4 %collective-permute-start.25 = (bf16[2,256,768]{2,1,0:T(8,128)(2,1)S(1)}, bf16[2,256,768]{2,1,0:T(8,128)(2,1)S(1)}, u32[]{:S(2)}, u32[]{:S(2)}) collective-permute-start(bf16[2,256,768]{2,1,0:T(8,128)(2,1)S(1)} %get-tuple-element.123), channel_id=1, source_target_pairs={{0,1},{1,0},{2,3},{3,2},{4,5},{5,4},{6,7},{7,6},{8,9},{9,8},{10,11... | collective-permute-start | bytes 2359304 | tf_op jit(solution)/shard_map/ppermute | solution.py:51
  102.0 14.3 %collective-permute-start.32 = (bf16[128,2048]{1,0:T(8,128)(2,1)S(1)}, bf16[128,2048]{1,0:T(8,128)(2,1)S(1)}, u32[]{:S(2)}, u32[]{:S(2)}) collective-permute-start(bf16[128,2048]{1,0:T(8,128)(2,1)S(1)} %get-tuple-element.147), channel_id=1, source_target_pairs={{0,6},{1,7},{2,0},{3,1},{4,2},{5,3},{6,4},{7,5},{8,14},{9,15},{10,... | collective-permute-start | bytes 1572872 | tf_op jit(solution)/shard_map/ppermute | solution.py:51
  103.8 15.2 %collective-permute-start.31 = (bf16[128,2048]{1,0:T(8,128)(2,1)S(1)}, bf16[128,2048]{1,0:T(8,128)(2,1)S(1)}, u32[]{:S(2)}, u32[]{:S(2)}) collective-permute-start(bf16[128,2048]{1,0:T(8,128)(2,1)S(1)} %get-tuple-element.145), channel_id=1, source_target_pairs={{0,2},{1,3},{2,4},{3,5},{4,6},{5,7},{6,0},{7,1},{8,10},{9,11},{10,... | collective-permute-start | bytes 1572872 | tf_op jit(solution)/shard_map/ppermute | solution.py:51
  104.5 17.9 %collective-permute-start.27 = (bf16[256,768]{1,0:T(8,128)(2,1)S(1)}, bf16[256,768]{1,0:T(8,128)(2,1)S(1)}, u32[]{:S(2)}, u32[]{:S(2)}) collective-permute-start(bf16[256,768]{1,0:T(8,128)(2,1)S(1)} %get-tuple-element.175), channel_id=1, source_target_pairs={{0,96},{16,112},{32,0},{48,16},{64,32},{80,48},{96,64},{112,80},{1... | collective-permute-start | bytes 1179656 | tf_op jit(solution)/shard_map/ppermute | solution.py:55
  104.6 17.8 %collective-permute-start.26 = (bf16[256,768]{1,0:T(8,128)(2,1)S(1)}, bf16[256,768]{1,0:T(8,128)(2,1)S(1)}, u32[]{:S(2)}, u32[]{:S(2)}) collective-permute-start(bf16[256,768]{1,0:T(8,128)(2,1)S(1)} %get-tuple-element.176), channel_id=1, source_target_pairs={{0,32},{16,48},{32,64},{48,80},{64,96},{80,112},{96,0},{112,16},{1... | collective-permute-start | bytes 1179656 | tf_op jit(solution)/shard_map/ppermute | solution.py:55
  119.1 14.4 %collective-permute-start.33 = (bf16[128,2048]{1,0:T(8,128)(2,1)S(1)}, bf16[128,2048]{1,0:T(8,128)(2,1)S(1)}, u32[]{:S(2)}, u32[]{:S(2)}) collective-permute-start(bf16[128,2048]{1,0:T(8,128)(2,1)S(1)} %add_convert_fusion.3), channel_id=1, source_target_pairs={{0,2},{1,3},{2,4},{3,5},{4,6},{5,7},{6,0},{7,1},{8,10},{9,11},{10,... | collective-permute-start | bytes 1572872 | tf_op jit(solution)/shard_map/ppermute | solution.py:51
  119.2 14.4 %collective-permute-start.34 = (bf16[128,2048]{1,0:T(8,128)(2,1)S(1)}, bf16[128,2048]{1,0:T(8,128)(2,1)S(1)}, u32[]{:S(2)}, u32[]{:S(2)}) collective-permute-start(bf16[128,2048]{1,0:T(8,128)(2,1)S(1)} %get-tuple-element.150), channel_id=1, source_target_pairs={{0,6},{1,7},{2,0},{3,1},{4,2},{5,3},{6,4},{7,5},{8,14},{9,15},{10,... | collective-permute-start | bytes 1572872 | tf_op jit(solution)/shard_map/ppermute | solution.py:51
  122.4 11.1 %collective-permute-start.28 = (bf16[4,256,768]{2,1,0:T(8,128)(2,1)S(1)}, bf16[4,256,768]{2,1,0:T(8,128)(2,1)S(1)}, u32[]{:S(2)}, u32[]{:S(2)}) collective-permute-start(bf16[4,256,768]{2,1,0:T(8,128)(2,1)S(1)} %get-tuple-element.130), channel_id=1, source_target_pairs={{0,1},{1,0},{2,3},{3,2},{4,5},{5,4},{6,7},{7,6},{8,9},{9,8},{10,11... | collective-permute-start | bytes 4718600 | tf_op jit(solution)/shard_map/ppermute | solution.py:51
  124.8 15.9 %collective-permute-start.37 = (bf16[2,256,768]{2,1,0:T(8,128)(2,1)S(1)}, bf16[2,256,768]{2,1,0:T(8,128)(2,1)S(1)}, u32[]{:S(2)}, u32[]{:S(2)}) collective-permute-start(bf16[2,256,768]{2,1,0:T(8,128)(2,1)S(1)} %get-tuple-element.157), channel_id=1, source_target_pairs={{0,1},{1,0},{2,3},{3,2},{4,5},{5,4},{6,7},{7,6},{8,9},{9,8},{10,11... | collective-permute-start | bytes 2359304 | tf_op jit(solution)/shard_map/ppermute | solution.py:51
  134.2 19.1 %collective-permute-start.29 = (bf16[2,256,768]{2,1,0:T(8,128)(2,1)S(1)}, bf16[2,256,768]{2,1,0:T(8,128)(2,1)S(1)}, u32[]{:S(2)}, u32[]{:S(2)}) collective-permute-start(bf16[2,256,768]{2,1,0:T(8,128)(2,1)S(1)} %get-tuple-element.140), channel_id=1, source_target_pairs={{0,32},{16,48},{32,64},{48,80},{64,96},{80,112},{96,0},{112,16},{1... | collective-permute-start | bytes 2359304 | tf_op jit(solution)/shard_map/ppermute | solution.py:55
  134.3 19.1 %collective-permute-start.30 = (bf16[2,256,768]{2,1,0:T(8,128)(2,1)S(1)}, bf16[2,256,768]{2,1,0:T(8,128)(2,1)S(1)}, u32[]{:S(2)}, u32[]{:S(2)}) collective-permute-start(bf16[2,256,768]{2,1,0:T(8,128)(2,1)S(1)} %get-tuple-element.141), channel_id=1, source_target_pairs={{0,96},{16,112},{32,0},{48,16},{64,32},{80,48},{96,64},{112,80},{1... | collective-permute-start | bytes 2359304 | tf_op jit(solution)/shard_map/ppermute | solution.py:55
  137.7 11.9 %collective-permute-start.35 = (bf16[128,2048]{1,0:T(8,128)(2,1)S(1)}, bf16[128,2048]{1,0:T(8,128)(2,1)S(1)}, u32[]{:S(2)}, u32[]{:S(2)}) collective-permute-start(bf16[128,2048]{1,0:T(8,128)(2,1)S(1)} %add_convert_fusion.2), channel_id=1, source_target_pairs={{0,6},{1,7},{2,0},{3,1},{4,2},{5,3},{6,4},{7,5},{8,14},{9,15},{10,... | collective-permute-start | bytes 1572872 | tf_op jit(solution)/shard_map/ppermute | solution.py:51
  140.7 12.3 %collective-permute-start.36 = (bf16[128,2048]{1,0:T(8,128)(2,1)S(1)}, bf16[128,2048]{1,0:T(8,128)(2,1)S(1)}, u32[]{:S(2)}, u32[]{:S(2)}) collective-permute-start(bf16[128,2048]{1,0:T(8,128)(2,1)S(1)} %get-tuple-element.153), channel_id=1, source_target_pairs={{0,2},{1,3},{2,4},{3,5},{4,6},{5,7},{6,0},{7,1},{8,10},{9,11},{10,... | collective-permute-start | bytes 1572872 | tf_op jit(solution)/shard_map/ppermute | solution.py:51
  140.9 16.7 %collective-permute-start.38 = (bf16[128,2048]{1,0:T(8,128)(2,1)S(1)}, bf16[128,2048]{1,0:T(8,128)(2,1)S(1)}, u32[]{:S(2)}, u32[]{:S(2)}) collective-permute-start(bf16[128,2048]{1,0:T(8,128)(2,1)S(1)} %add_convert_fusion.1), channel_id=1, source_target_pairs={{0,8},{1,9},{2,10},{3,11},{4,12},{5,13},{6,14},{7,15},{8,0},{9,1},... | collective-permute-start | bytes 1572872 | tf_op jit(solution)/shard_map/ppermute | solution.py:51
  153.6 9.3 %collective-permute-start.40 = (bf16[256,384]{1,0:T(8,128)(2,1)S(1)}, bf16[256,384]{1,0:T(8,128)(2,1)S(1)}, u32[]{:S(2)}, u32[]{:S(2)}) collective-permute-start(bf16[256,384]{1,0:T(8,128)(2,1)S(1)} %fusion.4), channel_id=1, source_target_pairs={{0,16},{16,0},{32,48},{48,32},{64,80},{80,64},{96,112},{112,96},{1... | collective-permute-start | bytes 589832 | tf_op jit(solution)/shard_map/ppermute | solution.py:55
  156.6 11.9 %collective-permute-start.39 = (bf16[256,768]{1,0:T(8,128)(2,1)S(1)}, bf16[256,768]{1,0:T(8,128)(2,1)S(1)}, u32[]{:S(2)}, u32[]{:S(2)}) collective-permute-start(bf16[256,768]{1,0:T(8,128)(2,1)S(1)} %fusion.1), channel_id=1, source_target_pairs={{0,16},{16,0},{32,48},{48,32},{64,80},{80,64},{96,112},{112,96},{1... | collective-permute-start | bytes 1179656 | tf_op jit(solution)/shard_map/ppermute | solution.py:55

commit v4 on v3

--- a/solution.py
+++ b/solution.py
@@ -60,7 +60,7 @@
 
 
 def params():
-    return pltpu.CompilerParams(vmem_limit_bytes=24 << 20)
+    return pltpu.CompilerParams(vmem_limit_bytes=20 << 20)
 
 
 def cost(effort, flops, moved):

time: 170 us -> 170 us (level)
  no operation moved by 1% of the time
where the time goes in v4:
time: 170 us
  waiting for transfers between devices  59.6 us (35%)
  starting transfers between devices  55.9 us (33%)
  Pallas kernels  33.3 us (20%)
  local copies, waits for them, and re-layouts  16.6 us (10%)
  other arithmetic  2.93 us (2%)
    ppermute x32, waiting for transfers between devices, tsend(): return lax.ppermute(value, 'tensor', pairs)  46.4 us
    ppermute x32, starting transfers between devices, tsend(): return lax.ppermute(value, 'tensor', pairs)  37.2 us
    ppermute x9, starting transfers between devices, dsend(): return lax.ppermute(value, 'dp', pairs)  18.8 us
    pallas_call x4, Pallas kernels, weight_call(): pl.pallas_call(lambda *refs: weight_body(count, wide, *refs), out_shape=(...  14.9 us
    ppermute x9, waiting for transfers between devices, dsend(): return lax.ppermute(value, 'dp', pairs)  13.1 us
    unnamed x47, local copies, waits for them, and re-layouts  12.1 us
    pallas_call x2, Pallas kernels, slope_call(): pl.pallas_call(lambda *refs: slope_body(first, count, *refs), out_shape=(...  8.3 us
    pallas_call x1, Pallas kernels, input_call(): pl.pallas_call(lambda *refs: input_body(parts, *refs), out_shape=[jax.Sha...  7.7 us
  transfers between devices with their start and end apart: 41, of which 16 were waited for; matrix products, arithmetic and copies ran while one was open for 4% of the time, Pallas kernels for 18%

profile of v4, /device:TPU:0, one launch (start us, length us, event | category | flops | bytes accessed | tf_op | source)
XLA Modules:
  0.0 169.5 jit_solution(14835535093609598941)
XLA Ops:
  0.7 0.5 collective-permute-start.4
  1.2 1.6 collective-permute-start.2
  2.8 1.7 collective-permute-start.1
  4.5 1.7 collective-permute-start
  6.1 10.4 %collective-permute-done.2.refs_4_ = bf16[128,2048]{1,0:T(8,128)(2,1)S(1)} collective-permute-done((bf16[128,2048]{1,0:T(8,128)(2,1)}, bf16[128,2048]{1,0:T(8,128)(2,1)S(1)}, u32[]{:S(2)}, u32[]{:S(2)}) %collective-permute-start.2) | collective-permute-done | bytes 524320 | tf_op jit(solution)/shard_map/ppermute | solution.py:51
  16.7 1.4 collective-permute-done.refs_2_
  18.0 1.2 copy-done.15
  19.3 0.7 dynamic-slice_bitcast_fusion
  20.0 0.7 dynamic-slice_bitcast_fusion.1
  21.2 2.9 %collective-permute-start.6 = (bf16[128,2048]{1,0:T(8,128)(2,1)}, bf16[128,2048]{1,0:T(8,128)(2,1)S(1)}, u32[]{:S(2)}, u32[]{:S(2)}) collective-permute-start(bf16[128,2048]{1,0:T(8,128)(2,1)} %copy-done.20), channel_id=1, source_target_pairs={{0,6},{1,7},{2,0},{3,1},{4,2},{5,3},{6,4},{7,5},{8,14},{9,15},{10,... | collective-permute-start | bytes 1572872 | tf_op jit(solution)/shard_map/ppermute | solution.py:51
  24.0 1.0 slice.45
  25.0 1.0 slice.46
  26.1 3.2 %collective-permute-start.8 = (bf16[64,2048]{1,0:T(8,128)(2,1)S(1)}, bf16[64,2048]{1,0:T(8,128)(2,1)S(1)}, u32[]{:S(2)}, u32[]{:S(2)}) collective-permute-start(bf16[64,2048]{1,0:T(8,128)(2,1)S(1)} %slice.45), channel_id=1, source_target_pairs={{0,6},{1,7},{2,0},{3,1},{4,2},{5,3},{6,4},{7,5},{8,14},{9,15},{10,... | collective-permute-start | bytes 786440 | tf_op jit(solution)/shard_map/ppermute | solution.py:51
  29.3 1.4 copy-done
  30.7 1.4 copy-done.2
  32.1 1.0 copy-done.6
  33.2 1.0 copy-done.9
  34.2 1.4 copy-done.11
  35.6 1.4 copy-done.16
  37.0 1.0 copy-done.18
  38.1 1.0 copy-done.21
  39.1 4.1 %slope.2 = (bf16[512,768]{1,0:T(8,128)(2,1)S(1)}, bf16[512,768]{1,0:T(8,128)(2,1)S(1)}) custom-call(s32[13]{0:T(128)S(1)} %pad_add_fusion.refs_0_.table_ref, bf16[128,2048]{1,0:T(8,128)(2,1)S(1)} %copy-done.18, bf16[128,2048]{1,0:T(8,128)(2,1)S(1)} %copy-done.21, bf16[128,2048]{1,0:T(8,128)(2,1)S(1)} %copy-done.9, bf16[128,2048]{1,0:T(8,128)(2,1)S(1)} %copy-done.6, ...), custom_call_target="tpu_custom_call" | custom-call | flops 6442450944 | bytes 33554432 | tf_op jit(solution)/shard_map/slope/pallas_call | solution.py:149
  43.3 1.8 %hidden.1.refs_11_ = bf16[1024,768]{1,0:T(8,128)(2,1)S(1)} custom-call(s32[13]{0:T(128)S(1)} %pad_add_fusion.refs_0_.table_ref, bf16[2048,384]{1,0:T(8,128)(2,1)S(1)} %copy-done.1, bf16[2048,384]{1,0:T(8,128)(2,1)S(1)} %collective-permute-done.4.refs_8_.refs_1_.refs_10_, bf16[2048,384]{1,0:T(8,128)(2,1)S(1)} %copy-done.2, ...), custom_call_target="tpu_custom_call" | custom-call | flops 12582912 | bytes 4718592 | tf_op jit(solution)/shard_map/hidden/pallas_call | solution.py:81
  45.3 3.2 %collective-permute-start.10 = (bf16[64,2048]{1,0:T(8,128)(2,1)S(1)}, bf16[64,2048]{1,0:T(8,128)(2,1)S(1)}, u32[]{:S(2)}, u32[]{:S(2)}) collective-permute-start(bf16[64,2048]{1,0:T(8,128)(2,1)S(1)} %slice.47), channel_id=1, source_target_pairs={{0,6},{1,7},{2,0},{3,1},{4,2},{5,3},{6,4},{7,5},{8,14},{9,15},{10,... | collective-permute-start | bytes 786440 | tf_op jit(solution)/shard_map/ppermute | solution.py:51
  48.5 1.7 collective-permute-start.14
  50.2 3.2 %collective-permute-start.12 = (bf16[128,2048]{1,0:T(8,128)(2,1)S(1)}, bf16[128,2048]{1,0:T(8,128)(2,1)S(1)}, u32[]{:S(2)}, u32[]{:S(2)}) collective-permute-start(bf16[128,2048]{1,0:T(8,128)(2,1)S(1)} %copy-done.4), channel_id=1, source_target_pairs={{0,6},{1,7},{2,0},{3,1},{4,2},{5,3},{6,4},{7,5},{8,14},{9,15},{10,... | collective-permute-start | bytes 1572872 | tf_op jit(solution)/shard_map/ppermute | solution.py:51
  53.4 2.1 %collective-permute-done.11.refs_10_.refs_6_ = bf16[64,2048]{1,0:T(8,128)(2,1)S(1)} collective-permute-done((bf16[64,2048]{1,0:T(8,128)(2,1)S(1)}, bf16[64,2048]{1,0:T(8,128)(2,1)S(1)}, u32[]{:S(2)}, u32[]{:S(2)}) %collective-permute-start.11) | collective-permute-done | bytes 262176 | tf_op jit(solution)/shard_map/ppermute | solution.py:51
  55.6 5.5 %weight.4 = (f32[8,256,384]{2,1,0:T(8,128)S(1)}, bf16[8,256,384]{2,1,0:T(8,128)(2,1)S(1)}) custom-call(s32[13]{0:T(128)S(1)} %pad_add_fusion.refs_0_.table_ref, bf16[128,2048]{1,0:T(8,128)(2,1)S(1)} %copy-done.19, bf16[128,2048]{1,0:T(8,128)(2,1)S(1)} %copy-done.22, bf16[128,2048]{1,0:T(8,128)(2,1)S(1)} %copy-done.10, bf16[128,2048]{1,0:T(8,128)(2,1)S(1)} %copy-done.7, ...), custom_call_target="tpu_custom_call" | custom-call | flops 38654705664 | bytes 125829120 | tf_op jit(solution)/shard_map/weight/pallas_call | solution.py:204
  61.2 4.1 %collective-permute-done.13.refs_4_ = bf16[128,2048]{1,0:T(8,128)(2,1)S(1)} collective-permute-done((bf16[128,2048]{1,0:T(8,128)(2,1)S(1)}, bf16[128,2048]{1,0:T(8,128)(2,1)S(1)}, u32[]{:S(2)}, u32[]{:S(2)}) %collective-permute-start.13) | collective-permute-done | bytes 524320 | tf_op jit(solution)/shard_map/ppermute | solution.py:51
  65.3 3.2 %collective-permute-start.16 = (bf16[128,2048]{1,0:T(8,128)(2,1)S(1)}, bf16[128,2048]{1,0:T(8,128)(2,1)S(1)}, u32[]{:S(2)}, u32[]{:S(2)}) collective-permute-start(bf16[128,2048]{1,0:T(8,128)(2,1)S(1)} %collective-permute-done.14.refs_2_), channel_id=1, source_target_pairs={{0,6},{1,7},{2,0},{3,1},{4,2},{5,3},{6,4},{7,5},{8,14},{9,15},{10,... | collective-permute-start | bytes 1572872 | tf_op jit(solution)/shard_map/ppermute | solution.py:51
  68.5 0.5 collective-permute-start.19
  69.0 4.2 %slope.3 = (bf16[512,768]{1,0:T(8,128)(2,1)S(1)}, bf16[512,768]{1,0:T(8,128)(2,1)S(1)}) custom-call(s32[13]{0:T(128)S(1)} %pad_add_fusion.refs_0_.table_ref, bf16[128,2048]{1,0:T(8,128)(2,1)S(1)} %collective-permute-done.6.refs_5_.refs_1_, bf16[128,2048]{1,0:T(8,128)(2,1)S(1)} %collective-permute-done.7.refs_6_.refs_2_, ...), custom_call_target="tpu_custom_call" | custom-call | flops 19327352832 | bytes 100663296 | tf_op jit(solution)/shard_map/slope/pallas_call | solution.py:149
  73.2 0.4 fusion.5
  73.8 4.2 %collective-permute-start.24 = (bf16[2,256,384]{2,1,0:T(8,128)(2,1)S(1)}, bf16[2,256,384]{2,1,0:T(8,128)(2,1)S(1)}, u32[]{:S(2)}, u32[]{:S(2)}) collective-permute-start(bf16[2,256,384]{2,1,0:T(8,128)(2,1)S(1)} %get-tuple-element.170), channel_id=1, source_target_pairs={{0,96},{16,112},{32,0},{48,16},{64,32},{80,48},{96,64},{112,80},{1... | collective-permute-start | bytes 1179656 | tf_op jit(solution)/shard_map/ppermute | solution.py:55
  78.0 1.0 collective-permute-done.17.refs_6_
  78.9 1.9 %collective-permute-start.23 = (bf16[2,256,384]{2,1,0:T(8,128)(2,1)S(1)}, bf16[2,256,384]{2,1,0:T(8,128)(2,1)S(1)}, u32[]{:S(2)}, u32[]{:S(2)}) collective-permute-start(bf16[2,256,384]{2,1,0:T(8,128)(2,1)S(1)} %get-tuple-element.171), channel_id=1, source_target_pairs={{0,32},{16,48},{32,64},{48,80},{64,96},{80,112},{96,0},{112,16},{1... | collective-permute-start | bytes 1179656 | tf_op jit(solution)/shard_map/ppermute | solution.py:55
  80.9 3.6 %collective-permute-start.22 = (bf16[2,256,384]{2,1,0:T(8,128)(2,1)S(1)}, bf16[2,256,384]{2,1,0:T(8,128)(2,1)S(1)}, u32[]{:S(2)}, u32[]{:S(2)}) collective-permute-start(bf16[2,256,384]{2,1,0:T(8,128)(2,1)S(1)} %get-tuple-element.172), channel_id=1, source_target_pairs={{0,64},{16,80},{32,96},{48,112},{64,0},{80,16},{96,32},{112,48},{1... | collective-permute-start | bytes 1179656 | tf_op jit(solution)/shard_map/ppermute | solution.py:55
  84.5 3.2 %collective-permute-start.21 = (bf16[128,2048]{1,0:T(8,128)(2,1)S(1)}, bf16[128,2048]{1,0:T(8,128)(2,1)S(1)}, u32[]{:S(2)}, u32[]{:S(2)}) collective-permute-start(bf16[128,2048]{1,0:T(8,128)(2,1)S(1)} %collective-permute-done.16.refs_5_), channel_id=1, source_target_pairs={{0,6},{1,7},{2,0},{3,1},{4,2},{5,3},{6,4},{7,5},{8,14},{9,15},{10,... | collective-permute-start | bytes 1572872 | tf_op jit(solution)/shard_map/ppermute | solution.py:51
  87.7 7.7 %input.1 = (f32[128,2048]{1,0:T(8,128)S(1)}, f32[128,2048]{1,0:T(8,128)S(1)}, bf16[128,2048]{1,0:T(8,128)(2,1)S(1)}, f32[128,2048]{1,0:T(8,128)S(1)}, f32[128,20...) custom-call(bf16[512,768]{1,0:T(8,128)(2,1)S(1)} %get-tuple-element., ...), custom_call_target="tpu_custom_call" | custom-call | flops 77309411328 | bytes 176160768 | tf_op jit(solution)/shard_map/input/pallas_call | solution.py:276
  95.4 4.1 %collective-permute-done.22 = bf16[2,256,384]{2,1,0:T(8,128)(2,1)S(1)} collective-permute-done((bf16[2,256,384]{2,1,0:T(8,128)(2,1)S(1)}, bf16[2,256,384]{2,1,0:T(8,128)(2,1)S(1)}, u32[]{:S(2)}, u32[]{:S(2)}) %collective-permute-start.22) | collective-permute-done | bytes 393248 | tf_op jit(solution)/shard_map/ppermute | solution.py:55
  99.5 2.4 %weight.5 = (f32[2,256,768]{2,1,0:T(8,128)S(1)}, bf16[2,256,768]{2,1,0:T(8,128)(2,1)S(1)}) custom-call(s32[13]{0:T(128)S(1)} %pad_add_fusion.refs_0_.table_ref, bf16[128,2048]{1,0:T(8,128)(2,1)S(1)} %copy-done.4, bf16[128,2048]{1,0:T(8,128)(2,1)S(1)} %collective-permute-done.14.refs_2_, bf16[128,2048]{1,0:T(8,128)(2,1)S(1)} %collective-permute-done.12.refs_3_, ...), custom_call_target="tpu_custom_call" | custom-call | flops 161061280 | bytes 1048576 | tf_op jit(solution)/shard_map/weight/pallas_call | solution.py:204
  102.0 1.8 %collective-permute-start.32 = (bf16[128,2048]{1,0:T(8,128)(2,1)S(1)}, bf16[128,2048]{1,0:T(8,128)(2,1)S(1)}, u32[]{:S(2)}, u32[]{:S(2)}) collective-permute-start(bf16[128,2048]{1,0:T(8,128)(2,1)S(1)} %get-tuple-element.147), channel_id=1, source_target_pairs={{0,6},{1,7},{2,0},{3,1},{4,2},{5,3},{6,4},{7,5},{8,14},{9,15},{10,... | collective-permute-start | bytes 1572872 | tf_op jit(solution)/shard_map/ppermute | solution.py:51
  104.6 2.0 %collective-permute-start.26 = (bf16[256,768]{1,0:T(8,128)(2,1)S(1)}, bf16[256,768]{1,0:T(8,128)(2,1)S(1)}, u32[]{:S(2)}, u32[]{:S(2)}) collective-permute-start(bf16[256,768]{1,0:T(8,128)(2,1)S(1)} %get-tuple-element.176), channel_id=1, source_target_pairs={{0,32},{16,48},{32,64},{48,80},{64,96},{80,112},{96,0},{112,16},{1... | collective-permute-start | bytes 1179656 | tf_op jit(solution)/shard_map/ppermute | solution.py:55
  106.6 4.6 %weight.6 = (f32[4,256,768]{2,1,0:T(8,128)S(1)}, bf16[4,256,768]{2,1,0:T(8,128)(2,1)S(1)}) custom-call(s32[13]{0:T(128)S(1)} %pad_add_fusion.refs_0_.table_ref, bf16[128,2048]{1,0:T(8,128)(2,1)S(1)} %copy-done.4, bf16[128,2048]{1,0:T(8,128)(2,1)S(1)} %collective-permute-done.14.refs_2_, bf16[128,2048]{1,0:T(8,128)(2,1)S(1)} %collective-permute-done.12.refs_3_, ...), custom_call_target="tpu_custom_call" | custom-call | flops 38654705664 | bytes 125829120 | tf_op jit(solution)/shard_map/weight/pallas_call | solution.py:204
  111.2 5.1 %collective-permute-done.32 = bf16[128,2048]{1,0:T(8,128)(2,1)S(1)} collective-permute-done((bf16[128,2048]{1,0:T(8,128)(2,1)S(1)}, bf16[128,2048]{1,0:T(8,128)(2,1)S(1)}, u32[]{:S(2)}, u32[]{:S(2)}) %collective-permute-start.32) | collective-permute-done | bytes 524320 | tf_op jit(solution)/shard_map/ppermute | solution.py:51
  116.3 2.7 %collective-permute-done.31 = bf16[128,2048]{1,0:T(8,128)(2,1)S(1)} collective-permute-done((bf16[128,2048]{1,0:T(8,128)(2,1)S(1)}, bf16[128,2048]{1,0:T(8,128)(2,1)S(1)}, u32[]{:S(2)}, u32[]{:S(2)}) %collective-permute-start.31) | collective-permute-done | bytes 524320 | tf_op jit(solution)/shard_map/ppermute | solution.py:51
  119.2 3.2 %collective-permute-start.34 = (bf16[128,2048]{1,0:T(8,128)(2,1)S(1)}, bf16[128,2048]{1,0:T(8,128)(2,1)S(1)}, u32[]{:S(2)}, u32[]{:S(2)}) collective-permute-start(bf16[128,2048]{1,0:T(8,128)(2,1)S(1)} %get-tuple-element.150), channel_id=1, source_target_pairs={{0,6},{1,7},{2,0},{3,1},{4,2},{5,3},{6,4},{7,5},{8,14},{9,15},{10,... | collective-permute-start | bytes 1572872 | tf_op jit(solution)/shard_map/ppermute | solution.py:51
  122.4 2.4 %weight.7 = (f32[2,256,768]{2,1,0:T(8,128)S(1)}, bf16[2,256,768]{2,1,0:T(8,128)(2,1)S(1)}) custom-call(s32[13]{0:T(128)S(1)} %pad_add_fusion.refs_0_.table_ref, bf16[128,2048]{1,0:T(8,128)(2,1)S(1)} %copy-done.4, bf16[128,2048]{1,0:T(8,128)(2,1)S(1)} %collective-permute-done.14.refs_2_, bf16[128,2048]{1,0:T(8,128)(2,1)S(1)} %collective-permute-done.12.refs_3_, ...), custom_call_target="tpu_custom_call" | custom-call | flops 19327352832 | bytes 125829120 | tf_op jit(solution)/shard_map/weight/pallas_call | solution.py:204
  124.8 0.6 collective-permute-start.37
  125.4 8.1 %collective-permute-done.33 = bf16[128,2048]{1,0:T(8,128)(2,1)S(1)} collective-permute-done((bf16[128,2048]{1,0:T(8,128)(2,1)S(1)}, bf16[128,2048]{1,0:T(8,128)(2,1)S(1)}, u32[]{:S(2)}, u32[]{:S(2)}) %collective-permute-start.33) | collective-permute-done | bytes 524320 | tf_op jit(solution)/shard_map/ppermute | solution.py:51
  133.5 0.7 ring.1
  134.3 3.2 %collective-permute-start.30 = (bf16[2,256,768]{2,1,0:T(8,128)(2,1)S(1)}, bf16[2,256,768]{2,1,0:T(8,128)(2,1)S(1)}, u32[]{:S(2)}, u32[]{:S(2)}) collective-permute-start(bf16[2,256,768]{2,1,0:T(8,128)(2,1)S(1)} %get-tuple-element.141), channel_id=1, source_target_pairs={{0,96},{16,112},{32,0},{48,16},{64,32},{80,48},{96,64},{112,80},{1... | collective-permute-start | bytes 2359304 | tf_op jit(solution)/shard_map/ppermute | solution.py:55
  137.7 3.0 %collective-permute-start.35 = (bf16[128,2048]{1,0:T(8,128)(2,1)S(1)}, bf16[128,2048]{1,0:T(8,128)(2,1)S(1)}, u32[]{:S(2)}, u32[]{:S(2)}) collective-permute-start(bf16[128,2048]{1,0:T(8,128)(2,1)S(1)} %add_convert_fusion.2), channel_id=1, source_target_pairs={{0,6},{1,7},{2,0},{3,1},{4,2},{5,3},{6,4},{7,5},{8,14},{9,15},{10,... | collective-permute-start | bytes 1572872 | tf_op jit(solution)/shard_map/ppermute | solution.py:51
  140.9 0.8 collective-permute-start.38
  141.8 7.8 %collective-permute-done.35 = bf16[128,2048]{1,0:T(8,128)(2,1)S(1)} collective-permute-done((bf16[128,2048]{1,0:T(8,128)(2,1)S(1)}, bf16[128,2048]{1,0:T(8,128)(2,1)S(1)}, u32[]{:S(2)}, u32[]{:S(2)}) %collective-permute-start.35) | collective-permute-done | bytes 524320 | tf_op jit(solution)/shard_map/ppermute | solution.py:51
  149.6 3.4 %collective-permute-done.36 = bf16[128,2048]{1,0:T(8,128)(2,1)S(1)} collective-permute-done((bf16[128,2048]{1,0:T(8,128)(2,1)S(1)}, bf16[128,2048]{1,0:T(8,128)(2,1)S(1)}, u32[]{:S(2)}, u32[]{:S(2)}) %collective-permute-start.36) | collective-permute-done | bytes 524320 | tf_op jit(solution)/shard_map/ppermute | solution.py:51
  153.0 0.4 collective-permute-done.29
  153.6 2.7 %collective-permute-start.40 = (bf16[256,384]{1,0:T(8,128)(2,1)S(1)}, bf16[256,384]{1,0:T(8,128)(2,1)S(1)}, u32[]{:S(2)}, u32[]{:S(2)}) collective-permute-start(bf16[256,384]{1,0:T(8,128)(2,1)S(1)} %fusion.4), channel_id=1, source_target_pairs={{0,16},{16,0},{32,48},{48,32},{64,80},{80,64},{96,112},{112,96},{1... | collective-permute-start | bytes 589832 | tf_op jit(solution)/shard_map/ppermute | solution.py:55
  156.6 1.0 collective-permute-start.39
  157.6 1.2 convert_add_fusion.2
  158.9 4.0 %collective-permute-done.40 = bf16[256,384]{1,0:T(8,128)(2,1)S(1)} collective-permute-done((bf16[256,384]{1,0:T(8,128)(2,1)S(1)}, bf16[256,384]{1,0:T(8,128)(2,1)S(1)}, u32[]{:S(2)}, u32[]{:S(2)}) %collective-permute-start.40) | collective-permute-done | bytes 196640 | tf_op jit(solution)/shard_map/ppermute | solution.py:55
  162.9 0.9 copy.13
  163.9 4.7 %collective-permute-done.39 = bf16[256,768]{1,0:T(8,128)(2,1)S(1)} collective-permute-done((bf16[256,768]{1,0:T(8,128)(2,1)S(1)}, bf16[256,768]{1,0:T(8,128)(2,1)S(1)}, u32[]{:S(2)}, u32[]{:S(2)}) %collective-permute-start.39) | collective-permute-done | bytes 393248 | tf_op jit(solution)/shard_map/ppermute | solution.py:55
  168.6 0.9 fusion.7
  (97 shorter events, 3.4 us)
Async XLA Ops:
  0.6 17.4 %collective-permute-start.3 = (bf16[384,2048]{1,0:T(8,128)(2,1)}, bf16[384,2048]{1,0:T(8,128)(2,1)S(1)}, u32[]{:S(2)}, u32[]{:S(2)}) collective-permute-start(bf16[384,2048]{1,0:T(8,128)(2,1)} %refs_7_.2), channel_id=1, source_target_pairs={{0,1},{1,0},{2,3},{3,2},{4,5},{5,4},{6,7},{7,6},{8,9},{9,8},{10,11... | collective-permute-start | bytes 4718600 | tf_op jit(solution)/shard_map/ppermute | solution.py:51
  0.7 18.5 %collective-permute-start.4 = (bf16[2048,384]{1,0:T(8,128)(2,1)}, bf16[2048,384]{1,0:T(8,128)(2,1)S(1)}, u32[]{:S(2)}, u32[]{:S(2)}) collective-permute-start(bf16[2048,384]{1,0:T(8,128)(2,1)} %refs_9_.2), channel_id=1, source_target_pairs={{0,1},{1,0},{2,3},{3,2},{4,5},{5,4},{6,7},{7,6},{8,9},{9,8},{10,11... | collective-permute-start | bytes 4718600 | tf_op jit(solution)/shard_map/ppermute | solution.py:51
  1.2 15.3 %collective-permute-start.2 = (bf16[128,2048]{1,0:T(8,128)(2,1)}, bf16[128,2048]{1,0:T(8,128)(2,1)S(1)}, u32[]{:S(2)}, u32[]{:S(2)}) collective-permute-start(bf16[128,2048]{1,0:T(8,128)(2,1)} %refs_1_.3), channel_id=1, source_target_pairs={{0,2},{1,3},{2,4},{3,5},{4,6},{5,7},{6,0},{7,1},{8,10},{9,11},{10,... | collective-permute-start | bytes 1572872 | tf_op jit(solution)/shard_map/ppermute | solution.py:51
  2.8 13.9 %collective-permute-start.1 = (bf16[128,2048]{1,0:T(8,128)(2,1)}, bf16[128,2048]{1,0:T(8,128)(2,1)S(1)}, u32[]{:S(2)}, u32[]{:S(2)}) collective-permute-start(bf16[128,2048]{1,0:T(8,128)(2,1)} %refs_1_.3), channel_id=1, source_target_pairs={{0,6},{1,7},{2,0},{3,1},{4,2},{5,3},{6,4},{7,5},{8,14},{9,15},{10,... | collective-permute-start | bytes 1572872 | tf_op jit(solution)/shard_map/ppermute | solution.py:51
  4.5 13.6 %collective-permute-start = (bf16[128,2048]{1,0:T(8,128)(2,1)}, bf16[128,2048]{1,0:T(8,128)(2,1)S(1)}, u32[]{:S(2)}, u32[]{:S(2)}) collective-permute-start(bf16[128,2048]{1,0:T(8,128)(2,1)} %refs_1_.3), channel_id=1, source_target_pairs={{0,8},{1,9},{2,10},{3,11},{4,12},{5,13},{6,14},{7,15},{8,0},{9,1},... | collective-permute-start | bytes 1572872 | tf_op jit(solution)/shard_map/ppermute | solution.py:51
  16.6 2.7 %copy-start.5 = (bf16[128,2048]{1,0:T(8,128)(2,1)}, bf16[128,2048]{1,0:T(8,128)(2,1)S(1)}, u32[]{:S(2)}) copy-start(bf16[128,2048]{1,0:T(8,128)(2,1)S(1)} %collective-permute-done.2.refs_4_) | copy-start | bytes 1572868
  16.6 2.6 %copy-start.8 = (bf16[128,2048]{1,0:T(8,128)(2,1)}, bf16[128,2048]{1,0:T(8,128)(2,1)S(1)}, u32[]{:S(2)}) copy-start(bf16[128,2048]{1,0:T(8,128)(2,1)S(1)} %collective-permute-done.1.refs_3_) | copy-start | bytes 1572868
  18.0 1.3 copy-start.20
  18.0 1.2 copy-start.15
  19.2 10.0 %collective-permute-start.5 = (bf16[2048,384]{1,0:T(8,128)(2,1)}, bf16[2048,384]{1,0:T(8,128)(2,1)S(1)}, u32[]{:S(2)}, u32[]{:S(2)}) collective-permute-start(bf16[2048,384]{1,0:T(8,128)(2,1)} %refs_11_), channel_id=1, source_target_pairs={{0,1},{1,0},{2,3},{3,2},{4,5},{5,4},{6,7},{7,6},{8,9},{9,8},{10,11... | collective-permute-start | bytes 4718600 | tf_op jit(solution)/shard_map/ppermute | solution.py:51
  20.8 24.3 %collective-permute-start.7 = (bf16[128,2048]{1,0:T(8,128)(2,1)}, bf16[128,2048]{1,0:T(8,128)(2,1)S(1)}, u32[]{:S(2)}, u32[]{:S(2)}) collective-permute-start(bf16[128,2048]{1,0:T(8,128)(2,1)} %copy-done.20), channel_id=1, source_target_pairs={{0,2},{1,3},{2,4},{3,5},{4,6},{5,7},{6,0},{7,1},{8,10},{9,11},{10,... | collective-permute-start | bytes 1572872 | tf_op jit(solution)/shard_map/ppermute | solution.py:51
  21.2 23.9 %collective-permute-start.6 = (bf16[128,2048]{1,0:T(8,128)(2,1)}, bf16[128,2048]{1,0:T(8,128)(2,1)S(1)}, u32[]{:S(2)}, u32[]{:S(2)}) collective-permute-start(bf16[128,2048]{1,0:T(8,128)(2,1)} %copy-done.20), channel_id=1, source_target_pairs={{0,6},{1,7},{2,0},{3,1},{4,2},{5,3},{6,4},{7,5},{8,14},{9,15},{10,... | collective-permute-start | bytes 1572872 | tf_op jit(solution)/shard_map/ppermute | solution.py:51
  26.0 19.1 %collective-permute-start.9 = (bf16[64,2048]{1,0:T(8,128)(2,1)S(1)}, bf16[64,2048]{1,0:T(8,128)(2,1)S(1)}, u32[]{:S(2)}, u32[]{:S(2)}) collective-permute-start(bf16[64,2048]{1,0:T(8,128)(2,1)S(1)} %slice.46), channel_id=1, source_target_pairs={{0,2},{1,3},{2,4},{3,5},{4,6},{5,7},{6,0},{7,1},{8,10},{9,11},{10,... | collective-permute-start | bytes 786440 | tf_op jit(solution)/shard_map/ppermute | solution.py:51
  26.1 19.0 %collective-permute-start.8 = (bf16[64,2048]{1,0:T(8,128)(2,1)S(1)}, bf16[64,2048]{1,0:T(8,128)(2,1)S(1)}, u32[]{:S(2)}, u32[]{:S(2)}) collective-permute-start(bf16[64,2048]{1,0:T(8,128)(2,1)S(1)} %slice.45), channel_id=1, source_target_pairs={{0,6},{1,7},{2,0},{3,1},{4,2},{5,3},{6,4},{7,5},{8,14},{9,15},{10,... | collective-permute-start | bytes 786440 | tf_op jit(solution)/shard_map/ppermute | solution.py:51
  29.3 1.4 copy-start
  30.7 1.4 copy-start.2
  32.1 1.0 copy-start.6
  33.2 1.0 copy-start.9
  34.2 1.4 copy-start.11
  35.6 1.4 copy-start.16
  37.0 1.0 copy-start.18
  38.1 1.0 copy-start.21
  39.1 4.1 %copy-start.1 = (bf16[2048,384]{1,0:T(8,128)(2,1)S(1)}, bf16[2048,384]{1,0:T(8,128)(2,1)}, u32[]{:S(2)}) copy-start(bf16[2048,384]{1,0:T(8,128)(2,1)} %refs_9_.2) | copy-start | bytes 4718596
  43.3 5.3 %copy-start.4 = (bf16[128,2048]{1,0:T(8,128)(2,1)S(1)}, bf16[128,2048]{1,0:T(8,128)(2,1)}, u32[]{:S(2)}) copy-start(bf16[128,2048]{1,0:T(8,128)(2,1)} %refs_1_.6) | copy-start | bytes 1572868
  43.3 12.3 %copy-start.7 = (bf16[128,2048]{1,0:T(8,128)(2,1)S(1)}, bf16[128,2048]{1,0:T(8,128)(2,1)}, u32[]{:S(2)}) copy-start(bf16[128,2048]{1,0:T(8,128)(2,1)} %copy-done.5) | copy-start | bytes 1572868
  43.3 12.3 %copy-start.10 = (bf16[128,2048]{1,0:T(8,128)(2,1)S(1)}, bf16[128,2048]{1,0:T(8,128)(2,1)}, u32[]{:S(2)}) copy-start(bf16[128,2048]{1,0:T(8,128)(2,1)} %copy-done.8) | copy-start | bytes 1572868
  43.3 12.3 %copy-start.19 = (bf16[128,2048]{1,0:T(8,128)(2,1)S(1)}, bf16[128,2048]{1,0:T(8,128)(2,1)}, u32[]{:S(2)}) copy-start(bf16[128,2048]{1,0:T(8,128)(2,1)} %refs_1_.3) | copy-start | bytes 1572868
  43.3 12.3 %copy-start.22 = (bf16[128,2048]{1,0:T(8,128)(2,1)S(1)}, bf16[128,2048]{1,0:T(8,128)(2,1)}, u32[]{:S(2)}) copy-start(bf16[128,2048]{1,0:T(8,128)(2,1)} %copy-done.20) | copy-start | bytes 1572868
  45.2 23.3 %copy-start.13 = (bf16[2048,384]{1,0:T(8,128)(2,1)S(1)}, bf16[2048,384]{1,0:T(8,128)(2,1)}, u32[]{:S(2)}) copy-start(bf16[2048,384]{1,0:T(8,128)(2,1)} %refs_4_) | copy-start | bytes 4718596
  45.2 23.3 %copy-start.14 = (bf16[2048,384]{1,0:T(8,128)(2,1)S(1)}, bf16[2048,384]{1,0:T(8,128)(2,1)}, u32[]{:S(2)}) copy-start(bf16[2048,384]{1,0:T(8,128)(2,1)} %refs_6_) | copy-start | bytes 4718596
  45.2 23.8 %copy-start.3 = (bf16[2048,384]{1,0:T(8,128)(2,1)S(1)}, bf16[2048,384]{1,0:T(8,128)(2,1)}, u32[]{:S(2)}) copy-start(bf16[2048,384]{1,0:T(8,128)(2,1)} %refs_11_) | copy-start | bytes 4718596
  45.2 23.8 %copy-start.12 = (bf16[384,2048]{1,0:T(8,128)(2,1)S(1)}, bf16[384,2048]{1,0:T(8,128)(2,1)}, u32[]{:S(2)}) copy-start(bf16[384,2048]{1,0:T(8,128)(2,1)} %refs_7_.2) | copy-start | bytes 4718596
  45.2 23.8 %copy-start.17 = (bf16[384,2048]{1,0:T(8,128)(2,1)S(1)}, bf16[384,2048]{1,0:T(8,128)(2,1)}, u32[]{:S(2)}) copy-start(bf16[384,2048]{1,0:T(8,128)(2,1)} %copy-done.15) | copy-start | bytes 4718596
  45.2 10.3 %collective-permute-start.11 = (bf16[64,2048]{1,0:T(8,128)(2,1)S(1)}, bf16[64,2048]{1,0:T(8,128)(2,1)S(1)}, u32[]{:S(2)}, u32[]{:S(2)}) collective-permute-start(bf16[64,2048]{1,0:T(8,128)(2,1)S(1)} %slice.48), channel_id=1, source_target_pairs={{0,2},{1,3},{2,4},{3,5},{4,6},{5,7},{6,0},{7,1},{8,10},{9,11},{10,... | collective-permute-start | bytes 786440 | tf_op jit(solution)/shard_map/ppermute | solution.py:51
  45.3 10.2 %collective-permute-start.10 = (bf16[64,2048]{1,0:T(8,128)(2,1)S(1)}, bf16[64,2048]{1,0:T(8,128)(2,1)S(1)}, u32[]{:S(2)}, u32[]{:S(2)}) collective-permute-start(bf16[64,2048]{1,0:T(8,128)(2,1)S(1)} %slice.47), channel_id=1, source_target_pairs={{0,6},{1,7},{2,0},{3,1},{4,2},{5,3},{6,4},{7,5},{8,14},{9,15},{10,... | collective-permute-start | bytes 786440 | tf_op jit(solution)/shard_map/ppermute | solution.py:51
  48.5 12.6 %collective-permute-start.14 = (bf16[128,2048]{1,0:T(8,128)(2,1)S(1)}, bf16[128,2048]{1,0:T(8,128)(2,1)S(1)}, u32[]{:S(2)}, u32[]{:S(2)}) collective-permute-start(bf16[128,2048]{1,0:T(8,128)(2,1)S(1)} %copy-done.4), channel_id=1, source_target_pairs={{0,8},{1,9},{2,10},{3,11},{4,12},{5,13},{6,14},{7,15},{8,0},{9,1},... | collective-permute-start | bytes 1572872 | tf_op jit(solution)/shard_map/ppermute | solution.py:51
  50.2 15.1 %collective-permute-start.13 = (bf16[128,2048]{1,0:T(8,128)(2,1)S(1)}, bf16[128,2048]{1,0:T(8,128)(2,1)S(1)}, u32[]{:S(2)}, u32[]{:S(2)}) collective-permute-start(bf16[128,2048]{1,0:T(8,128)(2,1)S(1)} %copy-done.4), channel_id=1, source_target_pairs={{0,2},{1,3},{2,4},{3,5},{4,6},{5,7},{6,0},{7,1},{8,10},{9,11},{10,... | collective-permute-start | bytes 1572872 | tf_op jit(solution)/shard_map/ppermute | solution.py:51
  50.2 15.1 %collective-permute-start.12 = (bf16[128,2048]{1,0:T(8,128)(2,1)S(1)}, bf16[128,2048]{1,0:T(8,128)(2,1)S(1)}, u32[]{:S(2)}, u32[]{:S(2)}) collective-permute-start(bf16[128,2048]{1,0:T(8,128)(2,1)S(1)} %copy-done.4), channel_id=1, source_target_pairs={{0,6},{1,7},{2,0},{3,1},{4,2},{5,3},{6,4},{7,5},{8,14},{9,15},{10,... | collective-permute-start | bytes 1572872 | tf_op jit(solution)/shard_map/ppermute | solution.py:51
  61.1 12.2 %collective-permute-start.15 = (bf16[8,256,384]{2,1,0:T(8,128)(2,1)S(1)}, bf16[8,256,384]{2,1,0:T(8,128)(2,1)S(1)}, u32[]{:S(2)}, u32[]{:S(2)}) collective-permute-start(bf16[8,256,384]{2,1,0:T(8,128)(2,1)S(1)} %get-tuple-element.104), channel_id=1, source_target_pairs={{0,1},{1,0},{2,3},{3,2},{4,5},{5,4},{6,7},{7,6},{8,9},{9,8},{10,11... | collective-permute-start | bytes 4718600 | tf_op jit(solution)/shard_map/ppermute | solution.py:51
  65.3 13.7 %collective-permute-start.17 = (bf16[128,2048]{1,0:T(8,128)(2,1)S(1)}, bf16[128,2048]{1,0:T(8,128)(2,1)S(1)}, u32[]{:S(2)}, u32[]{:S(2)}) collective-permute-start(bf16[128,2048]{1,0:T(8,128)(2,1)S(1)} %collective-permute-done.14.refs_2_), channel_id=1, source_target_pairs={{0,2},{1,3},{2,4},{3,5},{4,6},{5,7},{6,0},{7,1},{8,10},{9,11},{10,... | collective-permute-start | bytes 1572872 | tf_op jit(solution)/shard_map/ppermute | solution.py:51
  65.3 15.6 %collective-permute-start.16 = (bf16[128,2048]{1,0:T(8,128)(2,1)S(1)}, bf16[128,2048]{1,0:T(8,128)(2,1)S(1)}, u32[]{:S(2)}, u32[]{:S(2)}) collective-permute-start(bf16[128,2048]{1,0:T(8,128)(2,1)S(1)} %collective-permute-done.14.refs_2_), channel_id=1, source_target_pairs={{0,6},{1,7},{2,0},{3,1},{4,2},{5,3},{6,4},{7,5},{8,14},{9,15},{10,... | collective-permute-start | bytes 1572872 | tf_op jit(solution)/shard_map/ppermute | solution.py:51
  68.5 15.9 %collective-permute-start.18 = (bf16[2048,384]{1,0:T(8,128)(2,1)S(1)}, bf16[2048,384]{1,0:T(8,128)(2,1)S(1)}, u32[]{:S(2)}, u32[]{:S(2)}) collective-permute-start(bf16[2048,384]{1,0:T(8,128)(2,1)S(1)} %copy-done.13), channel_id=1, source_target_pairs={{0,1},{1,0},{2,3},{3,2},{4,5},{5,4},{6,7},{7,6},{8,9},{9,8},{10,11... | collective-permute-start | bytes 4718600 | tf_op jit(solution)/shard_map/ppermute | solution.py:51
  68.5 15.9 %collective-permute-start.19 = (bf16[2048,384]{1,0:T(8,128)(2,1)S(1)}, bf16[2048,384]{1,0:T(8,128)(2,1)S(1)}, u32[]{:S(2)}, u32[]{:S(2)}) collective-permute-start(bf16[2048,384]{1,0:T(8,128)(2,1)S(1)} %copy-done.14), channel_id=1, source_target_pairs={{0,1},{1,0},{2,3},{3,2},{4,5},{5,4},{6,7},{7,6},{8,9},{9,8},{10,11... | collective-permute-start | bytes 4718600 | tf_op jit(solution)/shard_map/ppermute | solution.py:51
  73.8 21.6 %collective-permute-start.24 = (bf16[2,256,384]{2,1,0:T(8,128)(2,1)S(1)}, bf16[2,256,384]{2,1,0:T(8,128)(2,1)S(1)}, u32[]{:S(2)}, u32[]{:S(2)}) collective-permute-start(bf16[2,256,384]{2,1,0:T(8,128)(2,1)S(1)} %get-tuple-element.170), channel_id=1, source_target_pairs={{0,96},{16,112},{32,0},{48,16},{64,32},{80,48},{96,64},{112,80},{1... | collective-permute-start | bytes 1179656 | tf_op jit(solution)/shard_map/ppermute | solution.py:55
  78.9 16.5 %collective-permute-start.23 = (bf16[2,256,384]{2,1,0:T(8,128)(2,1)S(1)}, bf16[2,256,384]{2,1,0:T(8,128)(2,1)S(1)}, u32[]{:S(2)}, u32[]{:S(2)}) collective-permute-start(bf16[2,256,384]{2,1,0:T(8,128)(2,1)S(1)} %get-tuple-element.171), channel_id=1, source_target_pairs={{0,32},{16,48},{32,64},{48,80},{64,96},{80,112},{96,0},{112,16},{1... | collective-permute-start | bytes 1179656 | tf_op jit(solution)/shard_map/ppermute | solution.py:55
  80.9 18.6 %collective-permute-start.22 = (bf16[2,256,384]{2,1,0:T(8,128)(2,1)S(1)}, bf16[2,256,384]{2,1,0:T(8,128)(2,1)S(1)}, u32[]{:S(2)}, u32[]{:S(2)}) collective-permute-start(bf16[2,256,384]{2,1,0:T(8,128)(2,1)S(1)} %get-tuple-element.172), channel_id=1, source_target_pairs={{0,64},{16,80},{32,96},{48,112},{64,0},{80,16},{96,32},{112,48},{1... | collective-permute-start | bytes 1179656 | tf_op jit(solution)/shard_map/ppermute | solution.py:55
  84.5 15.0 %collective-permute-start.20 = (bf16[128,2048]{1,0:T(8,128)(2,1)S(1)}, bf16[128,2048]{1,0:T(8,128)(2,1)S(1)}, u32[]{:S(2)}, u32[]{:S(2)}) collective-permute-start(bf16[128,2048]{1,0:T(8,128)(2,1)S(1)} %collective-permute-done.13.refs_4_), channel_id=1, source_target_pairs={{0,2},{1,3},{2,4},{3,5},{4,6},{5,7},{6,0},{7,1},{8,10},{9,11},{10,... | collective-permute-start | bytes 1572872 | tf_op jit(solution)/shard_map/ppermute | solution.py:51
  84.5 15.0 %collective-permute-start.21 = (bf16[128,2048]{1,0:T(8,128)(2,1)S(1)}, bf16[128,2048]{1,0:T(8,128)(2,1)S(1)}, u32[]{:S(2)}, u32[]{:S(2)}) collective-permute-start(bf16[128,2048]{1,0:T(8,128)(2,1)S(1)} %collective-permute-done.16.refs_5_), channel_id=1, source_target_pairs={{0,6},{1,7},{2,0},{3,1},{4,2},{5,3},{6,4},{7,5},{8,14},{9,15},{10,... | collective-permute-start | bytes 1572872 | tf_op jit(solution)/shard_map/ppermute | solution.py:51
  101.9 2.4 %collective-permute-start.25 = (bf16[2,256,768]{2,1,0:T(8,128)(2,1)S(1)}, bf16[2,256,768]{2,1,0:T(8,128)(2,1)S(1)}, u32[]{:S(2)}, u32[]{:S(2)}) collective-permute-start(bf16[2,256,768]{2,1,0:T(8,128)(2,1)S(1)} %get-tuple-element.123), channel_id=1, source_target_pairs={{0,1},{1,0},{2,3},{3,2},{4,5},{5,4},{6,7},{7,6},{8,9},{9,8},{10,11... | collective-permute-start | bytes 2359304 | tf_op jit(solution)/shard_map/ppermute | solution.py:51
  102.0 14.3 %collective-permute-start.32 = (bf16[128,2048]{1,0:T(8,128)(2,1)S(1)}, bf16[128,2048]{1,0:T(8,128)(2,1)S(1)}, u32[]{:S(2)}, u32[]{:S(2)}) collective-permute-start(bf16[128,2048]{1,0:T(8,128)(2,1)S(1)} %get-tuple-element.147), channel_id=1, source_target_pairs={{0,6},{1,7},{2,0},{3,1},{4,2},{5,3},{6,4},{7,5},{8,14},{9,15},{10,... | collective-permute-start | bytes 1572872 | tf_op jit(solution)/shard_map/ppermute | solution.py:51
  103.8 15.2 %collective-permute-start.31 = (bf16[128,2048]{1,0:T(8,128)(2,1)S(1)}, bf16[128,2048]{1,0:T(8,128)(2,1)S(1)}, u32[]{:S(2)}, u32[]{:S(2)}) collective-permute-start(bf16[128,2048]{1,0:T(8,128)(2,1)S(1)} %get-tuple-element.145), channel_id=1, source_target_pairs={{0,2},{1,3},{2,4},{3,5},{4,6},{5,7},{6,0},{7,1},{8,10},{9,11},{10,... | collective-permute-start | bytes 1572872 | tf_op jit(solution)/shard_map/ppermute | solution.py:51
  104.5 17.9 %collective-permute-start.27 = (bf16[256,768]{1,0:T(8,128)(2,1)S(1)}, bf16[256,768]{1,0:T(8,128)(2,1)S(1)}, u32[]{:S(2)}, u32[]{:S(2)}) collective-permute-start(bf16[256,768]{1,0:T(8,128)(2,1)S(1)} %get-tuple-element.175), channel_id=1, source_target_pairs={{0,96},{16,112},{32,0},{48,16},{64,32},{80,48},{96,64},{112,80},{1... | collective-permute-start | bytes 1179656 | tf_op jit(solution)/shard_map/ppermute | solution.py:55
  104.6 17.8 %collective-permute-start.26 = (bf16[256,768]{1,0:T(8,128)(2,1)S(1)}, bf16[256,768]{1,0:T(8,128)(2,1)S(1)}, u32[]{:S(2)}, u32[]{:S(2)}) collective-permute-start(bf16[256,768]{1,0:T(8,128)(2,1)S(1)} %get-tuple-element.176), channel_id=1, source_target_pairs={{0,32},{16,48},{32,64},{48,80},{64,96},{80,112},{96,0},{112,16},{1... | collective-permute-start | bytes 1179656 | tf_op jit(solution)/shard_map/ppermute | solution.py:55
  119.1 14.4 %collective-permute-start.33 = (bf16[128,2048]{1,0:T(8,128)(2,1)S(1)}, bf16[128,2048]{1,0:T(8,128)(2,1)S(1)}, u32[]{:S(2)}, u32[]{:S(2)}) collective-permute-start(bf16[128,2048]{1,0:T(8,128)(2,1)S(1)} %add_convert_fusion.3), channel_id=1, source_target_pairs={{0,2},{1,3},{2,4},{3,5},{4,6},{5,7},{6,0},{7,1},{8,10},{9,11},{10,... | collective-permute-start | bytes 1572872 | tf_op jit(solution)/shard_map/ppermute | solution.py:51
  119.2 14.4 %collective-permute-start.34 = (bf16[128,2048]{1,0:T(8,128)(2,1)S(1)}, bf16[128,2048]{1,0:T(8,128)(2,1)S(1)}, u32[]{:S(2)}, u32[]{:S(2)}) collective-permute-start(bf16[128,2048]{1,0:T(8,128)(2,1)S(1)} %get-tuple-element.150), channel_id=1, source_target_pairs={{0,6},{1,7},{2,0},{3,1},{4,2},{5,3},{6,4},{7,5},{8,14},{9,15},{10,... | collective-permute-start | bytes 1572872 | tf_op jit(solution)/shard_map/ppermute | solution.py:51
  122.4 11.1 %collective-permute-start.28 = (bf16[4,256,768]{2,1,0:T(8,128)(2,1)S(1)}, bf16[4,256,768]{2,1,0:T(8,128)(2,1)S(1)}, u32[]{:S(2)}, u32[]{:S(2)}) collective-permute-start(bf16[4,256,768]{2,1,0:T(8,128)(2,1)S(1)} %get-tuple-element.130), channel_id=1, source_target_pairs={{0,1},{1,0},{2,3},{3,2},{4,5},{5,4},{6,7},{7,6},{8,9},{9,8},{10,11... | collective-permute-start | bytes 4718600 | tf_op jit(solution)/shard_map/ppermute | solution.py:51
  124.8 15.9 %collective-permute-start.37 = (bf16[2,256,768]{2,1,0:T(8,128)(2,1)S(1)}, bf16[2,256,768]{2,1,0:T(8,128)(2,1)S(1)}, u32[]{:S(2)}, u32[]{:S(2)}) collective-permute-start(bf16[2,256,768]{2,1,0:T(8,128)(2,1)S(1)} %get-tuple-element.157), channel_id=1, source_target_pairs={{0,1},{1,0},{2,3},{3,2},{4,5},{5,4},{6,7},{7,6},{8,9},{9,8},{10,11... | collective-permute-start | bytes 2359304 | tf_op jit(solution)/shard_map/ppermute | solution.py:51
  134.2 19.1 %collective-permute-start.29 = (bf16[2,256,768]{2,1,0:T(8,128)(2,1)S(1)}, bf16[2,256,768]{2,1,0:T(8,128)(2,1)S(1)}, u32[]{:S(2)}, u32[]{:S(2)}) collective-permute-start(bf16[2,256,768]{2,1,0:T(8,128)(2,1)S(1)} %get-tuple-element.140), channel_id=1, source_target_pairs={{0,32},{16,48},{32,64},{48,80},{64,96},{80,112},{96,0},{112,16},{1... | collective-permute-start | bytes 2359304 | tf_op jit(solution)/shard_map/ppermute | solution.py:55
  134.3 19.1 %collective-permute-start.30 = (bf16[2,256,768]{2,1,0:T(8,128)(2,1)S(1)}, bf16[2,256,768]{2,1,0:T(8,128)(2,1)S(1)}, u32[]{:S(2)}, u32[]{:S(2)}) collective-permute-start(bf16[2,256,768]{2,1,0:T(8,128)(2,1)S(1)} %get-tuple-element.141), channel_id=1, source_target_pairs={{0,96},{16,112},{32,0},{48,16},{64,32},{80,48},{96,64},{112,80},{1... | collective-permute-start | bytes 2359304 | tf_op jit(solution)/shard_map/ppermute | solution.py:55
  137.7 11.9 %collective-permute-start.35 = (bf16[128,2048]{1,0:T(8,128)(2,1)S(1)}, bf16[128,2048]{1,0:T(8,128)(2,1)S(1)}, u32[]{:S(2)}, u32[]{:S(2)}) collective-permute-start(bf16[128,2048]{1,0:T(8,128)(2,1)S(1)} %add_convert_fusion.2), channel_id=1, source_target_pairs={{0,6},{1,7},{2,0},{3,1},{4,2},{5,3},{6,4},{7,5},{8,14},{9,15},{10,... | collective-permute-start | bytes 1572872 | tf_op jit(solution)/shard_map/ppermute | solution.py:51
  140.7 12.3 %collective-permute-start.36 = (bf16[128,2048]{1,0:T(8,128)(2,1)S(1)}, bf16[128,2048]{1,0:T(8,128)(2,1)S(1)}, u32[]{:S(2)}, u32[]{:S(2)}) collective-permute-start(bf16[128,2048]{1,0:T(8,128)(2,1)S(1)} %get-tuple-element.153), channel_id=1, source_target_pairs={{0,2},{1,3},{2,4},{3,5},{4,6},{5,7},{6,0},{7,1},{8,10},{9,11},{10,... | collective-permute-start | bytes 1572872 | tf_op jit(solution)/shard_map/ppermute | solution.py:51
  140.9 16.7 %collective-permute-start.38 = (bf16[128,2048]{1,0:T(8,128)(2,1)S(1)}, bf16[128,2048]{1,0:T(8,128)(2,1)S(1)}, u32[]{:S(2)}, u32[]{:S(2)}) collective-permute-start(bf16[128,2048]{1,0:T(8,128)(2,1)S(1)} %add_convert_fusion.1), channel_id=1, source_target_pairs={{0,8},{1,9},{2,10},{3,11},{4,12},{5,13},{6,14},{7,15},{8,0},{9,1},... | collective-permute-start | bytes 1572872 | tf_op jit(solution)/shard_map/ppermute | solution.py:51
  153.6 9.3 %collective-permute-start.40 = (bf16[256,384]{1,0:T(8,128)(2,1)S(1)}, bf16[256,384]{1,0:T(8,128)(2,1)S(1)}, u32[]{:S(2)}, u32[]{:S(2)}) collective-permute-start(bf16[256,384]{1,0:T(8,128)(2,1)S(1)} %fusion.4), channel_id=1, source_target_pairs={{0,16},{16,0},{32,48},{48,32},{64,80},{80,64},{96,112},{112,96},{1... | collective-permute-start | bytes 589832 | tf_op jit(solution)/shard_map/ppermute | solution.py:55
  156.6 11.9 %collective-permute-start.39 = (bf16[256,768]{1,0:T(8,128)(2,1)S(1)}, bf16[256,768]{1,0:T(8,128)(2,1)S(1)}, u32[]{:S(2)}, u32[]{:S(2)}) collective-permute-start(bf16[256,768]{1,0:T(8,128)(2,1)S(1)} %fusion.1), channel_id=1, source_target_pairs={{0,16},{16,0},{32,48},{48,32},{64,80},{80,64},{96,112},{112,96},{1... | collective-permute-start | bytes 1179656 | tf_op jit(solution)/shard_map/ppermute | solution.py:55
